TPU v7x, 1024 devices: a whole 4x4x32 slice. The times are simulated.
1024 devices in a mesh: gx: 16 (over x, y), gy: 64 (over z, core).
Axes of the slice: x: 4, y: 4, z: 32, core: 2. Of those that a mesh axis runs over, the one named last changes fastest.
Arguments:
- right_side: float32 [112, 448, 168], P('gx', 'gy'), may hold values from -18 to 18
- stiff_coef: float32 [16, 64, 24], P('gx', 'gy'), may hold values from 0.3 to 3
- mass_coef: float32 [16, 64, 24], P('gx', 'gy'), may hold values from 2 to 200
- coarse_factor: float32 [8192, 8192], P(('gx', 'gy')), may hold values from -0.0068359375 to 0.0068359375
Outputs:
- solution: float32 [112, 448, 168], P('gx', 'gy')
- residual: float32 [112, 448, 168], P('gx', 'gy')
All inputs are finite; a program needn't handle non-finite values.
Results may differ from a plain program's by a relative error of at most 0.0003.
Values sent between devices are 32-bit elements; how exact they have to be, the bound alone decides.
No kernel may reach another device: no remote copies, remote signals or barrier semaphores. Data moves between devices by JAX's collectives and lax.ppermute only.
A program may use at most 32 MiB of HBM per device.

v0:
```python
import math

import jax
import jax.numpy as jnp
import numpy as np
from jax import lax
from jax.sharding import PartitionSpec as P

ITERS = 2


exact_mode = lax.Precision.HIGHEST


def with_halo(block, sides, width):
    for axis, dim in sides:
        count = lax.axis_size(axis)
        forward = [(i, i + 1) for i in range(count - 1)]
        forward.append((count - 1, 0))
        backward = [(target, source) for source, target in forward]
        low = lax.ppermute(
            lax.slice_in_dim(block, block.shape[dim] - width, None, axis=dim), axis, forward
        )
        high = lax.ppermute(lax.slice_in_dim(block, 0, width, axis=dim), axis, backward)
        block = jnp.concatenate([low, block, high], axis=dim)
    return block


def swapped(shard, axis, apart):
    return lax.ppermute(shard, axis, [(i, i ^ 1 << apart) for i in range(lax.axis_size(axis))])


def legendre_pair(position, degree):
    p_prev = 1.0
    p_now = position
    for order in range(2, degree + 1):
        p_next = ((2 * order - 1) * position * p_now - (order - 1) * p_prev) / order
        p_prev = p_now
        p_now = p_next
    return (p_now, p_prev)


def jacobi_eigen(matrix):
    size_n = matrix.shape[0]
    current = np.array(matrix)
    vectors = np.eye(size_n)
    for sweep in range(20):
        for row_p in range(size_n - 1):
            for row_q in range(row_p + 1, size_n):
                off_value = current[row_p, row_q]
                if abs(off_value) > 1e-300:
                    theta = (current[row_q, row_q] - current[row_p, row_p]) / (2.0 * off_value)
                    sign_t = 1.0 if theta >= 0.0 else -1.0
                    tangent = sign_t / (abs(theta) + math.sqrt(theta * theta + 1.0))
                    cosine = 1.0 / math.sqrt(tangent * tangent + 1.0)
                    sine = tangent * cosine
                    rotation = np.eye(size_n)
                    rotation[row_p, row_p] = cosine
                    rotation[row_q, row_q] = cosine
                    rotation[row_p, row_q] = sine
                    rotation[row_q, row_p] = -sine
                    current = rotation.T @ current @ rotation
                    vectors = vectors @ rotation
    return (np.array([current[idx, idx] for idx in range(size_n)]), vectors)


def gll_tables():
    degree = 7
    guesses = [
        -0.8717401485096066,
        -0.5917001814331423,
        -0.2092992179024789,
        0.2092992179024789,
        0.5917001814331423,
        0.8717401485096066,
    ]
    interior = []
    for guess in guesses:
        position = guess
        for newton in range(30):
            p_now, p_prev = legendre_pair(position, degree)
            first = degree * (position * p_now - p_prev) / (position * position - 1.0)
            second = (2.0 * position * first - degree * (degree + 1) * p_now) / (
                1.0 - position * position
            )
            position = position - first / second
        interior.append(position)
    points = np.array([-1.0] + interior + [1.0])
    values = np.array([legendre_pair(float(pt), degree)[0] for pt in points])
    weights = 2.0 / (degree * (degree + 1) * values**2)
    deriv_mat = np.zeros((8, 8))
    for left_idx in range(8):
        for right_idx in range(8):
            if left_idx != right_idx:
                deriv_mat[left_idx, right_idx] = values[left_idx] / (
                    values[right_idx] * (points[left_idx] - points[right_idx])
                )
    deriv_mat[0, 0] = -degree * (degree + 1) / 4.0
    deriv_mat[7, 7] = degree * (degree + 1) / 4.0
    stiffness = deriv_mat.T @ (weights[:, None] * deriv_mat)
    ext_stiff = np.zeros((10, 10))
    ext_stiff[1:9, 1:9] += stiffness
    ext_stiff[0:2, 0:2] += stiffness[6:8, 6:8]
    ext_stiff[8:10, 8:10] += stiffness[0:2, 0:2]
    ext_mass = np.zeros(10)
    ext_mass[1:9] += weights
    ext_mass[0:2] += weights[6:8]
    ext_mass[8:10] += weights[0:2]
    inv_root = 1.0 / np.sqrt(ext_mass)
    eigen_vals, eigen_vecs = jacobi_eigen(inv_root[:, None] * ext_stiff * inv_root[None, :])
    eigen_basis = inv_root[:, None] * eigen_vecs
    return (
        jnp.asarray(stiffness, jnp.float32),
        jnp.asarray(weights, jnp.float32),
        jnp.asarray(eigen_basis, jnp.float32),
        jnp.asarray(eigen_vals, jnp.float32),
    )


def take_rows(widened, low, high, fold_axis):
    return lax.slice_in_dim(widened, low, high, axis=fold_axis)


def face_fold(widened, fold_axis):
    pieces = [
        take_rows(widened, 0, 1, fold_axis),
        take_rows(widened, 2, 3, fold_axis) + take_rows(widened, 1, 2, fold_axis),
        take_rows(widened, 3, 9, fold_axis),
        take_rows(widened, 9, 10, fold_axis) + take_rows(widened, 10, 11, fold_axis),
        take_rows(widened, 11, 12, fold_axis),
    ]
    return jnp.concatenate(pieces, axis=fold_axis)


def spread_fold(widened, fold_axis):
    pieces = [
        take_rows(widened, 3, 5, fold_axis) + take_rows(widened, 0, 2, fold_axis),
        take_rows(widened, 5, 9, fold_axis),
        take_rows(widened, 9, 11, fold_axis) + take_rows(widened, 12, 14, fold_axis),
    ]
    return jnp.concatenate(pieces, axis=fold_axis)


def z_windows(field_in, span):
    leading = field_in.shape[:2]
    elements = field_in.shape[2] // 7
    blocks = jnp.moveaxis(field_in.reshape(leading + (elements, 7)), 2, 3)
    if span == 8:
        return jnp.concatenate([blocks, jnp.roll(blocks[:, :, 0:1], -1, axis=3)], axis=2)
    behind = jnp.roll(blocks[:, :, 6:7], 1, axis=3)
    forward = jnp.roll(blocks[:, :, 0:2], -1, axis=3)
    return jnp.concatenate([behind, blocks, forward], axis=2)


def z_fold(blocks):
    if blocks.shape[2] == 8:
        owned = jnp.concatenate(
            [blocks[:, :, 0:1] + jnp.roll(blocks[:, :, 7:8], 1, axis=3), blocks[:, :, 1:7]], axis=2
        )
    else:
        first_two = blocks[:, :, 1:3] + jnp.roll(blocks[:, :, 8:10], 1, axis=3)
        last_one = blocks[:, :, 7:8] + jnp.roll(blocks[:, :, 0:1], -1, axis=3)
        owned = jnp.concatenate([first_two, blocks[:, :, 3:7], last_one], axis=2)
    leading = owned.shape[:2]
    return jnp.moveaxis(owned, 2, 3).reshape(leading + (-1,))


def element_apply(blocks, stiff_line, mass_line, stiffness, weights):
    along_x = jnp.einsum("ai,ijte->ajte", stiffness, blocks, precision=exact_mode)
    along_y = jnp.einsum("aj,ijte->iate", stiffness, blocks, precision=exact_mode)
    along_z = jnp.einsum("at,ijte->ijae", stiffness, blocks, precision=exact_mode)
    weight_x = weights[:, None, None, None]
    weight_y = weights[None, :, None, None]
    weight_z = weights[None, None, :, None]
    laplace = (
        along_x * weight_y * weight_z
        + along_y * weight_x * weight_z
        + along_z * weight_x * weight_y
    )
    return stiff_line * laplace + mass_line * (weight_x * weight_y * weight_z) * blocks


def local_solve(blocks, stiff_line, mass_line, eigen_basis, eigen_vals):
    spectral = jnp.einsum("ia,ijte->ajte", eigen_basis, blocks, precision=exact_mode)
    spectral = jnp.einsum("jb,ajte->abte", eigen_basis, spectral, precision=exact_mode)
    spectral = jnp.einsum("tc,abte->abce", eigen_basis, spectral, precision=exact_mode)
    eigen_sum = eigen_vals[:, None, None] + eigen_vals[None, :, None] + eigen_vals[None, None, :]
    spectral = spectral / (stiff_line * eigen_sum[..., None] + mass_line)
    restored = jnp.einsum("ai,ijte->ajte", eigen_basis, spectral, precision=exact_mode)
    restored = jnp.einsum("bj,ajte->abte", eigen_basis, restored, precision=exact_mode)
    return jnp.einsum("ct,abte->abce", eigen_basis, restored, precision=exact_mode)


def local(right_side, stiff_coef, mass_coef, coarse_factor):
    stiffness, weights, eigen_basis, eigen_vals = gll_tables()
    stiff_line = stiff_coef.reshape(-1)
    mass_line = mass_coef.reshape(-1)
    z_points = right_side.shape[2]
    coarse_count = coarse_factor.shape[0]

    def widen(field_in):
        widened = with_halo(field_in, (("gx", 0), ("gy", 1)), 2)
        return face_fold(face_fold(widened, 0), 1)

    def owned_part(current):
        return current[1:8, 1:8]

    def coarse_total(partial_y):
        summed_rows = partial_y
        rounds = lax.axis_size(("gx", "gy")).bit_length() - 1
        for address_bit in range(rounds):
            summed_rows = summed_rows + swapped(summed_rows, ("gx", "gy"), address_bit)
        return summed_rows

    def precondition(extended):
        summed = z_fold(
            local_solve(z_windows(extended, 10), stiff_line, mass_line, eigen_basis, eigen_vals)
        )
        widened = with_halo(summed, (("gx", 0), ("gy", 1)), 2)
        smooth = spread_fold(spread_fold(widened, 0), 1)
        coarse_in = jnp.sum(extended[2:8, 2:8], axis=(0, 1)).reshape(coarse_count, -1).sum(axis=1)
        partial_y = jnp.dot(coarse_in, coarse_factor, precision=exact_mode)
        coarse_out = jnp.dot(coarse_factor, coarse_total(partial_y), precision=exact_mode)
        coarse_line = jnp.broadcast_to(
            coarse_out[:, None], (coarse_count, z_points // coarse_count)
        ).reshape(-1)
        coarse_plate = jnp.pad(
            jnp.broadcast_to(coarse_line, (6, 6, z_points)), ((1, 1), (1, 1), (0, 0))
        )
        return smooth + coarse_plate

    def global_dot(left_term, right_term):
        return lax.psum(jnp.sum(left_term * right_term), ("gx", "gy"))

    current = widen(jnp.pad(right_side, ((0, 1), (0, 1), (0, 0))))
    solution = jnp.zeros(right_side.shape, jnp.float32)
    smooth = precondition(current)
    direction = smooth
    rho_now = global_dot(owned_part(current), smooth[:7, :7])
    for iteration in range(ITERS):
        operate_summed = z_fold(
            element_apply(z_windows(direction, 8), stiff_line, mass_line, stiffness, weights)
        )
        applied = widen(operate_summed)
        step_len = rho_now / global_dot(direction[:7, :7], owned_part(applied))
        solution = solution + step_len * direction[:7, :7]
        current = current - step_len * applied
        if iteration + 1 < ITERS:
            smooth = precondition(current)
            rho_next = global_dot(owned_part(current), smooth[:7, :7])
            direction = smooth + rho_next / rho_now * direction
            rho_now = rho_next
    return (solution, owned_part(current))


def solution(mesh):
    placed = (P("gx", "gy", None), P("gx", "gy", None), P("gx", "gy", None), P(("gx", "gy"), None))
    return jax.shard_map(
        local,
        mesh=mesh,
        in_specs=placed,
        out_specs=(P("gx", "gy", None), P("gx", "gy", None)),
        check_vma=False,
    )
```

profile of v0, /device:TPU:1, one launch (start us, length us, event | category | flops | bytes accessed | tf_op | source)
XLA Modules:
  0.0 767.5 jit_solution(9046775875850230778)
XLA Ops:
  2.1 16.0 %collective-permute-start.8 = (f32[8192]{0:T(1024)S(1)}, f32[8192]{0:T(1024)S(1)}, u32[]{:S(2)}, u32[]{:S(2)}) collective-permute-start(f32[8192]{0:T(1024)S(1)} %bitcast.151), channel_id=1, source_target_pairs={{0,1},{1,0},{2,3},{3,2},{4,5},{5,4},{6,7},{7,6},{8,9},{9,8},{10,11... | collective-permute-start | bytes 98312 | tf_op jit(solution)/shard_map/ppermute | solution.py:30
  20.8 6.7 collective-permute-start.1
  46.4 6.7 collective-permute-start.5
  65.8 7.0 collective-permute-done.11
  72.9 9.2 %collective-permute-start.12 = (f32[8192]{0:T(1024)S(1)}, f32[8192]{0:T(1024)S(1)}, u32[]{:S(2)}, u32[]{:S(2)}) collective-permute-start(f32[8192]{0:T(1024)S(1)} %add.267), channel_id=1, source_target_pairs={{0,16},{1,17},{2,18},{3,19},{4,20},{5,21},{6,22},{7,23},{8,24},{9,... | collective-permute-start | bytes 98312 | tf_op jit(solution)/shard_map/ppermute | solution.py:30
  82.1 4.5 collective-permute-done.12
  86.6 16.4 %collective-permute-start.13 = (f32[8192]{0:T(1024)S(1)}, f32[8192]{0:T(1024)S(1)}, u32[]{:S(2)}, u32[]{:S(2)}) collective-permute-start(f32[8192]{0:T(1024)S(1)} %add.268), channel_id=1, source_target_pairs={{0,32},{1,33},{2,34},{3,35},{4,36},{5,37},{6,38},{7,39},{8,40},{9,... | collective-permute-start | bytes 98312 | tf_op jit(solution)/shard_map/ppermute | solution.py:30
  103.1 7.5 collective-permute-start.6
  118.7 4.2 collective-permute-done.15
  141.0 6.7 collective-permute-start.19
  148.5 13.7 %collective-permute-start.20 = (f32[12,2,168]{2,1,0:T(2,128)S(1)}, f32[12,2,168]{2,1,0:T(2,128)S(1)}, u32[]{:S(2)}, u32[]{:S(2)}) collective-permute-start(f32[12,2,168]{2,1,0:T(2,128)S(1)} %get-tuple-element.60), channel_id=1, source_target_pairs={{0,1},{1,2},{2,3},{3,4},{4,5},{5,6},{6,7},{7,8},{8,9},{9,10},{10,1... | collective-permute-start | bytes 48392 | tf_op jit(solution)/shard_map/ppermute | solution.py:21
  169.1 156.9 %all-reduce.3 = (f32[]{:T(128)}, f32[]{:T(128)}) all-reduce(f32[]{:T(128)} %get-tuple-element.7, f32[]{:T(128)} %get-tuple-element.6), channel_id=1, replica_groups=mesh['gx'=16,'gy'=64] {'gx','gy'}, use_global_device_ids=true, to_apply=%region_3.4 | all-reduce | flops 2 | bytes 16 | tf_op jit(solution)/shard_map/psum | solution.py:233
  349.3 6.7 collective-permute-start.23
  356.0 4.2 collective-permute-start.29
  360.2 4.3 collective-permute-done.29
  364.5 8.3 %collective-permute-start.30 = (f32[8192]{0:T(1024)S(1)}, f32[8192]{0:T(1024)S(1)}, u32[]{:S(2)}, u32[]{:S(2)}) collective-permute-start(f32[8192]{0:T(1024)S(1)} %add.292), channel_id=1, source_target_pairs={{0,16},{1,17},{2,18},{3,19},{4,20},{5,21},{6,22},{7,23},{8,24},{9,... | collective-permute-start | bytes 98312 | tf_op jit(solution)/shard_map/ppermute | solution.py:30
  373.0 5.0 collective-permute-done.30
  377.9 15.7 %collective-permute-start.31 = (f32[8192]{0:T(1024)S(1)}, f32[8192]{0:T(1024)S(1)}, u32[]{:S(2)}, u32[]{:S(2)}) collective-permute-start(f32[8192]{0:T(1024)S(1)} %add.293), channel_id=1, source_target_pairs={{0,32},{1,33},{2,34},{3,35},{4,36},{5,37},{6,38},{7,39},{8,40},{9,... | collective-permute-start | bytes 98312 | tf_op jit(solution)/shard_map/ppermute | solution.py:30
  393.6 7.3 collective-permute-done.31
  402.9 6.8 collective-permute-start.24
  423.3 4.2 collective-permute-done.35
  429.0 157.3 %psum.30 = f32[]{:T(128)} all-reduce(f32[]{:T(128)} %fusion.62), channel_id=1, replica_groups=mesh['gx'=16,'gy'=64] {'gx','gy'}, use_global_device_ids=true, to_apply=%region_9.10 | all-reduce | flops 1 | bytes 8 | tf_op jit(solution)/shard_map/psum | solution.py:233
  594.4 6.2 collective-permute-start.37
  609.0 155.9 %psum.31 = f32[]{:T(128)} all-reduce(f32[]{:T(128)} %fusion.61), channel_id=1, replica_groups=mesh['gx'=16,'gy'=64] {'gx','gy'}, use_global_device_ids=true, to_apply=%region_11.12 | all-reduce | flops 1 | bytes 8 | tf_op jit(solution)/shard_map/psum | solution.py:233
  (318 shorter events, 124.2 us)
Async XLA Ops:
  2.1 51.3 %collective-permute-start.8 = (f32[8192]{0:T(1024)S(1)}, f32[8192]{0:T(1024)S(1)}, u32[]{:S(2)}, u32[]{:S(2)}) collective-permute-start(f32[8192]{0:T(1024)S(1)} %bitcast.151), channel_id=1, source_target_pairs={{0,1},{1,0},{2,3},{3,2},{4,5},{5,4},{6,7},{7,6},{8,9},{9,8},{10,11... | collective-permute-start | bytes 98312 | tf_op jit(solution)/shard_map/ppermute | solution.py:30
  18.9 11.8 %collective-permute-start = (f32[2,8,168]{2,1,0:T(8,128)S(1)}, f32[2,8,168]{2,1,0:T(8,128)S(1)}, u32[]{:S(2)}, u32[]{:S(2)}) collective-permute-start(f32[2,8,168]{2,1,0:T(8,128)S(1)} %get-tuple-element.64), channel_id=1, source_target_pairs={{0,64},{64,128},{128,192},{192,256},{256,320},{320,384},{384,448},... | collective-permute-start | bytes 32264 | tf_op jit(solution)/shard_map/ppermute | solution.py:21
  20.8 9.9 %collective-permute-start.1 = (f32[2,8,168]{2,1,0:T(8,128)S(1)}, f32[2,8,168]{2,1,0:T(8,128)S(1)}, u32[]{:S(2)}, u32[]{:S(2)}) collective-permute-start(f32[2,8,168]{2,1,0:T(8,128)S(1)} %get-tuple-element.65), channel_id=1, source_target_pairs={{64,0},{128,64},{192,128},{256,192},{320,256},{384,320},{448,384},... | collective-permute-start | bytes 32264 | tf_op jit(solution)/shard_map/ppermute | solution.py:24
  44.2 15.9 %collective-permute-start.4 = (f32[2,10,168]{2,0,1:T(2,128)S(1)}, f32[2,10,168]{2,0,1:T(2,128)S(1)}, u32[]{:S(2)}, u32[]{:S(2)}) collective-permute-start(f32[2,10,168]{2,0,1:T(2,128)S(1)} %slice.493), channel_id=1, source_target_pairs={{0,64},{64,128},{128,192},{192,256},{256,320},{320,384},{384,448},... | collective-permute-start | bytes 40328 | tf_op jit(solution)/shard_map/ppermute | solution.py:21
  46.4 35.6 %collective-permute-start.5 = (f32[2,10,168]{2,1,0:T(8,128)S(1)}, f32[2,10,168]{2,1,0:T(8,128)S(1)}, u32[]{:S(2)}, u32[]{:S(2)}) collective-permute-start(f32[2,10,168]{2,1,0:T(8,128)S(1)} %reshape.155), channel_id=1, source_target_pairs={{64,0},{128,64},{192,128},{256,192},{320,256},{384,320},{448,384},... | collective-permute-start | bytes 40328 | tf_op jit(solution)/shard_map/ppermute | solution.py:24
  63.9 9.0 %collective-permute-start.11 = (f32[8192]{0:T(1024)S(1)}, f32[8192]{0:T(1024)S(1)}, u32[]{:S(2)}, u32[]{:S(2)}) collective-permute-start(f32[8192]{0:T(1024)S(1)} %add.266), channel_id=1, source_target_pairs={{0,8},{1,9},{2,10},{3,11},{4,12},{5,13},{6,14},{7,15},{8,0},{9,1},... | collective-permute-start | bytes 98312 | tf_op jit(solution)/shard_map/ppermute | solution.py:30
  72.9 13.8 %collective-permute-start.12 = (f32[8192]{0:T(1024)S(1)}, f32[8192]{0:T(1024)S(1)}, u32[]{:S(2)}, u32[]{:S(2)}) collective-permute-start(f32[8192]{0:T(1024)S(1)} %add.267), channel_id=1, source_target_pairs={{0,16},{1,17},{2,18},{3,19},{4,20},{5,21},{6,22},{7,23},{8,24},{9,... | collective-permute-start | bytes 98312 | tf_op jit(solution)/shard_map/ppermute | solution.py:30
  86.6 25.1 %collective-permute-start.13 = (f32[8192]{0:T(1024)S(1)}, f32[8192]{0:T(1024)S(1)}, u32[]{:S(2)}, u32[]{:S(2)}) collective-permute-start(f32[8192]{0:T(1024)S(1)} %add.268), channel_id=1, source_target_pairs={{0,32},{1,33},{2,34},{3,35},{4,36},{5,37},{6,38},{7,39},{8,40},{9,... | collective-permute-start | bytes 98312 | tf_op jit(solution)/shard_map/ppermute | solution.py:30
  103.1 15.6 %collective-permute-start.6 = (f32[14,2,168]{2,1,0:T(2,128)S(1)}, f32[14,2,168]{2,1,0:T(2,128)S(1)}, u32[]{:S(2)}, u32[]{:S(2)}) collective-permute-start(f32[14,2,168]{2,1,0:T(2,128)S(1)} %get-tuple-element.32), channel_id=1, source_target_pairs={{0,1},{1,2},{2,3},{3,4},{4,5},{5,6},{6,7},{7,8},{8,9},{9,10},{10,1... | collective-permute-start | bytes 56456 | tf_op jit(solution)/shard_map/ppermute | solution.py:21
  110.6 8.1 %collective-permute-start.7 = (f32[14,2,168]{2,1,0:T(2,128)S(1)}, f32[14,2,168]{2,1,0:T(2,128)S(1)}, u32[]{:S(2)}, u32[]{:S(2)}) collective-permute-start(f32[14,2,168]{2,1,0:T(2,128)S(1)} %get-tuple-element.33), channel_id=1, source_target_pairs={{1,0},{2,1},{3,2},{4,3},{5,4},{6,5},{7,6},{8,7},{9,8},{10,9},{11,1... | collective-permute-start | bytes 56456 | tf_op jit(solution)/shard_map/ppermute | solution.py:24
  137.7 10.0 %collective-permute-start.18 = (f32[2,8,168]{2,1,0:T(8,128)S(1)}, f32[2,8,168]{2,1,0:T(8,128)S(1)}, u32[]{:S(2)}, u32[]{:S(2)}) collective-permute-start(f32[2,8,168]{2,1,0:T(8,128)S(1)} %slice.517), channel_id=1, source_target_pairs={{0,64},{64,128},{128,192},{192,256},{256,320},{320,384},{384,448},... | collective-permute-start | bytes 32264 | tf_op jit(solution)/shard_map/ppermute | solution.py:21
  141.0 7.5 collective-permute-start.19
  148.5 14.6 %collective-permute-start.20 = (f32[12,2,168]{2,1,0:T(2,128)S(1)}, f32[12,2,168]{2,1,0:T(2,128)S(1)}, u32[]{:S(2)}, u32[]{:S(2)}) collective-permute-start(f32[12,2,168]{2,1,0:T(2,128)S(1)} %get-tuple-element.60), channel_id=1, source_target_pairs={{0,1},{1,2},{2,3},{3,4},{4,5},{5,6},{6,7},{7,8},{8,9},{9,10},{10,1... | collective-permute-start | bytes 48392 | tf_op jit(solution)/shard_map/ppermute | solution.py:21
  343.7 12.3 %collective-permute-start.28 = (f32[8192]{0:T(1024)S(1)}, f32[8192]{0:T(1024)S(1)}, u32[]{:S(2)}, u32[]{:S(2)}) collective-permute-start(f32[8192]{0:T(1024)S(1)} %add.290), channel_id=1, source_target_pairs={{0,4},{1,5},{2,6},{3,7},{4,0},{5,1},{6,2},{7,3},{8,12},{9,13},{10,... | collective-permute-start | bytes 98312 | tf_op jit(solution)/shard_map/ppermute | solution.py:30
  345.9 14.3 %collective-permute-start.22 = (f32[2,10,168]{2,1,0:T(8,128)S(1)}, f32[2,10,168]{2,1,0:T(8,128)S(1)}, u32[]{:S(2)}, u32[]{:S(2)}) collective-permute-start(f32[2,10,168]{2,1,0:T(8,128)S(1)} %reshape.156), channel_id=1, source_target_pairs={{0,64},{64,128},{128,192},{192,256},{256,320},{320,384},{384,448},... | collective-permute-start | bytes 40328 | tf_op jit(solution)/shard_map/ppermute | solution.py:21
  349.3 44.4 %collective-permute-start.23 = (f32[2,10,168]{2,1,0:T(8,128)S(1)}, f32[2,10,168]{2,1,0:T(8,128)S(1)}, u32[]{:S(2)}, u32[]{:S(2)}) collective-permute-start(f32[2,10,168]{2,1,0:T(8,128)S(1)} %reshape.157), channel_id=1, source_target_pairs={{64,0},{128,64},{192,128},{256,192},{320,256},{384,320},{448,384},... | collective-permute-start | bytes 40328 | tf_op jit(solution)/shard_map/ppermute | solution.py:24
  356.0 8.6 %collective-permute-start.29 = (f32[8192]{0:T(1024)S(1)}, f32[8192]{0:T(1024)S(1)}, u32[]{:S(2)}, u32[]{:S(2)}) collective-permute-start(f32[8192]{0:T(1024)S(1)} %add.291), channel_id=1, source_target_pairs={{0,8},{1,9},{2,10},{3,11},{4,12},{5,13},{6,14},{7,15},{8,0},{9,1},... | collective-permute-start | bytes 98312 | tf_op jit(solution)/shard_map/ppermute | solution.py:30
  364.5 13.4 %collective-permute-start.30 = (f32[8192]{0:T(1024)S(1)}, f32[8192]{0:T(1024)S(1)}, u32[]{:S(2)}, u32[]{:S(2)}) collective-permute-start(f32[8192]{0:T(1024)S(1)} %add.292), channel_id=1, source_target_pairs={{0,16},{1,17},{2,18},{3,19},{4,20},{5,21},{6,22},{7,23},{8,24},{9,... | collective-permute-start | bytes 98312 | tf_op jit(solution)/shard_map/ppermute | solution.py:30
  377.9 23.0 %collective-permute-start.31 = (f32[8192]{0:T(1024)S(1)}, f32[8192]{0:T(1024)S(1)}, u32[]{:S(2)}, u32[]{:S(2)}) collective-permute-start(f32[8192]{0:T(1024)S(1)} %add.293), channel_id=1, source_target_pairs={{0,32},{1,33},{2,34},{3,35},{4,36},{5,37},{6,38},{7,39},{8,40},{9,... | collective-permute-start | bytes 98312 | tf_op jit(solution)/shard_map/ppermute | solution.py:30
  400.9 9.6 %collective-permute-start.32 = (f32[8192]{0:T(1024)S(1)}, f32[8192]{0:T(1024)S(1)}, u32[]{:S(2)}, u32[]{:S(2)}) collective-permute-start(f32[8192]{0:T(1024)S(1)} %add.294), channel_id=1, source_target_pairs={{0,64},{1,65},{2,66},{3,67},{4,68},{5,69},{6,70},{7,71},{8,72},{9,... | collective-permute-start | bytes 98312 | tf_op jit(solution)/shard_map/ppermute | solution.py:30
  402.9 9.6 %collective-permute-start.24 = (f32[14,2,168]{2,1,0:T(2,128)S(1)}, f32[14,2,168]{2,1,0:T(2,128)S(1)}, u32[]{:S(2)}, u32[]{:S(2)}) collective-permute-start(f32[14,2,168]{2,1,0:T(2,128)S(1)} %get-tuple-element.28), channel_id=1, source_target_pairs={{0,1},{1,2},{2,3},{3,4},{4,5},{5,6},{6,7},{7,8},{8,9},{9,10},{10,1... | collective-permute-start | bytes 56456 | tf_op jit(solution)/shard_map/ppermute | solution.py:21
  410.5 6.2 collective-permute-start.33
  591.0 9.6 %collective-permute-start.36 = (f32[2,8,168]{2,1,0:T(8,128)S(1)}, f32[2,8,168]{2,1,0:T(8,128)S(1)}, u32[]{:S(2)}, u32[]{:S(2)}) collective-permute-start(f32[2,8,168]{2,1,0:T(8,128)S(1)} %slice.575), channel_id=1, source_target_pairs={{0,64},{64,128},{128,192},{192,256},{256,320},{320,384},{384,448},... | collective-permute-start | bytes 32264 | tf_op jit(solution)/shard_map/ppermute | solution.py:21
  594.4 7.0 collective-permute-start.37
  (32 other events, 752.7 us)
where the time goes:
time: 769 us; the launch traced here: 768 us
  blocking collectives  470 us (61%)
  starting transfers between devices  176 us (23%)
  waiting for transfers between devices  69.3 us (9%)
  local copies, waits for them, and re-layouts  18.2 us (2%)
  matrix products  17.5 us (2%)
  other arithmetic  10.7 us (1%)
    psum x3, blocking collectives, global_dot(): return lax.psum(jnp.sum(left_term * right_term), ('gx', 'gy'))  470 us
    ppermute x20, starting transfers between devices, swapped(): lax.ppermute(shard, axis, [(i, i ^ 1 << apart) for i in range(lax.axis_si...  98.8 us
    ppermute x20, waiting for transfers between devices, swapped(): lax.ppermute(shard, axis, [(i, i ^ 1 << apart) for i in range(lax.axis_si...  58.6 us
    ppermute x10, starting transfers between devices, with_halo(): lax.ppermute(lax.slice_in_dim(block, block.shape[dim] - width, None, axis...  41.5 us
    ppermute x10, starting transfers between devices, with_halo(): lax.ppermute(lax.slice_in_dim(block, 0, width, axis=dim), axis, backward)  35.5 us
  transfers between devices with their start and end apart: 40, of which 24 were waited for; matrix products, arithmetic and copies ran while one was open for 3% of the time, Pallas kernels for 0%

commit v1 on v0

v1 whole, which is shorter than its diff:
```python
import math

import jax
import jax.numpy as jnp
import numpy as np
from jax import lax
from jax.experimental import pallas as pl
from jax.experimental.pallas import tpu as pltpu
from jax.sharding import PartitionSpec as P

HI = lax.Precision.HIGHEST
LANES = 128


def legendre_pair(position, degree):
    p_prev = 1.0
    p_now = position
    for order in range(2, degree + 1):
        p_next = ((2 * order - 1) * position * p_now - (order - 1) * p_prev) / order
        p_prev = p_now
        p_now = p_next
    return (p_now, p_prev)


def jacobi_eigen(matrix):
    size_n = matrix.shape[0]
    current = np.array(matrix)
    vectors = np.eye(size_n)
    for sweep in range(20):
        for row_p in range(size_n - 1):
            for row_q in range(row_p + 1, size_n):
                off_value = current[row_p, row_q]
                if abs(off_value) > 1e-300:
                    theta = (current[row_q, row_q] - current[row_p, row_p]) / (2.0 * off_value)
                    sign_t = 1.0 if theta >= 0.0 else -1.0
                    tangent = sign_t / (abs(theta) + math.sqrt(theta * theta + 1.0))
                    cosine = 1.0 / math.sqrt(tangent * tangent + 1.0)
                    sine = tangent * cosine
                    rotation = np.eye(size_n)
                    rotation[row_p, row_p] = cosine
                    rotation[row_q, row_q] = cosine
                    rotation[row_p, row_q] = sine
                    rotation[row_q, row_p] = -sine
                    current = rotation.T @ current @ rotation
                    vectors = vectors @ rotation
    return (np.array([current[idx, idx] for idx in range(size_n)]), vectors)


def gll_tables():
    degree = 7
    guesses = [
        -0.8717401485096066,
        -0.5917001814331423,
        -0.2092992179024789,
        0.2092992179024789,
        0.5917001814331423,
        0.8717401485096066,
    ]
    interior = []
    for guess in guesses:
        position = guess
        for newton in range(30):
            p_now, p_prev = legendre_pair(position, degree)
            first = degree * (position * p_now - p_prev) / (position * position - 1.0)
            second = (2.0 * position * first - degree * (degree + 1) * p_now) / (
                1.0 - position * position
            )
            position = position - first / second
        interior.append(position)
    points = np.array([-1.0] + interior + [1.0])
    values = np.array([legendre_pair(float(pt), degree)[0] for pt in points])
    weights = 2.0 / (degree * (degree + 1) * values**2)
    deriv_mat = np.zeros((8, 8))
    for left_idx in range(8):
        for right_idx in range(8):
            if left_idx != right_idx:
                deriv_mat[left_idx, right_idx] = values[left_idx] / (
                    values[right_idx] * (points[left_idx] - points[right_idx])
                )
    deriv_mat[0, 0] = -degree * (degree + 1) / 4.0
    deriv_mat[7, 7] = degree * (degree + 1) / 4.0
    stiffness = deriv_mat.T @ (weights[:, None] * deriv_mat)
    ext_stiff = np.zeros((10, 10))
    ext_stiff[1:9, 1:9] += stiffness
    ext_stiff[0:2, 0:2] += stiffness[6:8, 6:8]
    ext_stiff[8:10, 8:10] += stiffness[0:2, 0:2]
    ext_mass = np.zeros(10)
    ext_mass[1:9] += weights
    ext_mass[0:2] += weights[6:8]
    ext_mass[8:10] += weights[0:2]
    inv_root = 1.0 / np.sqrt(ext_mass)
    eigen_vals, eigen_vecs = jacobi_eigen(inv_root[:, None] * ext_stiff * inv_root[None, :])
    eigen_basis = inv_root[:, None] * eigen_vecs
    return (stiffness, weights, eigen_basis, eigen_vals)


def dot(left, right):
    return jnp.dot(left, right, precision=HI, preferred_element_type=jnp.float32)


def make_tables(ez, c_dev):
    stiffness, weights, basis, vals = gll_tables()
    stiffness = stiffness.astype(np.float32).astype(np.float64)
    weights = weights.astype(np.float32).astype(np.float64)
    basis = basis.astype(np.float32).astype(np.float64)
    vals = vals.astype(np.float32).astype(np.float64)
    nz = 7 * ez
    span = nz // c_dev
    f32 = lambda table: np.asarray(table, np.float32)

    qq = np.zeros((10, 16, 10, 16))
    qq[:, :10, :, :10] = np.einsum("ia,jb->ijab", basis, basis)
    qq = qq.reshape(160, 160)
    lam_ab = np.ones((10, 16))
    lam_ab[:, :10] = vals[:, None] + vals[None, :]
    lam_c = np.repeat(vals, ez)[None]
    zf = np.zeros((nz, 10, ez))
    g8 = np.zeros((nz, 8, ez))
    zk = np.zeros((nz, 8, ez))
    for elem in range(ez):
        for k in range(10):
            zf[(7 * elem - 1 + k) % nz, :, elem] += basis[k]
        for k in range(8):
            g8[(7 * elem + k) % nz, k, elem] += 1.0
            zk[(7 * elem + k) % nz, :, elem] += stiffness[:, k]
    zf, g8, zk = zf.reshape(nz, -1), g8.reshape(nz, -1), zk.reshape(nz, -1)
    diag = np.diag(weights)
    kk = np.einsum("ai,bj->abij", stiffness, diag) + np.einsum("ai,bj->abij", diag, stiffness)
    kk = kk.reshape(64, 64)
    ww = np.outer(weights, weights).reshape(64, 1)
    inner = np.zeros((8, 8))
    inner[1:7, 1:7] = 1.0
    owned = np.zeros((8, 8))
    owned[:7, :7] = 1.0
    plate = inner.reshape(64, 1)
    first = np.array([1.0] * 7 + [0.0])
    last = 1.0 - first
    k_parts = {}
    m_parts = {}
    for name, left, right in (("11", first, first), ("12", first, last), ("22", last, last)):
        wz = float(np.sum(left * weights * right))
        kz = float(left @ stiffness @ right)
        k_parts[name] = float((plate.T @ kk @ plate).item()) * wz + float(np.sum(plate * ww)) * kz
        m_parts[name] = float(np.sum(plate * ww)) * wz
    elems = np.arange(ez)
    per = ez // c_dev
    r1 = (elems[None, :] // per == np.arange(c_dev)[:, None]).astype(np.float64)
    r2 = (((elems[None, :] + 1) % ez) // per == np.arange(c_dev)[:, None]).astype(np.float64)
    wide = LANES // c_dev
    zc = (np.arange(nz)[:, None] // span == np.arange(c_dev)[None, :]).astype(np.float64)
    return dict(
        qq=f32(qq), qqt=f32(qq.T), zf=f32(zf), zft=f32(zf.T), lam_ab=f32(lam_ab.reshape(160, 1)), lam_c=f32(lam_c),
        rep10=f32(np.tile(np.eye(ez), (1, 10))), rep8=f32(np.tile(np.eye(ez), (1, 8))),
        g8=f32(g8), g8t=f32(g8.T), zk=f32(zk), kk=f32(kk), ww=f32(ww), wz=f32(np.repeat(weights, ez)[None]),
        inner=f32(plate), owned=f32(owned.reshape(64, 1)),
        r1=f32(r1), r2=f32(r2), r1t=f32(np.tile(r1.T, (1, wide))), r2t=f32(np.tile(r2.T, (1, wide))),
        zct=f32(np.tile(zc, (1, wide))), eye=f32(np.eye(LANES)),
        zl=f32(np.tile(zc.T, (wide, 1))),
        k_parts=k_parts, m_parts=m_parts,
    )


def run(kernel, outs, *args, scratch=()):
    shapes = [jax.ShapeDtypeStruct(shape, jnp.float32) for shape in outs]
    size = sum(math.prod(s) for s in outs) + sum(math.prod(a.shape) for a in args)
    return pl.pallas_call(
        kernel,
        out_shape=shapes,
        in_specs=[pl.BlockSpec(memory_space=pltpu.VMEM)] * len(args),
        out_specs=[pl.BlockSpec(memory_space=pltpu.VMEM)] * len(outs),
        scratch_shapes=[pltpu.VMEM(shape, jnp.float32) for shape in scratch],
        cost_estimate=pl.CostEstimate(flops=2 * 6 * 160 * 240 * 168, bytes_accessed=4 * size, transcendentals=0),
    )(*args)


def total(value):
    return jnp.sum(jnp.sum(value, axis=1, keepdims=True), axis=0, keepdims=True)


def total_row(row):
    return jnp.sum(row, axis=1, keepdims=True)


def as_col(row, eye):
    return jnp.sum(eye * row, axis=1, keepdims=True)


def as_row(col, eye):
    return jnp.sum(eye * col, axis=0, keepdims=True)


def lane_put(values):
    lane = lax.broadcasted_iota(jnp.int32, (1, LANES), 1)
    row = jnp.zeros((1, LANES), jnp.float32)
    for spot, value in enumerate(values):
        row = jnp.where(lane == spot, value, row)
    return row


def lane_get(row, spot):
    lane = lax.broadcasted_iota(jnp.int32, row.shape, 1)
    return jnp.sum(jnp.where(lane == spot, row, 0.0), axis=1, keepdims=True)


def rows_tile(rows):
    spot = lax.broadcasted_iota(jnp.int32, (8, LANES), 0)
    tile = jnp.zeros((8, LANES), jnp.float32)
    for place, row in enumerate(rows):
        tile = jnp.where(spot == place, row, tile)
    return tile


def first_kernel(k_parts, m_parts, width, b_ref, k_ref, m_ref, x_ref, sel_ref, r1_ref, r2_ref, r1t_ref, r2t_ref, zct_ref, out_ref):
    k, m = k_ref[...], m_ref[...]
    e11, e12, e22 = (k * k_parts[name] + m * m_parts[name] for name in ("11", "12", "22"))
    r1, r2 = r1_ref[...], r2_ref[...]
    sel = sel_ref[...]
    small = (dot(r1 * e11 + r2 * e12, r1t_ref[...]) + dot(r1 * e12 + r2 * e22, r2t_ref[...])) * sel
    acc = b_ref[1]
    for x in range(2, 7):
        acc = acc + b_ref[x]
    line = jnp.sum(acc[1:7], axis=0, keepdims=True)
    rc = dot(line, zct_ref[...]) * sel
    rc_tile = rows_tile([rc])
    for peer in range(out_ref.shape[0]):
        out_ref[peer, :, :width] = x_ref[:, peer * width : (peer + 1) * width]
        out_ref[peer, :, width : width + LANES] = small
        out_ref[peer, :, width + LANES :] = rc_tile


def split_group(xl_ref, width):
    rows = xl_ref.shape[0] * xl_ref.shape[1]
    wide = xl_ref[...].reshape(rows, xl_ref.shape[2])
    rc = jnp.sum(wide[:, width + LANES :], axis=0, keepdims=True)
    return wide[:, :width], wide[:, width : width + LANES], rc


def spread(out_ref, row):
    out_ref[...] = jnp.broadcast_to(row[None], out_ref.shape)


def coarse_in_kernel(width, xl_ref, eye_ref, out_ref):
    factor, _, rc = split_group(xl_ref, width)
    rows = factor.shape[0]
    rc_col = as_col(rc, eye_ref[:rows])
    part = jnp.sum(rc_col * factor, axis=0, keepdims=True)
    spread(out_ref, jnp.concatenate([part, jnp.zeros((1, LANES), jnp.float32)], axis=1))


def coarse_out_kernel(width, sums_ref, xl_ref, eye_ref, h_ref, out_ref):
    factor, _, _ = split_group(xl_ref, width)
    rows = factor.shape[0]
    sums = jnp.sum(sums_ref[...], axis=0)
    part = jnp.sum(factor * sums[:, :width], axis=1, keepdims=True)
    x_part = as_row(part, eye_ref[:rows])
    spot = lax.broadcasted_iota(jnp.int32, (8, LANES), 0)
    tile = jnp.where(spot == 0, x_part, h_ref[...])
    out_ref[...] = jnp.broadcast_to(tile[None], out_ref.shape)


def coarse_mid_kernel(width, got_ref, xl_ref, eye_ref, out_ref, x_ref):
    factor, small, rc = split_group(xl_ref, width)
    rows = factor.shape[0]
    eye = eye_ref[:rows]
    got = jnp.sum(got_ref[...], axis=0)
    x0, h, scal = got[0:1], got[1:2], got[2:3]
    rc1_col = jnp.sum(small * x0 + eye * h, axis=1, keepdims=True)
    rc1 = as_row(rc1_col, eye)
    part = jnp.sum(rc1_col * factor, axis=0, keepdims=True)
    rho = lane_get(scal, 0) + total_row(rc * x0)
    den = lane_get(scal, 1) + total_row(x0 * (h + rc1))
    spread(out_ref, jnp.concatenate([part, lane_put([rho, den])], axis=1))
    x_ref[...] = x0


def pair_kernel(width, sums_ref, xl_ref, eye_ref, b_ref, q_ref, u_ref, au_ref, s_ref, as_ref, inner_ref, owned_ref, zct_ref, sel_ref,
                out_ref, scal_ref, r_ref, qo_ref):
    factor, _, _ = split_group(xl_ref, width)
    rows = factor.shape[0]
    sums = jnp.sum(sums_ref[...], axis=0)
    part = jnp.sum(factor * sums[:, :width], axis=1, keepdims=True)
    x_part = as_row(part, eye_ref[:rows])
    scal = sums[:, width:]
    rho, den = lane_get(scal, 0), lane_get(scal, 1)
    step = rho / den
    for x in range(7):
        qo = q_ref[x + 1, 1:8]
        qo_ref[x, :7] = qo
        r_ref[x, :7] = b_ref[x] - step * qo
        qo_ref[x, 7:] = jnp.zeros_like(qo_ref[x, 7:])
        r_ref[x, 7:] = jnp.zeros_like(r_ref[x, 7:])
    qo_ref[7] = jnp.zeros_like(qo_ref[7])
    r_ref[7] = jnp.zeros_like(r_ref[7])
    nz = b_ref.shape[2]
    flat = lambda ref: ref[...].reshape(64, nz)
    resid = flat(r_ref)
    t = flat(u_ref) - step * flat(s_ref)
    at = flat(au_ref) - step * flat(as_ref)
    inner = inner_ref[...]
    wr = dot(jnp.sum(inner * resid, axis=0, keepdims=True), zct_ref[...]) * sel_ref[...]
    wt = dot(jnp.sum(inner * at, axis=0, keepdims=True), zct_ref[...]) * sel_ref[...]
    tile = rows_tile([x_part, wr, wt, lane_put([total(resid * t), total(t * at)])])
    out_ref[...] = jnp.broadcast_to(tile[None], out_ref.shape)
    scal_ref[...] = lane_put([rho, den])


def last_in_kernel(width, got_ref, xl_ref, x0_ref, scal_ref, eye_ref, out_ref, x_ref):
    _, small, _ = split_group(xl_ref, width)
    eye = eye_ref[: small.shape[0]]
    got = jnp.sum(got_ref[...], axis=0)
    x1, wr, wt, scal = got[0:1], got[1:2], got[2:3], got[3:4]
    step = lane_get(scal_ref[...], 0) / lane_get(scal_ref[...], 1)
    c = x0_ref[...] - step * x1
    tc = as_row(jnp.sum(small * c, axis=1, keepdims=True), eye)
    rho1 = lane_get(scal, 0) + total_row(wr * c)
    en1 = lane_get(scal, 1) + total_row(c * (2.0 * wt + tc))
    spread(out_ref, lane_put([rho1, en1]))
    x_ref[...] = x1


def final_kernel(sums_ref, scal_ref, p_ref, w_ref, r_ref, qo_ref, v_ref, vl_ref, sol_ref, res_ref):
    got = jnp.sum(sums_ref[...], axis=0)
    rho1, en1 = lane_get(got, 0), lane_get(got, 1)
    rho, den = lane_get(scal_ref[...], 0), lane_get(scal_ref[...], 1)
    step = rho / den
    beta = rho1 / rho
    step1 = rho1 / (en1 - beta * rho1 / step)
    p_mult = step + step1 * (1.0 + beta)
    w_mult = step1 * step
    q_mult = step1 * (1.0 + beta)
    for x in range(7):
        sol_ref[x] = p_mult * p_ref[x, :7] - w_mult * w_ref[x, :7]
        top = w_mult * vl_ref[x]
        res_ref[x] = r_ref[x, :7] - q_mult * qo_ref[x, :7] + w_mult * v_ref[x, :7]
        res_ref[x, 0:1] = res_ref[x, 0:1] + top


def solve(block, k, m, rep10, lam_ab, lam_c, qq, qqt, zf, zft):
    den = dot(k, rep10) * (lam_ab + lam_c) + dot(m, rep10)
    spectral = dot(dot(qqt, block), zf) / den
    return dot(dot(qq, spectral), zft)


SOLVE = ("rep10", "lam_ab", "lam_c", "qq", "qqt", "zf", "zft")
APPLY = ("rep8", "wz", "g8", "g8t", "zk", "kk", "ww")


def apply(block, k, m, rep8, wz, g8, g8t, zk, kk, ww):
    k_line, m_line = dot(k, rep8), dot(m, rep8) * wz
    spread_u = dot(block, g8)
    out = (k_line * wz) * dot(kk, spread_u) + ww * (k_line * dot(block, zk) + m_line * spread_u)
    return dot(out, g8t)


def schwarz_b_kernel(bx_ref, yl_ref, yh_ref, k_ref, m_ref, *refs):
    consts, (out_ref, hi_ref, lo_ref, scr) = refs[:-4], refs[-4:]
    scr[...] = jnp.zeros_like(scr)
    scr[:, 1:8] = bx_ref[...]
    scr[:, 0:1] = yl_ref[...]
    scr[:, 8:10] = yh_ref[...]
    schwarz_tail(scr, k_ref, m_ref, consts, out_ref, hi_ref, lo_ref)


def schwarz_q_kernel(qx_ref, yl_ref, yh_ref, k_ref, m_ref, *refs):
    consts, (q_ref, out_ref, hi_ref, lo_ref) = refs[:-4], refs[-4:]
    q_ref[...] = jnp.zeros_like(q_ref)
    q_ref[:, 1:9] = qx_ref[...]
    q_ref[:, 0:1] = yl_ref[:, 0:1]
    q_ref[:, 1:2] = q_ref[:, 1:2] + yl_ref[:, 1:2]
    q_ref[:, 8:9] = q_ref[:, 8:9] + yh_ref[:, 0:1]
    q_ref[:, 9:10] = yh_ref[:, 1:2]
    schwarz_tail(q_ref, k_ref, m_ref, consts, out_ref, hi_ref, lo_ref)


def schwarz_tail(src, k_ref, m_ref, consts, out_ref, hi_ref, lo_ref):
    nz = src.shape[2]
    block = solve(src[...].reshape(160, nz), k_ref[...], m_ref[...], *(ref[...] for ref in consts))
    block = block.reshape(10, 16, nz)
    out_ref[...] = block
    hi_ref[...] = block[8:10]
    lo_ref[...] = block[0:2]


def fold_s_kernel(y_ref, xl_ref, xh_ref, out_ref, hi_ref, lo_ref):
    out_ref[0:2] = y_ref[1:3] + xl_ref[...]
    out_ref[2:6] = y_ref[3:7]
    out_ref[6:8] = y_ref[7:9] + xh_ref[...]
    hi_ref[...] = out_ref[:, 8:10]
    lo_ref[...] = out_ref[:, 0:2]


def fold_a_kernel(q_ref, xl_ref, xh_ref, out_ref, hi_ref, lo_ref):
    out_ref[0] = xl_ref[0]
    out_ref[1] = q_ref[0] + xl_ref[1]
    out_ref[2:8] = q_ref[1:7]
    out_ref[8] = q_ref[7] + xh_ref[0]
    out_ref[9] = xh_ref[1]
    hi_ref[...] = out_ref[:, 6:8]
    lo_ref[...] = out_ref[:, 0:2]


def fold_b_kernel(b_ref, xl_ref, xh_ref, out_ref, hi_ref, lo_ref):
    out_ref[0:1] = xl_ref[...]
    out_ref[1:8] = b_ref[...]
    out_ref[8:10] = xh_ref[...]
    hi_ref[...] = out_ref[:, 6:7]
    lo_ref[...] = out_ref[:, 0:2]


def fold_v_kernel(v_ref, xl_ref, out_ref, hi_ref):
    out_ref[...] = v_ref[0:7]
    out_ref[0] = out_ref[0] + xl_ref[0]
    hi_ref[...] = out_ref[:, 7:8]


def gather_s(u_ref, y_ref, yl_ref, yh_ref):
    u_ref[...] = y_ref[:, 1:9]
    u_ref[:, 0:2] = u_ref[:, 0:2] + yl_ref[...]
    u_ref[:, 6:8] = u_ref[:, 6:8] + yh_ref[...]


def apply_u_kernel(b_ref, y_ref, yl_ref, yh_ref, k_ref, m_ref, inner_ref, zct_ref, sel_ref, *refs):
    consts, (u_ref, au_ref, h_ref) = refs[:-3], refs[-3:]
    nz = u_ref.shape[2]
    gather_s(u_ref, y_ref, yl_ref, yh_ref)
    u = u_ref[...].reshape(64, nz)
    au = apply(u, k_ref[...], m_ref[...], *(ref[...] for ref in consts))
    au_ref[...] = au.reshape(8, 8, nz)
    h = dot(jnp.sum(inner_ref[...] * au, axis=0, keepdims=True), zct_ref[...]) * sel_ref[...]
    acc = b_ref[0] * u_ref[0, :7]
    for x in range(1, 7):
        acc = acc + b_ref[x] * u_ref[x, :7]
    h_ref[...] = rows_tile([jnp.zeros((1, LANES), jnp.float32), h, lane_put([total(acc), total(u * au)])])


def apply_s_kernel(y_ref, yl_ref, yh_ref, k_ref, m_ref, *refs):
    consts, (s_ref, as_ref) = refs[:-2], refs[-2:]
    nz = s_ref.shape[2]
    gather_s(s_ref, y_ref, yl_ref, yh_ref)
    out = apply(s_ref[...].reshape(64, nz), k_ref[...], m_ref[...], *(ref[...] for ref in consts))
    as_ref[...] = out.reshape(8, 8, nz)


def apply_p_kernel(u_ref, x_ref, k_ref, m_ref, inner_ref, zl_ref, sel_ref, eye_ref, *refs):
    consts, (p_ref, q_ref, hi_ref, lo_ref) = refs[:-4], refs[-4:]
    nz = u_ref.shape[2]
    col = as_col(x_ref[...] * sel_ref[...], eye_ref[...])
    line = jnp.sum(col * zl_ref[...], axis=0, keepdims=True)
    p = u_ref[...].reshape(64, nz) + inner_ref[...] * line
    p_ref[...] = p.reshape(8, 8, nz)
    out = apply(p, k_ref[...], m_ref[...], *(ref[...] for ref in consts)).reshape(8, 8, nz)
    q_ref[...] = out
    hi_ref[...] = out[8 - hi_ref.shape[0] :]
    lo_ref[...] = out[0:2]


def shift(value, axis, step):
    count = lax.axis_size(axis)
    return lax.ppermute(value, axis, [(i, (i + step) % count) for i in range(count)])


def local(right_side, stiff_coef, mass_coef, coarse_factor):
    nz = right_side.shape[2]
    c_dev, n_coarse = coarse_factor.shape
    ez = stiff_coef.shape[2]
    n_gx, n_gy = lax.axis_size("gx"), lax.axis_size("gy")
    width = n_coarse // n_gx
    tab = {name: jnp.asarray(value) if isinstance(value, np.ndarray) else value for name, value in make_tables(ez, c_dev).items()}
    k = stiff_coef.reshape(1, ez)
    m = mass_coef.reshape(1, ez)
    b = right_side
    sel = (jnp.arange(LANES)[None] // c_dev == lax.axis_index("gx")).astype(jnp.float32)
    solve_tab = [tab[name] for name in SOLVE]
    apply_tab = [tab[name] for name in APPLY]
    inner, owned, zct, zl, eye = (tab[name] for name in ("inner", "owned", "zct", "zl", "eye"))

    def kernel(fn, *fixed):
        def call(*refs):
            return fn(*fixed, *refs)

        call.__name__ = fn.__name__
        return call

    def swap_gx(value):
        return lax.all_to_all(value, "gx", 0, 0)

    def swap_gy(value):
        return lax.all_to_all(value, "gy", 0, 0)

    group = (n_gx, c_dev, LANES)
    (pay,) = run(kernel(first_kernel, tab["k_parts"], tab["m_parts"], width), [(n_gx, c_dev, width + 2 * LANES)],
                 b, k, m, coarse_factor, sel, tab["r1"], tab["r2"], tab["r1t"], tab["r2t"], zct)
    b_low, b_high = shift(b[6:7], "gx", 1), shift(b[0:2], "gx", -1)
    xl = swap_gx(pay)

    (pay,) = run(kernel(coarse_in_kernel, width), [(n_gy, 1, width + LANES)], xl, eye)
    sums = swap_gy(pay)

    bx, hi, lo = run(fold_b_kernel, [(10, 7, nz), (10, 1, nz), (10, 2, nz)], b, b_low, b_high)
    y_low, y_high = shift(hi, "gy", 1), shift(lo, "gy", -1)

    strips = [(2, 16, nz), (2, 16, nz)]
    sides = [(8, 2, nz), (8, 2, nz)]
    y, hi, lo = run(schwarz_b_kernel, [(10, 16, nz)] + strips, bx, y_low, y_high, k, m, *solve_tab, scratch=[(10, 16, nz)])
    x_low, x_high = shift(hi, "gx", 1), shift(lo, "gx", -1)
    y, hi, lo = run(fold_s_kernel, [(8, 16, nz)] + sides, y, x_low, x_high)
    y_low, y_high = shift(hi, "gy", 1), shift(lo, "gy", -1)
    cube = (8, 8, nz)
    u, au, h = run(apply_u_kernel, [cube, cube, (8, LANES)], b, y, y_low, y_high, k, m, inner, zct, sel, *apply_tab)

    (pay,) = run(kernel(coarse_out_kernel, width), [group], sums, xl, eye, h)
    got = swap_gx(pay)
    pay, x0 = run(kernel(coarse_mid_kernel, width), [(n_gy, 1, width + LANES), (1, LANES)], got, xl, eye)
    sums = swap_gy(pay)

    p, q, hi, lo = run(apply_p_kernel, [cube, cube, (2, 8, nz), (2, 8, nz)], u, x0, k, m, inner, zl, sel, eye, *apply_tab)
    x_low, x_high = shift(hi, "gx", 1), shift(lo, "gx", -1)
    qx, hi, lo = run(fold_a_kernel, [(10, 8, nz), (10, 2, nz), (10, 2, nz)], q, x_low, x_high)
    y_low, y_high = shift(hi, "gy", 1), shift(lo, "gy", -1)
    q, y, hi, lo = run(schwarz_q_kernel, [(10, 16, nz), (10, 16, nz)] + strips, qx, y_low, y_high, k, m, *solve_tab)
    x_low, x_high = shift(hi, "gx", 1), shift(lo, "gx", -1)
    y, hi, lo = run(fold_s_kernel, [(8, 16, nz)] + sides, y, x_low, x_high)
    y_low, y_high = shift(hi, "gy", 1), shift(lo, "gy", -1)
    s, a_s = run(apply_s_kernel, [cube, cube], y, y_low, y_high, k, m, *apply_tab)

    pay, scal, resid, q_own = run(kernel(pair_kernel, width), [group, (1, LANES), cube, cube],
                                  sums, xl, eye, b, q, u, au, s, a_s, inner, owned, zct, sel)
    got = swap_gx(pay)
    pay, x1 = run(kernel(last_in_kernel, width), [(n_gy, 1, LANES), (1, LANES)], got, xl, x0, scal, eye)
    sums = swap_gy(pay)

    w, v, hi, _ = run(apply_p_kernel, [cube, cube, (1, 8, nz), (2, 8, nz)], s, x1, k, m, inner, zl, sel, eye, *apply_tab)
    x_low = shift(hi, "gx", 1)
    v, hi = run(fold_v_kernel, [(7, 8, nz), (7, 1, nz)], v, x_low)
    y_low = shift(hi, "gy", 1)
    sol, res = run(final_kernel, [(7, 7, nz), (7, 7, nz)], sums, scal, p, w, resid, q_own, v, y_low)
    return sol, res


def solution(mesh):
    placed = (P("gx", "gy", None), P("gx", "gy", None), P("gx", "gy", None), P(("gx", "gy"), None))
    return jax.shard_map(
        local,
        mesh=mesh,
        in_specs=placed,
        out_specs=(P("gx", "gy", None), P("gx", "gy", None)),
        check_vma=False,
    )
```

time: 769 us -> 255 us (0.33)
  blocking collectives: 470 us -> 41.9 us
  starting transfers between devices: 176 us -> 127 us
  Pallas kernels: 0 us -> 40.1 us
  waiting for transfers between devices: 69.3 us -> 33.2 us
  matrix products: 17.5 us -> 0 us
  other arithmetic: 10.7 us -> 0.55 us
  local copies, waits for them, and re-layouts: 18.2 us -> 9.43 us
    psum x3 -> x0, blocking collectives: 470 us -> none  [global_dot(): return lax.psum(jnp.sum(left_term * right_term), ('gx', 'gy'))]
    ppermute x40 -> x18, starting transfers between devices: 176 us -> 46.5 us  [shift(): lax.ppermute(value, axis, [(i, (i + step) % count) for i in range(count)])]
    all_to_all x0 -> x3, starting transfers between devices: none -> 80.7 us  [swap_gy(): return lax.all_to_all(value, 'gy', 0, 0)]
    all_to_all x0 -> x3, blocking collectives: none -> 41.9 us  [swap_gx(): return lax.all_to_all(value, 'gx', 0, 0)]
    ppermute x40 -> x18, waiting for transfers between devices: 69.3 us -> 27.5 us  [shift(): lax.ppermute(value, axis, [(i, (i + step) % count) for i in range(count)])]
    pallas_call x0 -> x18, Pallas kernels: none -> 40.1 us  [run(): pl.pallas_call(kernel, out_shape=shapes, in_specs=[pl.BlockSpec(memory_sp...]
    dot_general x22 -> x0, matrix products: 17.5 us -> none  [the longest x2 2.4 us: local_solve(): jnp.einsum('bj,ajte->abte', eigen_basis, restored, precision=exact_mode)]
    unnamed x51 -> x42, local copies, waits for them, and re-layouts: 0.28 us -> 8 us
  transfers between devices with their start and end apart: 40 -> 21, of which waited for: 24 -> 16; matrix products, arithmetic and copies ran while one was open for 3% -> 1% of each run, Pallas kernels for 0% -> 10%
where the time goes in v1:
time: 255 us; the launch traced here: 253 us
  starting transfers between devices  127 us (50%)
  blocking collectives  41.9 us (16%)
  Pallas kernels  40.1 us (16%)
  waiting for transfers between devices  33.2 us (13%)
  local copies, waits for them, and re-layouts  9.43 us (4%)
    all_to_all x3, starting transfers between devices, swap_gy(): return lax.all_to_all(value, 'gy', 0, 0)  80.7 us
    ppermute x18, starting transfers between devices, shift(): lax.ppermute(value, axis, [(i, (i + step) % count) for i in range(count)])  46.5 us
    all_to_all x3, blocking collectives, swap_gx(): return lax.all_to_all(value, 'gx', 0, 0)  41.9 us
    pallas_call x18, Pallas kernels, run(): pl.pallas_call(kernel, out_shape=shapes, in_specs=[pl.BlockSpec(memory_sp...  40.1 us
    ppermute x18, waiting for transfers between devices, shift(): lax.ppermute(value, axis, [(i, (i + step) % count) for i in range(count)])  27.5 us
    unnamed x42, local copies, waits for them, and re-layouts  8 us
    all_to_all x3, waiting for transfers between devices, swap_gy(): return lax.all_to_all(value, 'gy', 0, 0)  5.69 us
  transfers between devices with their start and end apart: 21, of which 16 were waited for; matrix products, arithmetic and copies ran while one was open for 1% of the time, Pallas kernels for 10%

profile of v1, /device:TPU:1, one launch (start us, length us, event | category | flops | bytes accessed | tf_op | source)
XLA Modules:
  0.0 253.2 jit_solution(17447976751781965696)
XLA Ops:
  3.3 15.7 %all_to_all.30.refs_0_.refs_1_ = f32[16,8,768]{2,1,0:T(8,128)} all-to-all(f32[16,8,768]{2,1,0:T(8,128)} %shard_map.266), channel_id=1, replica_groups=mesh['gx'=16,'gy'=64] {'gx'}, dimensions={0} | all-to-all | bytes 786432 | tf_op jit(solution)/shard_map/all_to_all | solution.py:485
  20.7 31.7 %all-to-all-start.1 = ((f32[64,1,640]{2,1,0:T(1,128)}), f32[64,1,640]{2,1,0:T(1,128)S(1)}, u32[]{:S(2)}, u32[]{:S(2)}) async-start(f32[64,1,640]{2,1,0:T(1,128)} %shard_map.267), calls=%async_computation.1 | async-start | bytes 327680 | tf_op jit(solution)/shard_map/all_to_all | solution.py:488
  53.2 3.0 %collective-permute-start.1 = (f32[2,7,168]{2,1,0:T(8,128)S(1)}, f32[2,7,168]{2,1,0:T(8,128)S(1)}, u32[]{:S(2)}, u32[]{:S(2)}) collective-permute-start(f32[2,7,168]{2,1,0:T(8,128)S(1)} %slice.7), channel_id=1, source_target_pairs={{0,960},{64,0},{128,64},{192,128},{256,192},{320,256},{384,320},{4... | collective-permute-start | bytes 28232 | tf_op jit(solution)/shard_map/ppermute | solution.py:459
  59.1 5.7 %collective-permute-done.xl_ref = f32[1,7,168]{2,1,0:T(8,128)S(1)} collective-permute-done((f32[1,7,168]{2,1,0:T(8,128)S(1)}, f32[1,7,168]{2,1,0:T(8,128)S(1)}, u32[]{:S(2)}, u32[]{:S(2)}) %collective-permute-start) | collective-permute-done | bytes 4736 | tf_op jit(solution)/shard_map/ppermute | solution.py:459
  73.1 3.5 %shard_map.269 = (f32[10,16,168]{2,1,0:T(8,128)}, f32[2,16,168]{2,1,0:T(8,128)}, f32[2,16,168]{2,1,0:T(8,128)}) custom-call(f32[10,7,168]{2,1,0:T(8,128)} %get-tuple-element.43.bx_ref, f32[10,1,168]{2,1,0:T(1,128)} %copy-done.10, f32[10,2,168]{2,1,0:T(2,128)} %copy-done.5, f32[1,24]{1,0:T(1,128)} %bitcast.3, f32[1,24]{1,0:T(1,128)} %bitcast.10, ...), custom_call_target="tpu_custom_call" | custom-call | flops 77414400 | bytes 769920 | tf_op jit(solution)/shard_map/pallas_call | solution.py:166
  78.5 6.7 %collective-permute-start.5 = (f32[2,16,168]{2,1,0:T(8,128)}, f32[2,16,168]{2,1,0:T(8,128)S(1)}, u32[]{:S(2)}, u32[]{:S(2)}) collective-permute-start(f32[2,16,168]{2,1,0:T(8,128)} %get-tuple-element.48), channel_id=1, source_target_pairs={{0,960},{64,0},{128,64},{192,128},{256,192},{320,256},{384,320},{4... | collective-permute-start | bytes 64520 | tf_op jit(solution)/shard_map/ppermute | solution.py:459
  95.0 3.0 %shard_map.271 = (f32[8,8,168]{2,1,0:T(8,128)}, f32[8,8,168]{2,1,0:T(8,128)}, f32[8,128]{1,0:T(8,128)}) custom-call(f32[7,7,168]{2,1,0:T(8,128)} %refs_3_.9, f32[8,16,168]{2,1,0:T(8,128)} %get-tuple-element.49.y_ref, f32[8,2,168]{2,1,0:T(2,128)} %copy-done.6, f32[8,2,168]{2,1,0:T(2,128)} %copy-done.7, f32[1,24]{1,0:T(1,128)} %bitcast.4, f32[1,24]{1,0:T(1,128)} %bitcast.11, ...), custom_call_target="tpu_custom_call" | custom-call | flops 77414400 | bytes 740448 | tf_op jit(solution)/shard_map/pallas_call | solution.py:166
  100.6 13.3 %all_to_all.31.refs_0_ = f32[16,8,128]{2,1,0:T(8,128)} all-to-all(f32[16,8,128]{2,1,0:T(8,128)} %shard_map.272), channel_id=1, replica_groups=mesh['gx'=16,'gy'=64] {'gx'}, dimensions={0} | all-to-all | bytes 131072 | tf_op jit(solution)/shard_map/all_to_all | solution.py:485
  115.8 24.5 %all-to-all-start.3 = ((f32[64,1,640]{2,1,0:T(1,128)}), f32[64,1,640]{2,1,0:T(1,128)S(1)}, u32[]{:S(2)}, u32[]{:S(2)}) async-start(f32[64,1,640]{2,1,0:T(1,128)} %get-tuple-element.53), calls=%async_computation.3 | async-start | bytes 327680 | tf_op jit(solution)/shard_map/all_to_all | solution.py:488
  140.3 2.9 %shard_map.274 = (f32[8,8,168]{2,1,0:T(8,128)}, f32[8,8,168]{2,1,0:T(8,128)}, f32[2,8,168]{2,1,0:T(8,128)}, f32[2,8,168]{2,1,0:T(8,128)}) custom-call(f32[8,8,168]{2,1,0:T(8,128)} %get-tuple-element.54.u_ref.refs_5_, f32[1,128]{1,0:T(1,128)} %get-tuple-element.55.x_ref.refs_2_, f32[1,24]{1,0:T(1,128)} %bitcast.5, f32[1,24]{1,0:T(1,128)} %bitcast.12, ...), custom_call_target="tpu_custom_call" | custom-call | flops 77414400 | bytes 726464 | tf_op jit(solution)/shard_map/pallas_call | solution.py:166
  145.4 6.4 %collective-permute-start.9 = (f32[2,8,168]{2,1,0:T(8,128)}, f32[2,8,168]{2,1,0:T(8,128)S(1)}, u32[]{:S(2)}, u32[]{:S(2)}) collective-permute-start(f32[2,8,168]{2,1,0:T(8,128)} %get-tuple-element.58), channel_id=1, source_target_pairs={{0,960},{64,0},{128,64},{192,128},{256,192},{320,256},{384,320},{4... | collective-permute-start | bytes 32264 | tf_op jit(solution)/shard_map/ppermute | solution.py:459
  155.0 2.8 %collective-permute-start.10 = (f32[10,2,168]{2,1,0:T(2,128)}, f32[10,2,168]{2,1,0:T(2,128)S(1)}, u32[]{:S(2)}, u32[]{:S(2)}) collective-permute-start(f32[10,2,168]{2,1,0:T(2,128)} %get-tuple-element.60), channel_id=1, source_target_pairs={{0,1},{1,2},{2,3},{3,4},{4,5},{5,6},{6,7},{7,8},{8,9},{9,10},{10,1... | collective-permute-start | bytes 40328 | tf_op jit(solution)/shard_map/ppermute | solution.py:459
  158.9 2.6 %collective-permute-done.11.yh_ref = f32[10,2,168]{2,1,0:T(2,128)S(1)} collective-permute-done((f32[10,2,168]{2,1,0:T(2,128)}, f32[10,2,168]{2,1,0:T(2,128)S(1)}, u32[]{:S(2)}, u32[]{:S(2)}) %collective-permute-start.11) | collective-permute-done | bytes 13472 | tf_op jit(solution)/shard_map/ppermute | solution.py:459
  162.1 3.5 %shard_map.276 = (f32[10,16,168]{2,1,0:T(8,128)}, f32[10,16,168]{2,1,0:T(8,128)}, f32[2,16,168]{2,1,0:T(8,128)}, f32[2,16,168]{2,1,0:T(8,128)}) custom-call(f32[10,8,168]{2,1,0:T(8,128)} %get-tuple-element.59.qx_ref, f32[10,2,168]{2,1,0:T(2,128)} %copy-done.3, f32[10,2,168]{2,1,0:T(2,128)} %copy-done.4, f32[1,24]{1,0:T(1,128)} %bitcast.6, f32[1,24]{1,0:T(1,128)} %bitcast.13, ...), custom_call_target="tpu_custom_call" | custom-call | flops 77414400 | bytes 890880 | tf_op jit(solution)/shard_map/pallas_call | solution.py:166
  167.5 7.2 %collective-permute-start.13 = (f32[2,16,168]{2,1,0:T(8,128)}, f32[2,16,168]{2,1,0:T(8,128)S(1)}, u32[]{:S(2)}, u32[]{:S(2)}) collective-permute-start(f32[2,16,168]{2,1,0:T(8,128)} %get-tuple-element.66), channel_id=1, source_target_pairs={{0,960},{64,0},{128,64},{192,128},{256,192},{320,256},{384,320},{4... | collective-permute-start | bytes 64520 | tf_op jit(solution)/shard_map/ppermute | solution.py:459
  180.0 2.6 %collective-permute-done.15.yh_ref = f32[8,2,168]{2,1,0:T(2,128)S(1)} collective-permute-done((f32[8,2,168]{2,1,0:T(2,128)}, f32[8,2,168]{2,1,0:T(2,128)S(1)}, u32[]{:S(2)}, u32[]{:S(2)}) %collective-permute-start.15) | collective-permute-done | bytes 10784 | tf_op jit(solution)/shard_map/ppermute | solution.py:459
  183.2 2.8 %shard_map.278 = (f32[8,8,168]{2,1,0:T(8,128)}, f32[8,8,168]{2,1,0:T(8,128)}) custom-call(f32[8,16,168]{2,1,0:T(8,128)} %get-tuple-element.67.y_ref, f32[8,2,168]{2,1,0:T(2,128)} %copy-done.8, f32[8,2,168]{2,1,0:T(2,128)} %copy-done.9, f32[1,24]{1,0:T(1,128)} %bitcast.7, f32[1,24]{1,0:T(1,128)} %bitcast.14, f32[24,192]{1,0:T(8,128)} %constant.77.clone.refs_0_, ...), custom_call_target="tpu_custom_call" | custom-call | flops 77414400 | bytes 616640 | tf_op jit(solution)/shard_map/pallas_call | solution.py:166
  186.7 2.3 shard_map.279
  189.0 13.0 %all_to_all.32.refs_0_ = f32[16,8,128]{2,1,0:T(8,128)} all-to-all(f32[16,8,128]{2,1,0:T(8,128)} %get-tuple-element.72), channel_id=1, replica_groups=mesh['gx'=16,'gy'=64] {'gx'}, dimensions={0} | all-to-all | bytes 131072 | tf_op jit(solution)/shard_map/all_to_all | solution.py:485
  203.9 24.5 %all-to-all-start.5 = ((f32[64,1,128]{2,1,0:T(1,128)}), f32[64,1,128]{2,1,0:T(1,128)S(1)}, u32[]{:S(2)}, u32[]{:S(2)}) async-start(f32[64,1,128]{2,1,0:T(1,128)} %get-tuple-element.74), calls=%async_computation.5 | async-start | bytes 65536 | tf_op jit(solution)/shard_map/all_to_all | solution.py:488
  228.5 2.9 %shard_map.281 = (f32[8,8,168]{2,1,0:T(8,128)}, f32[8,8,168]{2,1,0:T(8,128)}, f32[1,8,168]{2,1,0:T(8,128)}, f32[2,8,168]{2,1,0:T(8,128)}) custom-call(f32[8,8,168]{2,1,0:T(8,128)} %get-tuple-element.70.refs_7_.u_ref, f32[1,128]{1,0:T(1,128)} %get-tuple-element.76.x_ref, f32[1,24]{1,0:T(1,128)} %bitcast.8, f32[1,24]{1,0:T(1,128)} %bitcast.15, ...), custom_call_target="tpu_custom_call" | custom-call | flops 77414400 | bytes 721088 | tf_op jit(solution)/shard_map/pallas_call | solution.py:166
  233.6 6.0 %collective-permute-done.16.xl_ref = f32[1,8,168]{2,1,0:T(8,128)S(1)} collective-permute-done((f32[1,8,168]{2,1,0:T(8,128)}, f32[1,8,168]{2,1,0:T(8,128)S(1)}, u32[]{:S(2)}, u32[]{:S(2)}) %collective-permute-start.16) | collective-permute-done | bytes 5408 | tf_op jit(solution)/shard_map/ppermute | solution.py:459
  241.6 2.5 collective-permute-start.17
  245.1 5.7 %all-to-all-done.5.sums_ref = f32[64,1,128]{2,1,0:T(1,128)S(1)} async-done(((f32[64,1,128]{2,1,0:T(1,128)}), f32[64,1,128]{2,1,0:T(1,128)S(1)}, u32[]{:S(2)}, u32[]{:S(2)}) %all-to-all-start.5) | async-done | bytes 32800 | tf_op jit(solution)/shard_map/all_to_all | solution.py:488
  (84 shorter events, 57.7 us)
Async XLA Ops:
  20.7 77.3 %all-to-all-start.1 = ((f32[64,1,640]{2,1,0:T(1,128)}), f32[64,1,640]{2,1,0:T(1,128)S(1)}, u32[]{:S(2)}, u32[]{:S(2)}) async-start(f32[64,1,640]{2,1,0:T(1,128)} %shard_map.267), calls=%async_computation.1 | async-start | bytes 327680 | tf_op jit(solution)/shard_map/all_to_all | solution.py:488
  53.2 11.7 %collective-permute-start.1 = (f32[2,7,168]{2,1,0:T(8,128)S(1)}, f32[2,7,168]{2,1,0:T(8,128)S(1)}, u32[]{:S(2)}, u32[]{:S(2)}) collective-permute-start(f32[2,7,168]{2,1,0:T(8,128)S(1)} %slice.7), channel_id=1, source_target_pairs={{0,960},{64,0},{128,64},{192,128},{256,192},{320,256},{384,320},{4... | collective-permute-start | bytes 28232 | tf_op jit(solution)/shard_map/ppermute | solution.py:459
  56.9 8.0 %collective-permute-start = (f32[1,7,168]{2,1,0:T(8,128)S(1)}, f32[1,7,168]{2,1,0:T(8,128)S(1)}, u32[]{:S(2)}, u32[]{:S(2)}) collective-permute-start(f32[1,7,168]{2,1,0:T(8,128)S(1)} %slice.6), channel_id=1, source_target_pairs={{0,64},{64,128},{128,192},{192,256},{256,320},{320,384},{384,448},... | collective-permute-start | bytes 14120 | tf_op jit(solution)/shard_map/ppermute | solution.py:459
  67.6 4.9 %collective-permute-start.3 = (f32[10,2,168]{2,1,0:T(2,128)}, f32[10,2,168]{2,1,0:T(2,128)S(1)}, u32[]{:S(2)}, u32[]{:S(2)}) collective-permute-start(f32[10,2,168]{2,1,0:T(2,128)} %get-tuple-element.45), channel_id=1, source_target_pairs={{0,63},{1,0},{2,1},{3,2},{4,3},{5,4},{6,5},{7,6},{8,7},{9,8},{10,9... | collective-permute-start | bytes 40328 | tf_op jit(solution)/shard_map/ppermute | solution.py:459
  69.1 2.6 %collective-permute-start.2 = (f32[10,1,168]{2,1,0:T(1,128)}, f32[10,1,168]{2,1,0:T(1,128)S(1)}, u32[]{:S(2)}, u32[]{:S(2)}) collective-permute-start(f32[10,1,168]{2,1,0:T(1,128)} %get-tuple-element.44), channel_id=1, source_target_pairs={{0,1},{1,2},{2,3},{3,4},{4,5},{5,6},{6,7},{7,8},{8,9},{9,10},{10,1... | collective-permute-start | bytes 20168 | tf_op jit(solution)/shard_map/ppermute | solution.py:459
  76.5 8.6 %collective-permute-start.4 = (f32[2,16,168]{2,1,0:T(8,128)}, f32[2,16,168]{2,1,0:T(8,128)S(1)}, u32[]{:S(2)}, u32[]{:S(2)}) collective-permute-start(f32[2,16,168]{2,1,0:T(8,128)} %get-tuple-element.47), channel_id=1, source_target_pairs={{0,64},{64,128},{128,192},{192,256},{256,320},{320,384},{384,448},... | collective-permute-start | bytes 64520 | tf_op jit(solution)/shard_map/ppermute | solution.py:459
  78.5 8.0 %collective-permute-start.5 = (f32[2,16,168]{2,1,0:T(8,128)}, f32[2,16,168]{2,1,0:T(8,128)S(1)}, u32[]{:S(2)}, u32[]{:S(2)}) collective-permute-start(f32[2,16,168]{2,1,0:T(8,128)} %get-tuple-element.48), channel_id=1, source_target_pairs={{0,960},{64,0},{128,64},{192,128},{256,192},{320,256},{384,320},{4... | collective-permute-start | bytes 64520 | tf_op jit(solution)/shard_map/ppermute | solution.py:459
  88.7 4.9 %collective-permute-start.6 = (f32[8,2,168]{2,1,0:T(2,128)}, f32[8,2,168]{2,1,0:T(2,128)S(1)}, u32[]{:S(2)}, u32[]{:S(2)}) collective-permute-start(f32[8,2,168]{2,1,0:T(2,128)} %get-tuple-element.50), channel_id=1, source_target_pairs={{0,1},{1,2},{2,3},{3,4},{4,5},{5,6},{6,7},{7,8},{8,9},{9,10},{10,1... | collective-permute-start | bytes 32264 | tf_op jit(solution)/shard_map/ppermute | solution.py:459
  91.0 3.4 %collective-permute-start.7 = (f32[8,2,168]{2,1,0:T(2,128)}, f32[8,2,168]{2,1,0:T(2,128)S(1)}, u32[]{:S(2)}, u32[]{:S(2)}) collective-permute-start(f32[8,2,168]{2,1,0:T(2,128)} %get-tuple-element.51), channel_id=1, source_target_pairs={{0,63},{1,0},{2,1},{3,2},{4,3},{5,4},{6,5},{7,6},{8,7},{9,8},{10,9... | collective-permute-start | bytes 32264 | tf_op jit(solution)/shard_map/ppermute | solution.py:459
  115.8 70.2 %all-to-all-start.3 = ((f32[64,1,640]{2,1,0:T(1,128)}), f32[64,1,640]{2,1,0:T(1,128)S(1)}, u32[]{:S(2)}, u32[]{:S(2)}) async-start(f32[64,1,640]{2,1,0:T(1,128)} %get-tuple-element.53), calls=%async_computation.3 | async-start | bytes 327680 | tf_op jit(solution)/shard_map/all_to_all | solution.py:488
  143.2 8.6 %collective-permute-start.8 = (f32[2,8,168]{2,1,0:T(8,128)}, f32[2,8,168]{2,1,0:T(8,128)S(1)}, u32[]{:S(2)}, u32[]{:S(2)}) collective-permute-start(f32[2,8,168]{2,1,0:T(8,128)} %get-tuple-element.57), channel_id=1, source_target_pairs={{0,64},{64,128},{128,192},{192,256},{256,320},{320,384},{384,448},... | collective-permute-start | bytes 32264 | tf_op jit(solution)/shard_map/ppermute | solution.py:459
  145.4 7.5 %collective-permute-start.9 = (f32[2,8,168]{2,1,0:T(8,128)}, f32[2,8,168]{2,1,0:T(8,128)S(1)}, u32[]{:S(2)}, u32[]{:S(2)}) collective-permute-start(f32[2,8,168]{2,1,0:T(8,128)} %get-tuple-element.58), channel_id=1, source_target_pairs={{0,960},{64,0},{128,64},{192,128},{256,192},{320,256},{384,320},{4... | collective-permute-start | bytes 32264 | tf_op jit(solution)/shard_map/ppermute | solution.py:459
  155.0 3.9 %collective-permute-start.10 = (f32[10,2,168]{2,1,0:T(2,128)}, f32[10,2,168]{2,1,0:T(2,128)S(1)}, u32[]{:S(2)}, u32[]{:S(2)}) collective-permute-start(f32[10,2,168]{2,1,0:T(2,128)} %get-tuple-element.60), channel_id=1, source_target_pairs={{0,1},{1,2},{2,3},{3,4},{4,5},{5,6},{6,7},{7,8},{8,9},{9,10},{10,1... | collective-permute-start | bytes 40328 | tf_op jit(solution)/shard_map/ppermute | solution.py:459
  157.7 3.7 %collective-permute-start.11 = (f32[10,2,168]{2,1,0:T(2,128)}, f32[10,2,168]{2,1,0:T(2,128)S(1)}, u32[]{:S(2)}, u32[]{:S(2)}) collective-permute-start(f32[10,2,168]{2,1,0:T(2,128)} %get-tuple-element.61), channel_id=1, source_target_pairs={{0,63},{1,0},{2,1},{3,2},{4,3},{5,4},{6,5},{7,6},{8,7},{9,8},{10,9... | collective-permute-start | bytes 40328 | tf_op jit(solution)/shard_map/ppermute | solution.py:459
  158.9 2.6 %copy-start.3 = (f32[10,2,168]{2,1,0:T(2,128)}, f32[10,2,168]{2,1,0:T(2,128)S(1)}, u32[]{:S(2)}) copy-start(f32[10,2,168]{2,1,0:T(2,128)S(1)} %collective-permute-done.10.yl_ref) | copy-start | bytes 40324
  165.6 9.3 %collective-permute-start.12 = (f32[2,16,168]{2,1,0:T(8,128)}, f32[2,16,168]{2,1,0:T(8,128)S(1)}, u32[]{:S(2)}, u32[]{:S(2)}) collective-permute-start(f32[2,16,168]{2,1,0:T(8,128)} %get-tuple-element.65), channel_id=1, source_target_pairs={{0,64},{64,128},{128,192},{192,256},{256,320},{320,384},{384,448},... | collective-permute-start | bytes 64520 | tf_op jit(solution)/shard_map/ppermute | solution.py:459
  167.5 8.6 %collective-permute-start.13 = (f32[2,16,168]{2,1,0:T(8,128)}, f32[2,16,168]{2,1,0:T(8,128)S(1)}, u32[]{:S(2)}, u32[]{:S(2)}) collective-permute-start(f32[2,16,168]{2,1,0:T(8,128)} %get-tuple-element.66), channel_id=1, source_target_pairs={{0,960},{64,0},{128,64},{192,128},{256,192},{320,256},{384,320},{4... | collective-permute-start | bytes 64520 | tf_op jit(solution)/shard_map/ppermute | solution.py:459
  178.3 1.7 collective-permute-start.14
  178.9 3.7 %collective-permute-start.15 = (f32[8,2,168]{2,1,0:T(2,128)}, f32[8,2,168]{2,1,0:T(2,128)S(1)}, u32[]{:S(2)}, u32[]{:S(2)}) collective-permute-start(f32[8,2,168]{2,1,0:T(2,128)} %get-tuple-element.69), channel_id=1, source_target_pairs={{0,63},{1,0},{2,1},{3,2},{4,3},{5,4},{6,5},{7,6},{8,7},{9,8},{10,9... | collective-permute-start | bytes 32264 | tf_op jit(solution)/shard_map/ppermute | solution.py:459
  180.0 2.6 %copy-start.8 = (f32[8,2,168]{2,1,0:T(2,128)}, f32[8,2,168]{2,1,0:T(2,128)S(1)}, u32[]{:S(2)}) copy-start(f32[8,2,168]{2,1,0:T(2,128)S(1)} %collective-permute-done.14.yl_ref) | copy-start | bytes 32260
  203.9 46.9 %all-to-all-start.5 = ((f32[64,1,128]{2,1,0:T(1,128)}), f32[64,1,128]{2,1,0:T(1,128)S(1)}, u32[]{:S(2)}, u32[]{:S(2)}) async-start(f32[64,1,128]{2,1,0:T(1,128)} %get-tuple-element.74), calls=%async_computation.5 | async-start | bytes 65536 | tf_op jit(solution)/shard_map/all_to_all | solution.py:488
  231.4 8.2 %collective-permute-start.16 = (f32[1,8,168]{2,1,0:T(8,128)}, f32[1,8,168]{2,1,0:T(8,128)S(1)}, u32[]{:S(2)}, u32[]{:S(2)}) collective-permute-start(f32[1,8,168]{2,1,0:T(8,128)} %get-tuple-element.81), channel_id=1, source_target_pairs={{0,64},{64,128},{128,192},{192,256},{256,320},{320,384},{384,448},... | collective-permute-start | bytes 16136 | tf_op jit(solution)/shard_map/ppermute | solution.py:459
  241.6 3.5 %collective-permute-start.17 = (f32[7,1,168]{2,1,0:T(1,128)}, f32[7,1,168]{2,1,0:T(1,128)S(1)}, u32[]{:S(2)}, u32[]{:S(2)}) collective-permute-start(f32[7,1,168]{2,1,0:T(1,128)} %get-tuple-element.83), channel_id=1, source_target_pairs={{0,1},{1,2},{2,3},{3,4},{4,5},{5,6},{6,7},{7,8},{8,9},{9,10},{10,1... | collective-permute-start | bytes 14120 | tf_op jit(solution)/shard_map/ppermute | solution.py:459
  245.1 5.7 %copy-start.11 = (f32[7,1,168]{2,1,0:T(1,128)}, f32[7,1,168]{2,1,0:T(1,128)S(1)}, u32[]{:S(2)}) copy-start(f32[7,1,168]{2,1,0:T(1,128)S(1)} %collective-permute-done.17.vl_ref) | copy-start | bytes 14116
  (18 other events, 13.1 us)

commit v2 on v1

--- a/solution.py
+++ b/solution.py
@@ -160,15 +160,16 @@
     )
 
 
-def run(kernel, outs, *args, scratch=()):
-    shapes = [jax.ShapeDtypeStruct(shape, jnp.float32) for shape in outs]
+def run(kernel, outs, *args, scratch=(), free=()):
+    spaces = [pltpu.SMEM if a.dtype == jnp.int32 else pltpu.VMEM for a in args]
     size = sum(math.prod(s) for s in outs) + sum(math.prod(a.shape) for a in args)
     return pl.pallas_call(
         kernel,
-        out_shape=shapes,
-        in_specs=[pl.BlockSpec(memory_space=pltpu.VMEM)] * len(args),
+        out_shape=[(jax.ShapeDtypeStruct if i in free else pltpu.VMEM)(shape, jnp.float32) for i, shape in enumerate(outs)],
+        in_specs=[pl.BlockSpec(memory_space=space) for space in spaces],
         out_specs=[pl.BlockSpec(memory_space=pltpu.VMEM)] * len(outs),
         scratch_shapes=[pltpu.VMEM(shape, jnp.float32) for shape in scratch],
+        compiler_params=pltpu.CompilerParams(vmem_limit_bytes=16 << 20),
         cost_estimate=pl.CostEstimate(flops=2 * 6 * 160 * 240 * 168, bytes_accessed=4 * size, transcendentals=0),
     )(*args)
 
@@ -202,6 +203,11 @@
     return jnp.sum(jnp.where(lane == spot, row, 0.0), axis=1, keepdims=True)
 
 
+def lane_sel(spot):
+    lane = lax.broadcasted_iota(jnp.int32, (1, LANES), 1)
+    return jnp.where(lane // 8 == spot, 1.0, 0.0).astype(jnp.float32)
+
+
 def rows_tile(rows):
     spot = lax.broadcasted_iota(jnp.int32, (8, LANES), 0)
     tile = jnp.zeros((8, LANES), jnp.float32)
@@ -210,41 +216,63 @@
     return tile
 
 
-def first_kernel(k_parts, m_parts, width, b_ref, k_ref, m_ref, x_ref, sel_ref, r1_ref, r2_ref, r1t_ref, r2t_ref, zct_ref, out_ref):
+def first_kernel(k_parts, m_parts, width, idx_ref, b_ref, k_ref, m_ref, x_ref, r1_ref, r2_ref, r1t_ref, r2t_ref, zct_ref, out_ref, scr):
     k, m = k_ref[...], m_ref[...]
     e11, e12, e22 = (k * k_parts[name] + m * m_parts[name] for name in ("11", "12", "22"))
     r1, r2 = r1_ref[...], r2_ref[...]
-    sel = sel_ref[...]
+    sel = lane_sel(idx_ref[0])
     small = (dot(r1 * e11 + r2 * e12, r1t_ref[...]) + dot(r1 * e12 + r2 * e22, r2t_ref[...])) * sel
     acc = b_ref[1]
     for x in range(2, 7):
         acc = acc + b_ref[x]
     line = jnp.sum(acc[1:7], axis=0, keepdims=True)
     rc = dot(line, zct_ref[...]) * sel
-    rc_tile = rows_tile([rc])
+    nz, ez = b_ref.shape[2], k.shape[1]
+    scr[...] = jnp.zeros_like(scr)
+    scr[:, :LANES] = small
+    scr[0:1, LANES : 2 * LANES] = rc
+    scr[1:2, LANES : LANES + ez] = k
+    scr[2:3, LANES : LANES + ez] = m
+    for x in range(7):
+        scr[:7, 2 * LANES + nz * x : 2 * LANES + nz * (x + 1)] = b_ref[x]
     for peer in range(out_ref.shape[0]):
         out_ref[peer, :, :width] = x_ref[:, peer * width : (peer + 1) * width]
-        out_ref[peer, :, width : width + LANES] = small
-        out_ref[peer, :, width + LANES :] = rc_tile
+        out_ref[peer, :, width:] = scr[...]
 
 
 def split_group(xl_ref, width):
     rows = xl_ref.shape[0] * xl_ref.shape[1]
-    wide = xl_ref[...].reshape(rows, xl_ref.shape[2])
-    rc = jnp.sum(wide[:, width + LANES :], axis=0, keepdims=True)
-    return wide[:, :width], wide[:, width : width + LANES], rc
+    small = xl_ref[:, :, width : width + LANES].reshape(rows, LANES)
+    rc = jnp.sum(xl_ref[:, 0:1, width + LANES : width + 2 * LANES], axis=0)
+    return xl_ref[:, :, :width].reshape(rows, width), small, rc
 
 
 def spread(out_ref, row):
     out_ref[...] = jnp.broadcast_to(row[None], out_ref.shape)
 
 
-def coarse_in_kernel(width, xl_ref, eye_ref, out_ref):
+def coarse_in_kernel(width, idx_ref, xl_ref, eye_ref, out_ref, bx_ref, hi_ref, lo_ref, k_ref, m_ref):
     factor, _, rc = split_group(xl_ref, width)
     rows = factor.shape[0]
     rc_col = as_col(rc, eye_ref[:rows])
     part = jnp.sum(rc_col * factor, axis=0, keepdims=True)
     spread(out_ref, jnp.concatenate([part, jnp.zeros((1, LANES), jnp.float32)], axis=1))
+    count = xl_ref.shape[0]
+    nz, ez = bx_ref.shape[2], k_ref.shape[1]
+    base = width + 2 * LANES
+    place = 0
+    for apart in range(-4, 5):
+        slot = lax.rem(idx_ref[0] + (apart + 2 * count), count)
+        for x in (6,) if apart == -4 else (0, 1) if apart == 4 else range(7):
+            bx_ref[place] = xl_ref[slot, :, base + nz * x : base + nz * (x + 1)]
+            place += 1
+        if -4 < apart < 4:
+            k_ref[apart + 3 : apart + 4] = xl_ref[slot, 1:2, width + LANES : width + LANES + ez]
+            m_ref[apart + 3 : apart + 4] = xl_ref[slot, 2:3, width + LANES : width + LANES + ez]
+    k_ref[7:8] = k_ref[6:7]
+    m_ref[7:8] = m_ref[6:7]
+    hi_ref[...] = bx_ref[:, 6:7]
+    lo_ref[...] = bx_ref[:, 0:2]
 
 
 def coarse_out_kernel(width, sums_ref, xl_ref, eye_ref, h_ref, out_ref):
@@ -273,8 +301,8 @@
     x_ref[...] = x0
 
 
-def pair_kernel(width, sums_ref, xl_ref, eye_ref, b_ref, q_ref, u_ref, au_ref, s_ref, as_ref, inner_ref, owned_ref, zct_ref, sel_ref,
-                out_ref, scal_ref, r_ref, qo_ref):
+def pair_kernel(width, idx_ref, sums_ref, xl_ref, eye_ref, b_ref, q_ref, u_ref, au_ref, s_ref, as_ref, inner_ref, zct_ref,
+                out_ref, scal_ref, r_ref):
     factor, _, _ = split_group(xl_ref, width)
     rows = factor.shape[0]
     sums = jnp.sum(sums_ref[...], axis=0)
@@ -283,22 +311,18 @@
     scal = sums[:, width:]
     rho, den = lane_get(scal, 0), lane_get(scal, 1)
     step = rho / den
+    sel = lane_sel(idx_ref[0])
+    r_ref[...] = jnp.zeros_like(r_ref)
     for x in range(7):
-        qo = q_ref[x + 1, 1:8]
-        qo_ref[x, :7] = qo
-        r_ref[x, :7] = b_ref[x] - step * qo
-        qo_ref[x, 7:] = jnp.zeros_like(qo_ref[x, 7:])
-        r_ref[x, 7:] = jnp.zeros_like(r_ref[x, 7:])
-    qo_ref[7] = jnp.zeros_like(qo_ref[7])
-    r_ref[7] = jnp.zeros_like(r_ref[7])
+        r_ref[x, :7] = b_ref[x] - step * q_ref[x, :7]
     nz = b_ref.shape[2]
     flat = lambda ref: ref[...].reshape(64, nz)
     resid = flat(r_ref)
     t = flat(u_ref) - step * flat(s_ref)
     at = flat(au_ref) - step * flat(as_ref)
     inner = inner_ref[...]
-    wr = dot(jnp.sum(inner * resid, axis=0, keepdims=True), zct_ref[...]) * sel_ref[...]
-    wt = dot(jnp.sum(inner * at, axis=0, keepdims=True), zct_ref[...]) * sel_ref[...]
+    wr = dot(jnp.sum(inner * resid, axis=0, keepdims=True), zct_ref[...]) * sel
+    wt = dot(jnp.sum(inner * at, axis=0, keepdims=True), zct_ref[...]) * sel
     tile = rows_tile([x_part, wr, wt, lane_put([total(resid * t), total(t * at)])])
     out_ref[...] = jnp.broadcast_to(tile[None], out_ref.shape)
     scal_ref[...] = lane_put([rho, den])
@@ -335,12 +359,6 @@
         res_ref[x, 0:1] = res_ref[x, 0:1] + top
 
 
-def solve(block, k, m, rep10, lam_ab, lam_c, qq, qqt, zf, zft):
-    den = dot(k, rep10) * (lam_ab + lam_c) + dot(m, rep10)
-    spectral = dot(dot(qqt, block), zf) / den
-    return dot(dot(qq, spectral), zft)
-
-
 SOLVE = ("rep10", "lam_ab", "lam_c", "qq", "qqt", "zf", "zft")
 APPLY = ("rep8", "wz", "g8", "g8t", "zk", "kk", "ww")
 
@@ -352,58 +370,48 @@
     return dot(out, g8t)
 
 
+def solve_columns(block, k_ref, m_ref, first, count, consts, lines, acc):
+    rep10, lam_ab, lam_c, qq, qqt, zf, zft = consts
+    lines[...] = dot(block, zf[...])
+    acc[...] = jnp.zeros_like(acc)
+    lam = lam_ab[...] + lam_c[...]
+    for c in range(count):
+        k, m = k_ref[first + c : first + c + 1], m_ref[first + c : first + c + 1]
+        den = dot(k, rep10[...]) * lam + dot(m, rep10[...])
+        spectral = dot(qqt[...], lines[112 * c : 112 * c + 160]) / den
+        low = max(128 - 112 * c, 0)
+        high = min(112 * (count - 1) + 32 - 112 * c, 160)
+        start = 112 * c + low - 128
+        acc[start : start + high - low] = acc[start : start + high - low] + dot(qq[low:high], spectral)
+    return dot(acc[...], zft[...])
+
+
 def schwarz_b_kernel(bx_ref, yl_ref, yh_ref, k_ref, m_ref, *refs):
-    consts, (out_ref, hi_ref, lo_ref, scr) = refs[:-4], refs[-4:]
+    consts, (out_ref, hi_ref, lo_ref, scr, lines, acc) = refs[:-6], refs[-6:]
+    nz = bx_ref.shape[2]
     scr[...] = jnp.zeros_like(scr)
-    scr[:, 1:8] = bx_ref[...]
+    scr[:, 1:8] = bx_ref[:, 0:7]
     scr[:, 0:1] = yl_ref[...]
     scr[:, 8:10] = yh_ref[...]
-    schwarz_tail(scr, k_ref, m_ref, consts, out_ref, hi_ref, lo_ref)
-
-
-def schwarz_q_kernel(qx_ref, yl_ref, yh_ref, k_ref, m_ref, *refs):
-    consts, (q_ref, out_ref, hi_ref, lo_ref) = refs[:-4], refs[-4:]
-    q_ref[...] = jnp.zeros_like(q_ref)
-    q_ref[:, 1:9] = qx_ref[...]
-    q_ref[:, 0:1] = yl_ref[:, 0:1]
-    q_ref[:, 1:2] = q_ref[:, 1:2] + yl_ref[:, 1:2]
-    q_ref[:, 8:9] = q_ref[:, 8:9] + yh_ref[:, 0:1]
-    q_ref[:, 9:10] = yh_ref[:, 1:2]
-    schwarz_tail(q_ref, k_ref, m_ref, consts, out_ref, hi_ref, lo_ref)
-
-
-def schwarz_tail(src, k_ref, m_ref, consts, out_ref, hi_ref, lo_ref):
-    nz = src.shape[2]
-    block = solve(src[...].reshape(160, nz), k_ref[...], m_ref[...], *(ref[...] for ref in consts))
-    block = block.reshape(10, 16, nz)
-    out_ref[...] = block
-    hi_ref[...] = block[8:10]
-    lo_ref[...] = block[0:2]
-
-
-def fold_s_kernel(y_ref, xl_ref, xh_ref, out_ref, hi_ref, lo_ref):
-    out_ref[0:2] = y_ref[1:3] + xl_ref[...]
-    out_ref[2:6] = y_ref[3:7]
-    out_ref[6:8] = y_ref[7:9] + xh_ref[...]
+    out = solve_columns(scr[...].reshape(52 * 16, nz), k_ref, m_ref, 0, 7, consts, lines, acc)
+    out_ref[...] = out.reshape(36, 16, nz)
     hi_ref[...] = out_ref[:, 8:10]
     lo_ref[...] = out_ref[:, 0:2]
 
 
-def fold_a_kernel(q_ref, xl_ref, xh_ref, out_ref, hi_ref, lo_ref):
-    out_ref[0] = xl_ref[0]
-    out_ref[1] = q_ref[0] + xl_ref[1]
-    out_ref[2:8] = q_ref[1:7]
-    out_ref[8] = q_ref[7] + xh_ref[0]
-    out_ref[9] = xh_ref[1]
-    hi_ref[...] = out_ref[:, 6:8]
-    lo_ref[...] = out_ref[:, 0:2]
-
-
-def fold_b_kernel(b_ref, xl_ref, xh_ref, out_ref, hi_ref, lo_ref):
-    out_ref[0:1] = xl_ref[...]
-    out_ref[1:8] = b_ref[...]
-    out_ref[8:10] = xh_ref[...]
-    hi_ref[...] = out_ref[:, 6:7]
+def schwarz_q_kernel(qx_ref, yl_ref, yh_ref, k_ref, m_ref, *refs):
+    consts, (q_ref, out_ref, hi_ref, lo_ref, scr, lines, acc) = refs[:-7], refs[-7:]
+    nz = qx_ref.shape[2]
+    scr[...] = jnp.zeros_like(scr)
+    scr[:, 1:9] = qx_ref[...]
+    scr[:, 0:1] = yl_ref[:, 0:1]
+    scr[:, 1:2] = scr[:, 1:2] + yl_ref[:, 1:2]
+    scr[:, 8:9] = scr[:, 8:9] + yh_ref[:, 0:1]
+    scr[:, 9:10] = yh_ref[:, 1:2]
+    q_ref[...] = scr[8:16, 1:9]
+    out = solve_columns(scr[...].reshape(24 * 16, nz), k_ref, m_ref, 2, 3, consts, lines, acc)
+    out_ref[...] = out.reshape(8, 16, nz)
+    hi_ref[...] = out_ref[:, 8:10]
     lo_ref[...] = out_ref[:, 0:2]
 
 
@@ -419,17 +427,18 @@
     u_ref[:, 6:8] = u_ref[:, 6:8] + yh_ref[...]
 
 
-def apply_u_kernel(b_ref, y_ref, yl_ref, yh_ref, k_ref, m_ref, inner_ref, zct_ref, sel_ref, *refs):
-    consts, (u_ref, au_ref, h_ref) = refs[:-3], refs[-3:]
+def apply_u_kernel(idx_ref, b_ref, y_ref, yl_ref, yh_ref, k_ref, m_ref, inner_ref, zct_ref, *refs):
+    consts, (u_ref, own_ref, au_ref, h_ref) = refs[:-4], refs[-4:]
     nz = u_ref.shape[2]
     gather_s(u_ref, y_ref, yl_ref, yh_ref)
-    u = u_ref[...].reshape(64, nz)
+    own_ref[...] = u_ref[14:22]
+    u = own_ref[...].reshape(64, nz)
     au = apply(u, k_ref[...], m_ref[...], *(ref[...] for ref in consts))
     au_ref[...] = au.reshape(8, 8, nz)
-    h = dot(jnp.sum(inner_ref[...] * au, axis=0, keepdims=True), zct_ref[...]) * sel_ref[...]
-    acc = b_ref[0] * u_ref[0, :7]
+    h = dot(jnp.sum(inner_ref[...] * au, axis=0, keepdims=True), zct_ref[...]) * lane_sel(idx_ref[0])
+    acc = b_ref[0] * own_ref[0, :7]
     for x in range(1, 7):
-        acc = acc + b_ref[x] * u_ref[x, :7]
+        acc = acc + b_ref[x] * own_ref[x, :7]
     h_ref[...] = rows_tile([jnp.zeros((1, LANES), jnp.float32), h, lane_put([total(acc), total(u * au)])])
 
 
@@ -441,17 +450,45 @@
     as_ref[...] = out.reshape(8, 8, nz)
 
 
-def apply_p_kernel(u_ref, x_ref, k_ref, m_ref, inner_ref, zl_ref, sel_ref, eye_ref, *refs):
-    consts, (p_ref, q_ref, hi_ref, lo_ref) = refs[:-4], refs[-4:]
+def apply_p_kernel(idx_ref, u_ref, x_ref, k_ref, m_ref, inner_ref, zl_ref, *refs):
+    (rep8, wz, g8, g8t, zk, kk, ww), (p_ref, q_ref, hi_ref, lo_ref, field, su, sk, acc) = refs[:-8], refs[-8:]
     nz = u_ref.shape[2]
-    col = as_col(x_ref[...] * sel_ref[...], eye_ref[...])
-    line = jnp.sum(col * zl_ref[...], axis=0, keepdims=True)
-    p = u_ref[...].reshape(64, nz) + inner_ref[...] * line
-    p_ref[...] = p.reshape(8, 8, nz)
-    out = apply(p, k_ref[...], m_ref[...], *(ref[...] for ref in consts)).reshape(8, 8, nz)
-    q_ref[...] = out
-    hi_ref[...] = out[8 - hi_ref.shape[0] :]
-    lo_ref[...] = out[0:2]
+    count = idx_ref[1]
+    x0 = x_ref[...]
+    picks = [x0 * lane_sel(lax.rem(idx_ref[0] + (apart + 2 * count), count)) for apart in range(-2, 3)]
+    lines = dot(rows_tile(picks), zl_ref[...])
+    field[...] = u_ref[...]
+    side = inner_ref[8:16]
+    for c in range(5):
+        add = side * lines[c : c + 1]
+        for x in range(7 * c + 1, 7 * c + 7):
+            field[x] = field[x] + add
+    p_ref[...] = field[14:22]
+    whole = field[...].reshape(36 * 8, nz)
+    su[...] = dot(whole, g8[...])
+    sk[...] = dot(whole, zk[...])
+    acc[...] = jnp.zeros_like(acc)
+    for c in range(5):
+        k_line = dot(k_ref[c + 1 : c + 2], rep8[...])
+        m_line = dot(m_ref[c + 1 : c + 2], rep8[...]) * wz[...]
+        part = slice(56 * c, 56 * c + 64)
+        u = su[part]
+        out = (k_line * wz[...]) * dot(kk[...], u) + ww[...] * (k_line * sk[part] + m_line * u)
+        acc[part] = acc[part] + out
+    q_ref[...] = dot(acc[48:240], g8t[...]).reshape(24, 8, nz)
+    hi_ref[...] = q_ref[:, 6:8]
+    lo_ref[...] = q_ref[:, 0:2]
+
+
+def apply_w_kernel(idx_ref, s_ref, x_ref, k_ref, m_ref, inner_ref, zl_ref, *refs):
+    consts, (w_ref, v_ref, hi_ref) = refs[:-3], refs[-3:]
+    nz = s_ref.shape[2]
+    line = dot(x_ref[...] * lane_sel(idx_ref[0]), zl_ref[...])
+    w = s_ref[...].reshape(64, nz) + inner_ref[...] * line
+    w_ref[...] = w.reshape(8, 8, nz)
+    out = apply(w, k_ref[...], m_ref[...], *(ref[...] for ref in consts)).reshape(8, 8, nz)
+    v_ref[...] = out
+    hi_ref[...] = out[7:8]
 
 
 def shift(value, axis, step):
@@ -469,10 +506,10 @@
     k = stiff_coef.reshape(1, ez)
     m = mass_coef.reshape(1, ez)
     b = right_side
-    sel = (jnp.arange(LANES)[None] // c_dev == lax.axis_index("gx")).astype(jnp.float32)
+    idx = jnp.stack([lax.axis_index("gx"), jnp.int32(n_gx)])
     solve_tab = [tab[name] for name in SOLVE]
     apply_tab = [tab[name] for name in APPLY]
-    inner, owned, zct, zl, eye = (tab[name] for name in ("inner", "owned", "zct", "zl", "eye"))
+    inner, zct, zl, eye = (tab[name] for name in ("inner", "zct", "zl", "eye"))
 
     def kernel(fn, *fixed):
         def call(*refs):
@@ -488,52 +525,47 @@
         return lax.all_to_all(value, "gy", 0, 0)
 
     group = (n_gx, c_dev, LANES)
-    (pay,) = run(kernel(first_kernel, tab["k_parts"], tab["m_parts"], width), [(n_gx, c_dev, width + 2 * LANES)],
-                 b, k, m, coarse_factor, sel, tab["r1"], tab["r2"], tab["r1t"], tab["r2t"], zct)
-    b_low, b_high = shift(b[6:7], "gx", 1), shift(b[0:2], "gx", -1)
+    aux = -(-(2 * LANES + 7 * nz) // LANES) * LANES
+    (pay,) = run(kernel(first_kernel, tab["k_parts"], tab["m_parts"], width), [(n_gx, c_dev, width + aux)],
+                 idx, b, k, m, coarse_factor, tab["r1"], tab["r2"], tab["r1t"], tab["r2t"], zct, scratch=[(8, aux)])
     xl = swap_gx(pay)
 
-    (pay,) = run(kernel(coarse_in_kernel, width), [(n_gy, 1, width + LANES)], xl, eye)
+    outs = [(n_gy, 1, width + LANES), (52, 8, nz), (52, 1, nz), (52, 2, nz), (8, ez), (8, ez)]
+    pay, bx, hi, lo, ks, ms = run(kernel(coarse_in_kernel, width), outs, idx, xl, eye, free=(0,))
+    y_low, y_high = shift(hi, "gy", 1), shift(lo, "gy", -1)
     sums = swap_gy(pay)
 
-    bx, hi, lo = run(fold_b_kernel, [(10, 7, nz), (10, 1, nz), (10, 2, nz)], b, b_low, b_high)
-    y_low, y_high = shift(hi, "gy", 1), shift(lo, "gy", -1)
-
-    strips = [(2, 16, nz), (2, 16, nz)]
     sides = [(8, 2, nz), (8, 2, nz)]
-    y, hi, lo = run(schwarz_b_kernel, [(10, 16, nz)] + strips, bx, y_low, y_high, k, m, *solve_tab, scratch=[(10, 16, nz)])
-    x_low, x_high = shift(hi, "gx", 1), shift(lo, "gx", -1)
-    y, hi, lo = run(fold_s_kernel, [(8, 16, nz)] + sides, y, x_low, x_high)
+    y, hi, lo = run(schwarz_b_kernel, [(36, 16, nz), (36, 2, nz), (36, 2, nz)], bx, y_low, y_high, ks, ms, *solve_tab,
+                    scratch=[(52, 16, nz), (832, 10 * ez), (576, 10 * ez)])
     y_low, y_high = shift(hi, "gy", 1), shift(lo, "gy", -1)
     cube = (8, 8, nz)
-    u, au, h = run(apply_u_kernel, [cube, cube, (8, LANES)], b, y, y_low, y_high, k, m, inner, zct, sel, *apply_tab)
+    wide_u, u, au, h = run(apply_u_kernel, [(36, 8, nz), cube, cube, (8, LANES)], idx, b, y, y_low, y_high, k, m, inner, zct, *apply_tab,
+                          free=(1, 2))
 
     (pay,) = run(kernel(coarse_out_kernel, width), [group], sums, xl, eye, h)
     got = swap_gx(pay)
-    pay, x0 = run(kernel(coarse_mid_kernel, width), [(n_gy, 1, width + LANES), (1, LANES)], got, xl, eye)
+    pay, x0 = run(kernel(coarse_mid_kernel, width), [(n_gy, 1, width + LANES), (1, LANES)], got, xl, eye, free=(0,))
     sums = swap_gy(pay)
 
-    p, q, hi, lo = run(apply_p_kernel, [cube, cube, (2, 8, nz), (2, 8, nz)], u, x0, k, m, inner, zl, sel, eye, *apply_tab)
-    x_low, x_high = shift(hi, "gx", 1), shift(lo, "gx", -1)
-    qx, hi, lo = run(fold_a_kernel, [(10, 8, nz), (10, 2, nz), (10, 2, nz)], q, x_low, x_high)
+    p, qx, hi, lo = run(apply_p_kernel, [cube, (24, 8, nz), (24, 2, nz), (24, 2, nz)], idx, wide_u, x0, ks, ms, inner, zl, *apply_tab,
+                        scratch=[(36, 8, nz)] + [(288, 8 * ez)] * 3)
     y_low, y_high = shift(hi, "gy", 1), shift(lo, "gy", -1)
-    q, y, hi, lo = run(schwarz_q_kernel, [(10, 16, nz), (10, 16, nz)] + strips, qx, y_low, y_high, k, m, *solve_tab)
-    x_low, x_high = shift(hi, "gx", 1), shift(lo, "gx", -1)
-    y, hi, lo = run(fold_s_kernel, [(8, 16, nz)] + sides, y, x_low, x_high)
+    q, y, hi, lo = run(schwarz_q_kernel, [cube, (8, 16, nz)] + sides, qx, y_low, y_high, ks, ms, *solve_tab,
+                       scratch=[(24, 16, nz), (384, 10 * ez), (128, 10 * ez)])
     y_low, y_high = shift(hi, "gy", 1), shift(lo, "gy", -1)
     s, a_s = run(apply_s_kernel, [cube, cube], y, y_low, y_high, k, m, *apply_tab)
 
-    pay, scal, resid, q_own = run(kernel(pair_kernel, width), [group, (1, LANES), cube, cube],
-                                  sums, xl, eye, b, q, u, au, s, a_s, inner, owned, zct, sel)
+    pay, scal, resid = run(kernel(pair_kernel, width), [group, (1, LANES), cube], idx, sums, xl, eye, b, q, u, au, s, a_s, inner, zct)
     got = swap_gx(pay)
-    pay, x1 = run(kernel(last_in_kernel, width), [(n_gy, 1, LANES), (1, LANES)], got, xl, x0, scal, eye)
+    pay, x1 = run(kernel(last_in_kernel, width), [(n_gy, 1, LANES), (1, LANES)], got, xl, x0, scal, eye, free=(0,))
     sums = swap_gy(pay)
 
-    w, v, hi, _ = run(apply_p_kernel, [cube, cube, (1, 8, nz), (2, 8, nz)], s, x1, k, m, inner, zl, sel, eye, *apply_tab)
+    w, v, hi = run(apply_w_kernel, [cube, cube, (1, 8, nz)], idx, s, x1, k, m, inner, zl, *apply_tab)
     x_low = shift(hi, "gx", 1)
     v, hi = run(fold_v_kernel, [(7, 8, nz), (7, 1, nz)], v, x_low)
     y_low = shift(hi, "gy", 1)
-    sol, res = run(final_kernel, [(7, 7, nz), (7, 7, nz)], sums, scal, p, w, resid, q_own, v, y_low)
+    sol, res = run(final_kernel, [(7, 7, nz), (7, 7, nz)], sums, scal, p, w, resid, q, v, y_low, free=(0, 1))
     return sol, res
 
 

time: 255 us -> 209 us (0.82)
  starting transfers between devices: 127 us -> 81 us
  waiting for transfers between devices: 33.2 us -> 61.2 us
  Pallas kernels: 40.1 us -> 20.2 us
  blocking collectives: 41.9 us -> 38.6 us
  local copies, waits for them, and re-layouts: 9.43 us -> 6.66 us
    ppermute x18 -> x10, starting transfers between devices: 46.5 us -> 10.5 us  [shift(): lax.ppermute(value, axis, [(i, (i + step) % count) for i in range(count)])]
    all_to_all x3, waiting for transfers between devices: 5.69 us -> 27.9 us  [swap_gy(): return lax.all_to_all(value, 'gy', 0, 0)]
    pallas_call x18 -> x14, Pallas kernels: 40.1 us -> 20.2 us  [run(): pl.pallas_call(kernel, out_shape=[(jax.ShapeDtypeStruct if i in free else...]
    all_to_all x3, starting transfers between devices: 80.7 us -> 70.5 us  [swap_gy(): return lax.all_to_all(value, 'gy', 0, 0)]
    ppermute x18 -> x10, waiting for transfers between devices: 27.5 us -> 33.3 us  [shift(): lax.ppermute(value, axis, [(i, (i + step) % count) for i in range(count)])]
    all_to_all x3, blocking collectives: 41.9 us -> 38.6 us  [swap_gx(): return lax.all_to_all(value, 'gx', 0, 0)]
    unnamed x42 -> x68, local copies, waits for them, and re-layouts: 8 us -> 6.66 us
  transfers between devices with their start and end apart: 21 -> 13, of which waited for: 16 -> 13; matrix products, arithmetic and copies ran while one was open for 1% -> 0% of each run, Pallas kernels for 10% -> 7%
where the time goes in v2:
time: 209 us
  starting transfers between devices  81 us (39%)
  waiting for transfers between devices  61.2 us (29%)
  blocking collectives  38.6 us (18%)
  Pallas kernels  20.2 us (10%)
  local copies, waits for them, and re-layouts  6.66 us (3%)
    all_to_all x3, starting transfers between devices, swap_gy(): return lax.all_to_all(value, 'gy', 0, 0)  70.5 us
    all_to_all x3, blocking collectives, swap_gx(): return lax.all_to_all(value, 'gx', 0, 0)  38.6 us
    ppermute x10, waiting for transfers between devices, shift(): lax.ppermute(value, axis, [(i, (i + step) % count) for i in range(count)])  33.3 us
    all_to_all x3, waiting for transfers between devices, swap_gy(): return lax.all_to_all(value, 'gy', 0, 0)  27.9 us
    pallas_call x14, Pallas kernels, run(): pl.pallas_call(kernel, out_shape=[(jax.ShapeDtypeStruct if i in free else...  20.2 us
    ppermute x10, starting transfers between devices, shift(): lax.ppermute(value, axis, [(i, (i + step) % count) for i in range(count)])  10.5 us
    unnamed x68, local copies, waits for them, and re-layouts  6.66 us
  transfers between devices with their start and end apart: 13, of which 13 were waited for; matrix products, arithmetic and copies ran while one was open for 0% of the time, Pallas kernels for 7%

profile of v2, /device:TPU:1, one launch (start us, length us, event | category | flops | bytes accessed | tf_op | source)
XLA Modules:
  0.0 208.7 jit_solution(1715046073170727989)
XLA Ops:
  5.5 19.3 %all_to_all.30.refs_1_.refs_2_ = f32[16,8,2048]{2,1,0:T(8,128)S(1)} all-to-all(f32[16,8,2048]{2,1,0:T(8,128)S(1)} %shard_map.257), channel_id=1, replica_groups=mesh['gx'=16,'gy'=64] {'gx'}, dimensions={0} | all-to-all | bytes 2097152 | tf_op jit(solution)/shard_map/all_to_all | solution.py:522
  26.2 35.1 %all-to-all-start.1 = ((f32[64,1,640]{2,1,0:T(1,128)}), f32[64,1,640]{2,1,0:T(1,128)S(1)}, u32[]{:S(2)}, u32[]{:S(2)}) async-start(f32[64,1,640]{2,1,0:T(1,128)} %get-tuple-element.37), calls=%async_computation.1 | async-start | bytes 327680 | tf_op jit(solution)/shard_map/all_to_all | solution.py:525
  63.0 2.3 %collective-permute-done.yl_ref = f32[52,1,168]{2,1,0:T(1,128)S(1)} collective-permute-done((f32[52,1,168]{2,1,0:T(1,128)S(1)}, f32[52,1,168]{2,1,0:T(1,128)S(1)}, u32[]{:S(2)}, u32[]{:S(2)}) %collective-permute-start) | collective-permute-done | bytes 34976 | tf_op jit(solution)/shard_map/ppermute | solution.py:496
  65.3 10.9 %collective-permute-done.1.yh_ref = f32[52,2,168]{2,1,0:T(2,128)S(1)} collective-permute-done((f32[52,2,168]{2,1,0:T(2,128)S(1)}, f32[52,2,168]{2,1,0:T(2,128)S(1)}, u32[]{:S(2)}, u32[]{:S(2)}) %collective-permute-start.1) | collective-permute-done | bytes 69920 | tf_op jit(solution)/shard_map/ppermute | solution.py:496
  76.9 5.4 %shard_map.259 = (f32[36,16,168]{2,1,0:T(8,128)S(1)}, f32[36,2,168]{2,1,0:T(2,128)S(1)}, f32[36,2,168]{2,1,0:T(2,128)S(1)}) custom-call(f32[52,8,168]{2,1,0:T(8,128)S(1)} %get-tuple-element.38.bx_ref, f32[52,1,168]{2,1,0:T(1,128)S(1)} %collective-permute-done.yl_ref, f32[52,2,168]{2,1,0:T(2,128)S(1)} %collective-permute-done.1.yh_ref, ...), custom_call_target="tpu_custom_call" | custom-call | flops 77414400 | bytes 1421760 | tf_op jit(solution)/shard_map/pallas_call | solution.py:166
  83.8 2.7 %collective-permute-done.3.yh_ref = f32[36,2,168]{2,1,0:T(2,128)S(1)} collective-permute-done((f32[36,2,168]{2,1,0:T(2,128)S(1)}, f32[36,2,168]{2,1,0:T(2,128)S(1)}, u32[]{:S(2)}, u32[]{:S(2)}) %collective-permute-start.3) | collective-permute-done | bytes 48416 | tf_op jit(solution)/shard_map/ppermute | solution.py:496
  86.6 1.8 shard_map.260
  89.6 4.8 %all-to-all-done.1.refs_0_ = f32[64,1,640]{2,1,0:T(1,128)S(1)} async-done(((f32[64,1,640]{2,1,0:T(1,128)}), f32[64,1,640]{2,1,0:T(1,128)S(1)}, u32[]{:S(2)}, u32[]{:S(2)}) %all-to-all-start.1) | async-done | bytes 163872 | tf_op jit(solution)/shard_map/all_to_all | solution.py:525
  94.7 9.9 %all_to_all.31.refs_0_ = f32[16,8,128]{2,1,0:T(8,128)S(1)} all-to-all(f32[16,8,128]{2,1,0:T(8,128)S(1)} %shard_map.261), channel_id=1, replica_groups=mesh['gx'=16,'gy'=64] {'gx'}, dimensions={0} | all-to-all | bytes 131072 | tf_op jit(solution)/shard_map/all_to_all | solution.py:522
  105.5 21.0 %all-to-all-start.3 = ((f32[64,1,640]{2,1,0:T(1,128)}), f32[64,1,640]{2,1,0:T(1,128)S(1)}, u32[]{:S(2)}, u32[]{:S(2)}) async-start(f32[64,1,640]{2,1,0:T(1,128)} %copy-done.19), calls=%async_computation.3 | async-start | bytes 327680 | tf_op jit(solution)/shard_map/all_to_all | solution.py:525
  126.5 2.5 %shard_map.263 = (f32[8,8,168]{2,1,0:T(8,128)S(1)}, f32[24,8,168]{2,1,0:T(8,128)S(1)}, f32[24,2,168]{2,1,0:T(2,128)S(1)}, f32[24,2,168]{2,1,0:T(2,128)S(1)}) custom-call(s32[2]{0:T(128)S(1)} %pad_add_fusion.refs_0_.idx_ref, f32[36,8,168]{2,1,0:T(8,128)S(1)} %get-tuple-element.48.u_ref, f32[1,128]{1,0:T(1,128)S(1)} %get-tuple-element.49.x_ref.refs_2_, ...), custom_call_target="tpu_custom_call" | custom-call | flops 77414400 | bytes 941320 | tf_op jit(solution)/shard_map/pallas_call | solution.py:166
  129.0 1.6 collective-permute-start.4
  130.6 4.7 %collective-permute-done.4.yl_ref = f32[24,2,168]{2,1,0:T(2,128)S(1)} collective-permute-done((f32[24,2,168]{2,1,0:T(2,128)S(1)}, f32[24,2,168]{2,1,0:T(2,128)S(1)}, u32[]{:S(2)}, u32[]{:S(2)}) %collective-permute-start.4) | collective-permute-done | bytes 32288 | tf_op jit(solution)/shard_map/ppermute | solution.py:496
  135.3 3.6 %collective-permute-done.5.yh_ref = f32[24,2,168]{2,1,0:T(2,128)S(1)} collective-permute-done((f32[24,2,168]{2,1,0:T(2,128)S(1)}, f32[24,2,168]{2,1,0:T(2,128)S(1)}, u32[]{:S(2)}, u32[]{:S(2)}) %collective-permute-start.5) | collective-permute-done | bytes 32288 | tf_op jit(solution)/shard_map/ppermute | solution.py:496
  139.0 2.6 %shard_map.264 = (f32[8,8,168]{2,1,0:T(8,128)S(1)}, f32[8,16,168]{2,1,0:T(8,128)S(1)}, f32[8,2,168]{2,1,0:T(2,128)S(1)}, f32[8,2,168]{2,1,0:T(2,128)S(1)}) custom-call(f32[24,8,168]{2,1,0:T(8,128)S(1)} %get-tuple-element.50.qx_ref, f32[24,2,168]{2,1,0:T(2,128)S(1)} %collective-permute-done.4.yl_ref, f32[24,2,168]{2,1,0:T(2,128)S(1)} %collective-permute-done.5.yh_ref, ...), custom_call_target="tpu_custom_call" | custom-call | flops 77414400 | bytes 897600 | tf_op jit(solution)/shard_map/pallas_call | solution.py:166
  141.6 1.9 collective-permute-start.7
  146.1 13.6 %all-to-all-done.3.refs_1_ = f32[64,1,640]{2,1,0:T(1,128)S(1)} async-done(((f32[64,1,640]{2,1,0:T(1,128)}), f32[64,1,640]{2,1,0:T(1,128)S(1)}, u32[]{:S(2)}, u32[]{:S(2)}) %all-to-all-start.3) | async-done | bytes 163872 | tf_op jit(solution)/shard_map/all_to_all | solution.py:525
  160.7 9.5 %all_to_all.32.refs_0_ = f32[16,8,128]{2,1,0:T(8,128)S(1)} all-to-all(f32[16,8,128]{2,1,0:T(8,128)S(1)} %get-tuple-element.61), channel_id=1, replica_groups=mesh['gx'=16,'gy'=64] {'gx'}, dimensions={0} | all-to-all | bytes 131072 | tf_op jit(solution)/shard_map/all_to_all | solution.py:522
  171.1 14.4 %all-to-all-start.5 = ((f32[64,1,128]{2,1,0:T(1,128)}), f32[64,1,128]{2,1,0:T(1,128)S(1)}, u32[]{:S(2)}, u32[]{:S(2)}) async-start(f32[64,1,128]{2,1,0:T(1,128)} %get-tuple-element.63), calls=%async_computation.5 | async-start | bytes 65536 | tf_op jit(solution)/shard_map/all_to_all | solution.py:525
  185.5 1.5 shard_map.268
  187.0 2.2 %collective-permute-start.8 = (f32[1,8,168]{2,1,0:T(8,128)S(1)}, f32[1,8,168]{2,1,0:T(8,128)S(1)}, u32[]{:S(2)}, u32[]{:S(2)}) collective-permute-start(f32[1,8,168]{2,1,0:T(8,128)S(1)} %get-tuple-element.69), channel_id=1, source_target_pairs={{0,64},{64,128},{128,192},{192,256},{256,320},{320,384},{384,448},... | collective-permute-start | bytes 16136 | tf_op jit(solution)/shard_map/ppermute | solution.py:496
  189.2 5.8 %collective-permute-done.8.xl_ref = f32[1,8,168]{2,1,0:T(8,128)S(1)} collective-permute-done((f32[1,8,168]{2,1,0:T(8,128)S(1)}, f32[1,8,168]{2,1,0:T(8,128)S(1)}, u32[]{:S(2)}, u32[]{:S(2)}) %collective-permute-start.8) | collective-permute-done | bytes 5408 | tf_op jit(solution)/shard_map/ppermute | solution.py:496
  195.1 2.5 %collective-permute-start.9 = (f32[7,1,168]{2,1,0:T(1,128)S(1)}, f32[7,1,168]{2,1,0:T(1,128)S(1)}, u32[]{:S(2)}, u32[]{:S(2)}) collective-permute-start(f32[7,1,168]{2,1,0:T(1,128)S(1)} %get-tuple-element.71), channel_id=1, source_target_pairs={{0,1},{1,2},{2,3},{3,4},{4,5},{5,6},{6,7},{7,8},{8,9},{9,10},{10,1... | collective-permute-start | bytes 14120 | tf_op jit(solution)/shard_map/ppermute | solution.py:496
  198.3 9.5 %all-to-all-done.5.sums_ref = f32[64,1,128]{2,1,0:T(1,128)S(1)} async-done(((f32[64,1,128]{2,1,0:T(1,128)}), f32[64,1,128]{2,1,0:T(1,128)S(1)}, u32[]{:S(2)}, u32[]{:S(2)}) %all-to-all-start.5) | async-done | bytes 32800 | tf_op jit(solution)/shard_map/all_to_all | solution.py:525
  (88 shorter events, 18.7 us)
Async XLA Ops:
  5.5 19.3 %copy-start.3 = (f32[128,128]{1,0:T(8,128)S(1)}, f32[128,128]{1,0:T(8,128)}, u32[]{:S(2)}) copy-start(f32[128,128]{1,0:T(8,128)} %constant.72.clone.refs_2_.refs_3_.refs_4_) | copy-start | bytes 196612
  24.8 51.4 %copy-start.7 = (f32[168,240]{1,0:T(8,128)S(1)}, f32[168,240]{1,0:T(8,128)}, u32[]{:S(2)}) copy-start(f32[168,240]{1,0:T(8,128)} %constant.54.clone.refs_5_) | copy-start | bytes 483844
  24.8 51.4 %copy-start.8 = (f32[160,160]{1,0:T(8,128)S(1)}, f32[160,160]{1,0:T(8,128)}, u32[]{:S(2)}) copy-start(f32[160,160]{1,0:T(8,128)} %constant.53.clone.refs_4_) | copy-start | bytes 307204
  24.8 51.4 %copy-start.9 = (f32[160,160]{1,0:T(8,128)S(1)}, f32[160,160]{1,0:T(8,128)}, u32[]{:S(2)}) copy-start(f32[160,160]{1,0:T(8,128)} %constant.52.clone.refs_3_) | copy-start | bytes 307204
  24.8 51.4 %copy-start.20 = (f32[24,240]{1,0:T(8,128)S(1)}, f32[24,240]{1,0:T(8,128)}, u32[]{:S(2)}) copy-start(f32[24,240]{1,0:T(8,128)} %constant.58.clone.refs_0_) | copy-start | bytes 69124
  26.2 50.0 %copy-start.4 = (f32[240,168]{1,0:T(8,128)S(1)}, f32[240,168]{1,0:T(8,128)}, u32[]{:S(2)}) copy-start(f32[240,168]{1,0:T(8,128)} %constant.55.clone.refs_6_) | copy-start | bytes 483844
  26.2 50.0 %copy-start.17 = (f32[160,1]{1,0:T(8,128)S(1)}, f32[160,1]{1,0:T(8,128)}, u32[]{:S(2)}) copy-start(f32[160,1]{1,0:T(8,128)} %constant.56.clone.refs_1_) | copy-start | bytes 1924
  26.2 68.3 %all-to-all-start.1 = ((f32[64,1,640]{2,1,0:T(1,128)}), f32[64,1,640]{2,1,0:T(1,128)S(1)}, u32[]{:S(2)}, u32[]{:S(2)}) async-start(f32[64,1,640]{2,1,0:T(1,128)} %get-tuple-element.37), calls=%async_computation.1 | async-start | bytes 327680 | tf_op jit(solution)/shard_map/all_to_all | solution.py:525
  61.3 14.9 %collective-permute-start.1 = (f32[52,2,168]{2,1,0:T(2,128)S(1)}, f32[52,2,168]{2,1,0:T(2,128)S(1)}, u32[]{:S(2)}, u32[]{:S(2)}) collective-permute-start(f32[52,2,168]{2,1,0:T(2,128)S(1)} %get-tuple-element.40), channel_id=1, source_target_pairs={{0,63},{1,0},{2,1},{3,2},{4,3},{5,4},{6,5},{7,6},{8,7},{9,8},{10,9... | collective-permute-start | bytes 209672 | tf_op jit(solution)/shard_map/ppermute | solution.py:496
  61.7 3.5 %collective-permute-start = (f32[52,1,168]{2,1,0:T(1,128)S(1)}, f32[52,1,168]{2,1,0:T(1,128)S(1)}, u32[]{:S(2)}, u32[]{:S(2)}) collective-permute-start(f32[52,1,168]{2,1,0:T(1,128)S(1)} %get-tuple-element.39), channel_id=1, source_target_pairs={{0,1},{1,2},{2,3},{3,4},{4,5},{5,6},{6,7},{7,8},{8,9},{9,10},{10,1... | collective-permute-start | bytes 104840 | tf_op jit(solution)/shard_map/ppermute | solution.py:496
  76.9 9.7 %copy-start.11 = (f32[64,1]{1,0:T(8,128)S(1)}, f32[64,1]{1,0:T(8,128)}, u32[]{:S(2)}) copy-start(f32[64,1]{1,0:T(8,128)} %constant.64.clone.refs_6_) | copy-start | bytes 772
  82.4 1.4 collective-permute-start.2
  82.4 4.1 %collective-permute-start.3 = (f32[36,2,168]{2,1,0:T(2,128)S(1)}, f32[36,2,168]{2,1,0:T(2,128)S(1)}, u32[]{:S(2)}, u32[]{:S(2)}) collective-permute-start(f32[36,2,168]{2,1,0:T(2,128)S(1)} %get-tuple-element.45), channel_id=1, source_target_pairs={{0,63},{1,0},{2,1},{3,2},{4,3},{5,4},{6,5},{7,6},{8,7},{9,8},{10,9... | collective-permute-start | bytes 145160 | tf_op jit(solution)/shard_map/ppermute | solution.py:496
  105.5 21.0 %copy-start.10 = (f32[128,168]{1,0:T(8,128)S(1)}, f32[128,168]{1,0:T(8,128)}, u32[]{:S(2)}) copy-start(f32[128,168]{1,0:T(8,128)} %constant.73.clone.zl_ref) | copy-start | bytes 258052
  105.5 54.1 %all-to-all-start.3 = ((f32[64,1,640]{2,1,0:T(1,128)}), f32[64,1,640]{2,1,0:T(1,128)S(1)}, u32[]{:S(2)}, u32[]{:S(2)}) async-start(f32[64,1,640]{2,1,0:T(1,128)} %copy-done.19), calls=%async_computation.3 | async-start | bytes 327680 | tf_op jit(solution)/shard_map/all_to_all | solution.py:525
  129.0 6.3 %collective-permute-start.4 = (f32[24,2,168]{2,1,0:T(2,128)S(1)}, f32[24,2,168]{2,1,0:T(2,128)S(1)}, u32[]{:S(2)}, u32[]{:S(2)}) collective-permute-start(f32[24,2,168]{2,1,0:T(2,128)S(1)} %get-tuple-element.51), channel_id=1, source_target_pairs={{0,1},{1,2},{2,3},{3,4},{4,5},{5,6},{6,7},{7,8},{8,9},{9,10},{10,1... | collective-permute-start | bytes 96776 | tf_op jit(solution)/shard_map/ppermute | solution.py:496
  130.6 8.3 %collective-permute-start.5 = (f32[24,2,168]{2,1,0:T(2,128)S(1)}, f32[24,2,168]{2,1,0:T(2,128)S(1)}, u32[]{:S(2)}, u32[]{:S(2)}) collective-permute-start(f32[24,2,168]{2,1,0:T(2,128)S(1)} %get-tuple-element.52), channel_id=1, source_target_pairs={{0,63},{1,0},{2,1},{3,2},{4,3},{5,4},{6,5},{7,6},{8,7},{9,8},{10,9... | collective-permute-start | bytes 96776 | tf_op jit(solution)/shard_map/ppermute | solution.py:496
  141.6 2.6 %collective-permute-start.6 = (f32[8,2,168]{2,1,0:T(2,128)S(1)}, f32[8,2,168]{2,1,0:T(2,128)S(1)}, u32[]{:S(2)}, u32[]{:S(2)}) collective-permute-start(f32[8,2,168]{2,1,0:T(2,128)S(1)} %get-tuple-element.57), channel_id=1, source_target_pairs={{0,1},{1,2},{2,3},{3,4},{4,5},{5,6},{6,7},{7,8},{8,9},{9,10},{10,1... | collective-permute-start | bytes 32264 | tf_op jit(solution)/shard_map/ppermute | solution.py:496
  141.6 3.5 %collective-permute-start.7 = (f32[8,2,168]{2,1,0:T(2,128)S(1)}, f32[8,2,168]{2,1,0:T(2,128)S(1)}, u32[]{:S(2)}, u32[]{:S(2)}) collective-permute-start(f32[8,2,168]{2,1,0:T(2,128)S(1)} %get-tuple-element.58), channel_id=1, source_target_pairs={{0,63},{1,0},{2,1},{3,2},{4,3},{5,4},{6,5},{7,6},{8,7},{9,8},{10,9... | collective-permute-start | bytes 32264 | tf_op jit(solution)/shard_map/ppermute | solution.py:496
  145.1 14.5 %copy-start.22 = (f32[8,8,168]{2,1,0:T(8,128)S(1)}, f32[8,8,168]{2,1,0:T(8,128)}, u32[]{:S(2)}) copy-start(f32[8,8,168]{2,1,0:T(8,128)} %copy-done.21) | copy-start | bytes 129028
  145.1 14.5 %copy-start.24 = (f32[8,8,168]{2,1,0:T(8,128)S(1)}, f32[8,8,168]{2,1,0:T(8,128)}, u32[]{:S(2)}) copy-start(f32[8,8,168]{2,1,0:T(8,128)} %copy-done.23) | copy-start | bytes 129028
  171.1 36.8 %all-to-all-start.5 = ((f32[64,1,128]{2,1,0:T(1,128)}), f32[64,1,128]{2,1,0:T(1,128)S(1)}, u32[]{:S(2)}, u32[]{:S(2)}) async-start(f32[64,1,128]{2,1,0:T(1,128)} %get-tuple-element.63), calls=%async_computation.5 | async-start | bytes 65536 | tf_op jit(solution)/shard_map/all_to_all | solution.py:525
  187.0 8.0 %collective-permute-start.8 = (f32[1,8,168]{2,1,0:T(8,128)S(1)}, f32[1,8,168]{2,1,0:T(8,128)S(1)}, u32[]{:S(2)}, u32[]{:S(2)}) collective-permute-start(f32[1,8,168]{2,1,0:T(8,128)S(1)} %get-tuple-element.69), channel_id=1, source_target_pairs={{0,64},{64,128},{128,192},{192,256},{256,320},{320,384},{384,448},... | collective-permute-start | bytes 16136 | tf_op jit(solution)/shard_map/ppermute | solution.py:496
  195.1 3.3 %collective-permute-start.9 = (f32[7,1,168]{2,1,0:T(1,128)S(1)}, f32[7,1,168]{2,1,0:T(1,128)S(1)}, u32[]{:S(2)}, u32[]{:S(2)}) collective-permute-start(f32[7,1,168]{2,1,0:T(1,128)S(1)} %get-tuple-element.71), channel_id=1, source_target_pairs={{0,1},{1,2},{2,3},{3,4},{4,5},{5,6},{6,7},{7,8},{8,9},{9,10},{10,1... | collective-permute-start | bytes 14120 | tf_op jit(solution)/shard_map/ppermute | solution.py:496
  (23 other events, 95.1 us)

commit v3 on v2

--- a/solution.py
+++ b/solution.py
@@ -7,6 +7,7 @@
 from jax.experimental import pallas as pl
 from jax.experimental.pallas import tpu as pltpu
 from jax.sharding import PartitionSpec as P
+
 
 HI = lax.Precision.HIGHEST
 LANES = 128
@@ -26,7 +27,7 @@
     size_n = matrix.shape[0]
     current = np.array(matrix)
     vectors = np.eye(size_n)
-    for sweep in range(20):
+    for _ in range(20):
         for row_p in range(size_n - 1):
             for row_q in range(row_p + 1, size_n):
                 off_value = current[row_p, row_q]
@@ -59,7 +60,7 @@
     interior = []
     for guess in guesses:
         position = guess
-        for newton in range(30):
+        for _ in range(30):
             p_now, p_prev = legendre_pair(position, degree)
             first = degree * (position * p_now - p_prev) / (position * position - 1.0)
             second = (2.0 * position * first - degree * (degree + 1) * p_now) / (
@@ -130,8 +131,6 @@
     ww = np.outer(weights, weights).reshape(64, 1)
     inner = np.zeros((8, 8))
     inner[1:7, 1:7] = 1.0
-    owned = np.zeros((8, 8))
-    owned[:7, :7] = 1.0
     plate = inner.reshape(64, 1)
     first = np.array([1.0] * 7 + [0.0])
     last = 1.0 - first
@@ -142,25 +141,20 @@
         kz = float(left @ stiffness @ right)
         k_parts[name] = float((plate.T @ kk @ plate).item()) * wz + float(np.sum(plate * ww)) * kz
         m_parts[name] = float(np.sum(plate * ww)) * wz
-    elems = np.arange(ez)
-    per = ez // c_dev
-    r1 = (elems[None, :] // per == np.arange(c_dev)[:, None]).astype(np.float64)
-    r2 = (((elems[None, :] + 1) % ez) // per == np.arange(c_dev)[:, None]).astype(np.float64)
     wide = LANES // c_dev
     zc = (np.arange(nz)[:, None] // span == np.arange(c_dev)[None, :]).astype(np.float64)
     return dict(
         qq=f32(qq), qqt=f32(qq.T), zf=f32(zf), zft=f32(zf.T), lam_ab=f32(lam_ab.reshape(160, 1)), lam_c=f32(lam_c),
         rep10=f32(np.tile(np.eye(ez), (1, 10))), rep8=f32(np.tile(np.eye(ez), (1, 8))),
         g8=f32(g8), g8t=f32(g8.T), zk=f32(zk), kk=f32(kk), ww=f32(ww), wz=f32(np.repeat(weights, ez)[None]),
-        inner=f32(plate), owned=f32(owned.reshape(64, 1)),
-        r1=f32(r1), r2=f32(r2), r1t=f32(np.tile(r1.T, (1, wide))), r2t=f32(np.tile(r2.T, (1, wide))),
+        inner=f32(plate),
         zct=f32(np.tile(zc, (1, wide))), eye=f32(np.eye(LANES)),
         zl=f32(np.tile(zc.T, (wide, 1))),
         k_parts=k_parts, m_parts=m_parts,
     )
 
 
-def run(kernel, outs, *args, scratch=(), free=()):
+def run(kernel, outs, *args, scratch=(), free=(), limit=16):
     spaces = [pltpu.SMEM if a.dtype == jnp.int32 else pltpu.VMEM for a in args]
     size = sum(math.prod(s) for s in outs) + sum(math.prod(a.shape) for a in args)
     return pl.pallas_call(
@@ -169,7 +163,7 @@
         in_specs=[pl.BlockSpec(memory_space=space) for space in spaces],
         out_specs=[pl.BlockSpec(memory_space=pltpu.VMEM)] * len(outs),
         scratch_shapes=[pltpu.VMEM(shape, jnp.float32) for shape in scratch],
-        compiler_params=pltpu.CompilerParams(vmem_limit_bytes=16 << 20),
+        compiler_params=pltpu.CompilerParams(vmem_limit_bytes=limit << 20),
         cost_estimate=pl.CostEstimate(flops=2 * 6 * 160 * 240 * 168, bytes_accessed=4 * size, transcendentals=0),
     )(*args)
 
@@ -208,6 +202,13 @@
     return jnp.where(lane // 8 == spot, 1.0, 0.0).astype(jnp.float32)
 
 
+def span_mask(shape, axis, size, move):
+    row = lax.broadcasted_iota(jnp.int32, shape, axis) & 7
+    start = row * size + move
+    fine = lax.broadcasted_iota(jnp.int32, shape, 1 - axis)
+    return jnp.where((fine >= start) & (fine < start + size), 1.0, 0.0).astype(jnp.float32)
+
+
 def rows_tile(rows):
     spot = lax.broadcasted_iota(jnp.int32, (8, LANES), 0)
     tile = jnp.zeros((8, LANES), jnp.float32)
@@ -216,18 +217,22 @@
     return tile
 
 
-def first_kernel(k_parts, m_parts, width, idx_ref, b_ref, k_ref, m_ref, x_ref, r1_ref, r2_ref, r1t_ref, r2t_ref, zct_ref, out_ref, scr):
+def first_kernel(k_parts, m_parts, width, idx_ref, b_ref, k_ref, m_ref, x_ref, out_ref, scr):
     k, m = k_ref[...], m_ref[...]
     e11, e12, e22 = (k * k_parts[name] + m * m_parts[name] for name in ("11", "12", "22"))
-    r1, r2 = r1_ref[...], r2_ref[...]
+    nz, ez = b_ref.shape[2], k.shape[1]
+    per, span = ez // 8, nz // 8
     sel = lane_sel(idx_ref[0])
-    small = (dot(r1 * e11 + r2 * e12, r1t_ref[...]) + dot(r1 * e12 + r2 * e22, r2t_ref[...])) * sel
+    owner = span_mask((8, ez), 0, per, 0)
+    after = span_mask((8, ez), 0, per, -1) + span_mask((8, ez), 0, per, ez - 1)
+    owner_t = span_mask((ez, LANES), 1, per, 0)
+    after_t = span_mask((ez, LANES), 1, per, -1) + span_mask((ez, LANES), 1, per, ez - 1)
+    small = (dot(owner * e11 + after * e12, owner_t) + dot(owner * e12 + after * e22, after_t)) * sel
     acc = b_ref[1]
     for x in range(2, 7):
         acc = acc + b_ref[x]
     line = jnp.sum(acc[1:7], axis=0, keepdims=True)
-    rc = dot(line, zct_ref[...]) * sel
-    nz, ez = b_ref.shape[2], k.shape[1]
+    rc = dot(line, span_mask((nz, LANES), 1, span, 0)) * sel
     scr[...] = jnp.zeros_like(scr)
     scr[:, :LANES] = small
     scr[0:1, LANES : 2 * LANES] = rc
@@ -256,7 +261,7 @@
     rows = factor.shape[0]
     rc_col = as_col(rc, eye_ref[:rows])
     part = jnp.sum(rc_col * factor, axis=0, keepdims=True)
-    spread(out_ref, jnp.concatenate([part, jnp.zeros((1, LANES), jnp.float32)], axis=1))
+    spread(out_ref, part)
     count = xl_ref.shape[0]
     nz, ez = bx_ref.shape[2], k_ref.shape[1]
     base = width + 2 * LANES
@@ -527,10 +532,10 @@
     group = (n_gx, c_dev, LANES)
     aux = -(-(2 * LANES + 7 * nz) // LANES) * LANES
     (pay,) = run(kernel(first_kernel, tab["k_parts"], tab["m_parts"], width), [(n_gx, c_dev, width + aux)],
-                 idx, b, k, m, coarse_factor, tab["r1"], tab["r2"], tab["r1t"], tab["r2t"], zct, scratch=[(8, aux)])
+                 idx, b, k, m, coarse_factor, scratch=[(8, aux)], limit=56)
     xl = swap_gx(pay)
 
-    outs = [(n_gy, 1, width + LANES), (52, 8, nz), (52, 1, nz), (52, 2, nz), (8, ez), (8, ez)]
+    outs = [(n_gy, 1, width), (52, 8, nz), (52, 1, nz), (52, 2, nz), (8, ez), (8, ez)]
     pay, bx, hi, lo, ks, ms = run(kernel(coarse_in_kernel, width), outs, idx, xl, eye, free=(0,))
     y_low, y_high = shift(hi, "gy", 1), shift(lo, "gy", -1)
     sums = swap_gy(pay)
@@ -571,6 +576,7 @@
 
 def solution(mesh):
     placed = (P("gx", "gy", None), P("gx", "gy", None), P("gx", "gy", None), P(("gx", "gy"), None))
+
     return jax.shard_map(
         local,
         mesh=mesh,

time: 209 us -> 203 us (0.971)
  local copies, waits for them, and re-layouts: 6.66 us -> 2.08 us
    unnamed x68 -> x54, local copies, waits for them, and re-layouts: 6.66 us -> 2.08 us
    ppermute x10, waiting for transfers between devices: 33.3 us -> 29.7 us  [shift(): lax.ppermute(value, axis, [(i, (i + step) % count) for i in range(count)])]
where the time goes in v3:
time: 203 us
  starting transfers between devices  80.5 us (40%)
  waiting for transfers between devices  59.3 us (29%)
  blocking collectives  38.6 us (19%)
  Pallas kernels  20.7 us (10%)
  local copies, waits for them, and re-layouts  2.08 us (1%)
    all_to_all x3, starting transfers between devices, swap_gy(): return lax.all_to_all(value, 'gy', 0, 0)  69.9 us
    all_to_all x3, blocking collectives, swap_gx(): return lax.all_to_all(value, 'gx', 0, 0)  38.6 us
    ppermute x10, waiting for transfers between devices, shift(): lax.ppermute(value, axis, [(i, (i + step) % count) for i in range(count)])  29.7 us
    all_to_all x3, waiting for transfers between devices, swap_gy(): return lax.all_to_all(value, 'gy', 0, 0)  29.6 us
    pallas_call x14, Pallas kernels, run(): pl.pallas_call(kernel, out_shape=[(jax.ShapeDtypeStruct if i in free else...  20.7 us
    ppermute x10, starting transfers between devices, shift(): lax.ppermute(value, axis, [(i, (i + step) % count) for i in range(count)])  10.5 us
  transfers between devices with their start and end apart: 13, of which 13 were waited for; matrix products, arithmetic and copies ran while one was open for 0% of the time, Pallas kernels for 7%

profile of v3, /device:TPU:1, one launch (start us, length us, event | category | flops | bytes accessed | tf_op | source)
XLA Modules:
  0.0 202.7 jit_solution(13153785591558280694)
XLA Ops:
  2.5 19.3 %all_to_all.30.refs_1_.refs_2_ = f32[16,8,2048]{2,1,0:T(8,128)S(1)} all-to-all(f32[16,8,2048]{2,1,0:T(8,128)S(1)} %shard_map.221), channel_id=1, replica_groups=mesh['gx'=16,'gy'=64] {'gx'}, dimensions={0} | all-to-all | bytes 2097152 | tf_op jit(solution)/shard_map/all_to_all | solution.py:527
  23.2 35.1 %all-to-all-start.1 = ((f32[64,1,512]{2,1,0:T(1,128)}), f32[64,1,512]{2,1,0:T(1,128)S(1)}, u32[]{:S(2)}, u32[]{:S(2)}) async-start(f32[64,1,512]{2,1,0:T(1,128)} %get-tuple-element.37), calls=%async_computation.1 | async-start | bytes 262144 | tf_op jit(solution)/shard_map/all_to_all | solution.py:530
  60.1 2.3 %collective-permute-done.yl_ref = f32[52,1,168]{2,1,0:T(1,128)S(1)} collective-permute-done((f32[52,1,168]{2,1,0:T(1,128)S(1)}, f32[52,1,168]{2,1,0:T(1,128)S(1)}, u32[]{:S(2)}, u32[]{:S(2)}) %collective-permute-start) | collective-permute-done | bytes 34976 | tf_op jit(solution)/shard_map/ppermute | solution.py:501
  62.3 7.3 %collective-permute-done.1.yh_ref = f32[52,2,168]{2,1,0:T(2,128)S(1)} collective-permute-done((f32[52,2,168]{2,1,0:T(2,128)S(1)}, f32[52,2,168]{2,1,0:T(2,128)S(1)}, u32[]{:S(2)}, u32[]{:S(2)}) %collective-permute-start.1) | collective-permute-done | bytes 69920 | tf_op jit(solution)/shard_map/ppermute | solution.py:501
  70.4 5.4 %shard_map.223 = (f32[36,16,168]{2,1,0:T(8,128)S(1)}, f32[36,2,168]{2,1,0:T(2,128)S(1)}, f32[36,2,168]{2,1,0:T(2,128)S(1)}) custom-call(f32[52,8,168]{2,1,0:T(8,128)S(1)} %get-tuple-element.38.bx_ref, f32[52,1,168]{2,1,0:T(1,128)S(1)} %collective-permute-done.yl_ref, f32[52,2,168]{2,1,0:T(2,128)S(1)} %collective-permute-done.1.yh_ref, ...), custom_call_target="tpu_custom_call" | custom-call | flops 77414400 | bytes 1421760 | tf_op jit(solution)/shard_map/pallas_call | solution.py:160
  77.2 2.7 %collective-permute-done.3.yh_ref = f32[36,2,168]{2,1,0:T(2,128)S(1)} collective-permute-done((f32[36,2,168]{2,1,0:T(2,128)S(1)}, f32[36,2,168]{2,1,0:T(2,128)S(1)}, u32[]{:S(2)}, u32[]{:S(2)}) %collective-permute-start.3) | collective-permute-done | bytes 48416 | tf_op jit(solution)/shard_map/ppermute | solution.py:501
  80.1 1.8 shard_map.224
  82.5 6.5 %all-to-all-done.1.refs_0_ = f32[64,1,512]{2,1,0:T(1,128)S(1)} async-done(((f32[64,1,512]{2,1,0:T(1,128)}), f32[64,1,512]{2,1,0:T(1,128)S(1)}, u32[]{:S(2)}, u32[]{:S(2)}) %all-to-all-start.1) | async-done | bytes 131104 | tf_op jit(solution)/shard_map/all_to_all | solution.py:530
  89.2 9.9 %all_to_all.31.refs_0_ = f32[16,8,128]{2,1,0:T(8,128)S(1)} all-to-all(f32[16,8,128]{2,1,0:T(8,128)S(1)} %shard_map.225), channel_id=1, replica_groups=mesh['gx'=16,'gy'=64] {'gx'}, dimensions={0} | all-to-all | bytes 131072 | tf_op jit(solution)/shard_map/all_to_all | solution.py:527
  100.0 20.4 %all-to-all-start.3 = ((f32[64,1,640]{2,1,0:T(1,128)}), f32[64,1,640]{2,1,0:T(1,128)S(1)}, u32[]{:S(2)}, u32[]{:S(2)}) async-start(f32[64,1,640]{2,1,0:T(1,128)} %copy-done.16), calls=%async_computation.3 | async-start | bytes 327680 | tf_op jit(solution)/shard_map/all_to_all | solution.py:530
  120.5 2.5 %shard_map.227 = (f32[8,8,168]{2,1,0:T(8,128)S(1)}, f32[24,8,168]{2,1,0:T(8,128)S(1)}, f32[24,2,168]{2,1,0:T(2,128)S(1)}, f32[24,2,168]{2,1,0:T(2,128)S(1)}) custom-call(s32[2]{0:T(128)S(1)} %copy-done.22, f32[36,8,168]{2,1,0:T(8,128)S(1)} %get-tuple-element.48.u_ref, f32[1,128]{1,0:T(1,128)S(1)} %get-tuple-element.49.x_ref.refs_2_, ...), custom_call_target="tpu_custom_call" | custom-call | flops 77414400 | bytes 941320 | tf_op jit(solution)/shard_map/pallas_call | solution.py:160
  123.0 1.6 collective-permute-start.4
  124.6 4.7 %collective-permute-done.4.yl_ref = f32[24,2,168]{2,1,0:T(2,128)S(1)} collective-permute-done((f32[24,2,168]{2,1,0:T(2,128)S(1)}, f32[24,2,168]{2,1,0:T(2,128)S(1)}, u32[]{:S(2)}, u32[]{:S(2)}) %collective-permute-start.4) | collective-permute-done | bytes 32288 | tf_op jit(solution)/shard_map/ppermute | solution.py:501
  129.3 3.6 %collective-permute-done.5.yh_ref = f32[24,2,168]{2,1,0:T(2,128)S(1)} collective-permute-done((f32[24,2,168]{2,1,0:T(2,128)S(1)}, f32[24,2,168]{2,1,0:T(2,128)S(1)}, u32[]{:S(2)}, u32[]{:S(2)}) %collective-permute-start.5) | collective-permute-done | bytes 32288 | tf_op jit(solution)/shard_map/ppermute | solution.py:501
  133.0 2.6 %shard_map.228 = (f32[8,8,168]{2,1,0:T(8,128)S(1)}, f32[8,16,168]{2,1,0:T(8,128)S(1)}, f32[8,2,168]{2,1,0:T(2,128)S(1)}, f32[8,2,168]{2,1,0:T(2,128)S(1)}) custom-call(f32[24,8,168]{2,1,0:T(8,128)S(1)} %get-tuple-element.50.qx_ref, f32[24,2,168]{2,1,0:T(2,128)S(1)} %collective-permute-done.4.yl_ref, f32[24,2,168]{2,1,0:T(2,128)S(1)} %collective-permute-done.5.yh_ref, ...), custom_call_target="tpu_custom_call" | custom-call | flops 77414400 | bytes 897600 | tf_op jit(solution)/shard_map/pallas_call | solution.py:160
  135.6 1.9 collective-permute-start.7
  140.1 13.6 %all-to-all-done.3.refs_1_ = f32[64,1,640]{2,1,0:T(1,128)S(1)} async-done(((f32[64,1,640]{2,1,0:T(1,128)}), f32[64,1,640]{2,1,0:T(1,128)S(1)}, u32[]{:S(2)}, u32[]{:S(2)}) %all-to-all-start.3) | async-done | bytes 163872 | tf_op jit(solution)/shard_map/all_to_all | solution.py:530
  154.6 9.5 %all_to_all.32.refs_0_ = f32[16,8,128]{2,1,0:T(8,128)S(1)} all-to-all(f32[16,8,128]{2,1,0:T(8,128)S(1)} %get-tuple-element.61), channel_id=1, replica_groups=mesh['gx'=16,'gy'=64] {'gx'}, dimensions={0} | all-to-all | bytes 131072 | tf_op jit(solution)/shard_map/all_to_all | solution.py:527
  165.1 14.4 %all-to-all-start.5 = ((f32[64,1,128]{2,1,0:T(1,128)}), f32[64,1,128]{2,1,0:T(1,128)S(1)}, u32[]{:S(2)}, u32[]{:S(2)}) async-start(f32[64,1,128]{2,1,0:T(1,128)} %get-tuple-element.63), calls=%async_computation.5 | async-start | bytes 65536 | tf_op jit(solution)/shard_map/all_to_all | solution.py:530
  179.5 1.5 shard_map.232
  181.0 2.2 %collective-permute-start.8 = (f32[1,8,168]{2,1,0:T(8,128)S(1)}, f32[1,8,168]{2,1,0:T(8,128)S(1)}, u32[]{:S(2)}, u32[]{:S(2)}) collective-permute-start(f32[1,8,168]{2,1,0:T(8,128)S(1)} %get-tuple-element.69), channel_id=1, source_target_pairs={{0,64},{64,128},{128,192},{192,256},{256,320},{320,384},{384,448},... | collective-permute-start | bytes 16136 | tf_op jit(solution)/shard_map/ppermute | solution.py:501
  183.2 5.8 %collective-permute-done.8.xl_ref = f32[1,8,168]{2,1,0:T(8,128)S(1)} collective-permute-done((f32[1,8,168]{2,1,0:T(8,128)S(1)}, f32[1,8,168]{2,1,0:T(8,128)S(1)}, u32[]{:S(2)}, u32[]{:S(2)}) %collective-permute-start.8) | collective-permute-done | bytes 5408 | tf_op jit(solution)/shard_map/ppermute | solution.py:501
  189.1 2.5 %collective-permute-start.9 = (f32[7,1,168]{2,1,0:T(1,128)S(1)}, f32[7,1,168]{2,1,0:T(1,128)S(1)}, u32[]{:S(2)}, u32[]{:S(2)}) collective-permute-start(f32[7,1,168]{2,1,0:T(1,128)S(1)} %get-tuple-element.71), channel_id=1, source_target_pairs={{0,1},{1,2},{2,3},{3,4},{4,5},{5,6},{6,7},{7,8},{8,9},{9,10},{10,1... | collective-permute-start | bytes 14120 | tf_op jit(solution)/shard_map/ppermute | solution.py:501
  192.3 9.5 %all-to-all-done.5.sums_ref = f32[64,1,128]{2,1,0:T(1,128)S(1)} async-done(((f32[64,1,128]{2,1,0:T(1,128)}), f32[64,1,128]{2,1,0:T(1,128)S(1)}, u32[]{:S(2)}, u32[]{:S(2)}) %all-to-all-start.5) | async-done | bytes 32800 | tf_op jit(solution)/shard_map/all_to_all | solution.py:530
  (74 shorter events, 15.1 us)
Async XLA Ops:
  2.5 19.3 %copy-start.3 = (f32[128,128]{1,0:T(8,128)S(1)}, f32[128,128]{1,0:T(8,128)}, u32[]{:S(2)}) copy-start(f32[128,128]{1,0:T(8,128)} %constant.60.clone.refs_2_.refs_3_.refs_4_) | copy-start | bytes 196612
  2.5 19.3 %copy-start.22 = (s32[2]{0:T(128)S(1)}, s32[2]{0:T(128)}, u32[]{:S(2)}) copy-start(s32[2]{0:T(128)} %pad_add_fusion.refs_0_.idx_ref) | copy-start | bytes 28
  21.8 47.8 %copy-start.5 = (f32[168,240]{1,0:T(8,128)S(1)}, f32[168,240]{1,0:T(8,128)}, u32[]{:S(2)}) copy-start(f32[168,240]{1,0:T(8,128)} %constant.46.clone.refs_5_) | copy-start | bytes 483844
  21.8 47.8 %copy-start.6 = (f32[160,160]{1,0:T(8,128)S(1)}, f32[160,160]{1,0:T(8,128)}, u32[]{:S(2)}) copy-start(f32[160,160]{1,0:T(8,128)} %constant.45.clone.refs_4_) | copy-start | bytes 307204
  21.8 47.8 %copy-start.7 = (f32[160,160]{1,0:T(8,128)S(1)}, f32[160,160]{1,0:T(8,128)}, u32[]{:S(2)}) copy-start(f32[160,160]{1,0:T(8,128)} %constant.44.clone.refs_3_) | copy-start | bytes 307204
  21.8 47.8 %copy-start.15 = (f32[160,1]{1,0:T(8,128)S(1)}, f32[160,1]{1,0:T(8,128)}, u32[]{:S(2)}) copy-start(f32[160,1]{1,0:T(8,128)} %constant.48.clone.refs_1_) | copy-start | bytes 1924
  23.2 46.4 %copy-start.4 = (f32[240,168]{1,0:T(8,128)S(1)}, f32[240,168]{1,0:T(8,128)}, u32[]{:S(2)}) copy-start(f32[240,168]{1,0:T(8,128)} %constant.47.clone.refs_6_) | copy-start | bytes 483844
  23.2 46.4 %copy-start.17 = (f32[24,240]{1,0:T(8,128)S(1)}, f32[24,240]{1,0:T(8,128)}, u32[]{:S(2)}) copy-start(f32[24,240]{1,0:T(8,128)} %constant.50.clone.refs_0_) | copy-start | bytes 69124
  23.2 65.7 %all-to-all-start.1 = ((f32[64,1,512]{2,1,0:T(1,128)}), f32[64,1,512]{2,1,0:T(1,128)S(1)}, u32[]{:S(2)}, u32[]{:S(2)}) async-start(f32[64,1,512]{2,1,0:T(1,128)} %get-tuple-element.37), calls=%async_computation.1 | async-start | bytes 262144 | tf_op jit(solution)/shard_map/all_to_all | solution.py:530
  58.3 11.3 %collective-permute-start.1 = (f32[52,2,168]{2,1,0:T(2,128)S(1)}, f32[52,2,168]{2,1,0:T(2,128)S(1)}, u32[]{:S(2)}, u32[]{:S(2)}) collective-permute-start(f32[52,2,168]{2,1,0:T(2,128)S(1)} %get-tuple-element.40), channel_id=1, source_target_pairs={{0,63},{1,0},{2,1},{3,2},{4,3},{5,4},{6,5},{7,6},{8,7},{9,8},{10,9... | collective-permute-start | bytes 209672 | tf_op jit(solution)/shard_map/ppermute | solution.py:501
  58.8 3.5 %collective-permute-start = (f32[52,1,168]{2,1,0:T(1,128)S(1)}, f32[52,1,168]{2,1,0:T(1,128)S(1)}, u32[]{:S(2)}, u32[]{:S(2)}) collective-permute-start(f32[52,1,168]{2,1,0:T(1,128)S(1)} %get-tuple-element.39), channel_id=1, source_target_pairs={{0,1},{1,2},{2,3},{3,4},{4,5},{5,6},{6,7},{7,8},{8,9},{9,10},{10,1... | collective-permute-start | bytes 104840 | tf_op jit(solution)/shard_map/ppermute | solution.py:501
  75.8 1.4 collective-permute-start.2
  75.9 4.1 %collective-permute-start.3 = (f32[36,2,168]{2,1,0:T(2,128)S(1)}, f32[36,2,168]{2,1,0:T(2,128)S(1)}, u32[]{:S(2)}, u32[]{:S(2)}) collective-permute-start(f32[36,2,168]{2,1,0:T(2,128)S(1)} %get-tuple-element.45), channel_id=1, source_target_pairs={{0,63},{1,0},{2,1},{3,2},{4,3},{5,4},{6,5},{7,6},{8,7},{9,8},{10,9... | collective-permute-start | bytes 145160 | tf_op jit(solution)/shard_map/ppermute | solution.py:501
  100.0 20.4 %copy-start.8 = (f32[128,168]{1,0:T(8,128)S(1)}, f32[128,168]{1,0:T(8,128)}, u32[]{:S(2)}) copy-start(f32[128,168]{1,0:T(8,128)} %constant.61.clone.zl_ref) | copy-start | bytes 258052
  100.0 53.6 %all-to-all-start.3 = ((f32[64,1,640]{2,1,0:T(1,128)}), f32[64,1,640]{2,1,0:T(1,128)S(1)}, u32[]{:S(2)}, u32[]{:S(2)}) async-start(f32[64,1,640]{2,1,0:T(1,128)} %copy-done.16), calls=%async_computation.3 | async-start | bytes 327680 | tf_op jit(solution)/shard_map/all_to_all | solution.py:530
  123.0 6.3 %collective-permute-start.4 = (f32[24,2,168]{2,1,0:T(2,128)S(1)}, f32[24,2,168]{2,1,0:T(2,128)S(1)}, u32[]{:S(2)}, u32[]{:S(2)}) collective-permute-start(f32[24,2,168]{2,1,0:T(2,128)S(1)} %get-tuple-element.51), channel_id=1, source_target_pairs={{0,1},{1,2},{2,3},{3,4},{4,5},{5,6},{6,7},{7,8},{8,9},{9,10},{10,1... | collective-permute-start | bytes 96776 | tf_op jit(solution)/shard_map/ppermute | solution.py:501
  124.6 8.3 %collective-permute-start.5 = (f32[24,2,168]{2,1,0:T(2,128)S(1)}, f32[24,2,168]{2,1,0:T(2,128)S(1)}, u32[]{:S(2)}, u32[]{:S(2)}) collective-permute-start(f32[24,2,168]{2,1,0:T(2,128)S(1)} %get-tuple-element.52), channel_id=1, source_target_pairs={{0,63},{1,0},{2,1},{3,2},{4,3},{5,4},{6,5},{7,6},{8,7},{9,8},{10,9... | collective-permute-start | bytes 96776 | tf_op jit(solution)/shard_map/ppermute | solution.py:501
  135.6 2.6 %collective-permute-start.6 = (f32[8,2,168]{2,1,0:T(2,128)S(1)}, f32[8,2,168]{2,1,0:T(2,128)S(1)}, u32[]{:S(2)}, u32[]{:S(2)}) collective-permute-start(f32[8,2,168]{2,1,0:T(2,128)S(1)} %get-tuple-element.57), channel_id=1, source_target_pairs={{0,1},{1,2},{2,3},{3,4},{4,5},{5,6},{6,7},{7,8},{8,9},{9,10},{10,1... | collective-permute-start | bytes 32264 | tf_op jit(solution)/shard_map/ppermute | solution.py:501
  135.6 3.5 %collective-permute-start.7 = (f32[8,2,168]{2,1,0:T(2,128)S(1)}, f32[8,2,168]{2,1,0:T(2,128)S(1)}, u32[]{:S(2)}, u32[]{:S(2)}) collective-permute-start(f32[8,2,168]{2,1,0:T(2,128)S(1)} %get-tuple-element.58), channel_id=1, source_target_pairs={{0,63},{1,0},{2,1},{3,2},{4,3},{5,4},{6,5},{7,6},{8,7},{9,8},{10,9... | collective-permute-start | bytes 32264 | tf_op jit(solution)/shard_map/ppermute | solution.py:501
  139.1 14.5 %copy-start.19 = (f32[8,8,168]{2,1,0:T(8,128)S(1)}, f32[8,8,168]{2,1,0:T(8,128)}, u32[]{:S(2)}) copy-start(f32[8,8,168]{2,1,0:T(8,128)} %copy-done.18) | copy-start | bytes 129028
  139.1 14.5 %copy-start.21 = (f32[8,8,168]{2,1,0:T(8,128)S(1)}, f32[8,8,168]{2,1,0:T(8,128)}, u32[]{:S(2)}) copy-start(f32[8,8,168]{2,1,0:T(8,128)} %copy-done.20) | copy-start | bytes 129028
  165.1 36.8 %all-to-all-start.5 = ((f32[64,1,128]{2,1,0:T(1,128)}), f32[64,1,128]{2,1,0:T(1,128)S(1)}, u32[]{:S(2)}, u32[]{:S(2)}) async-start(f32[64,1,128]{2,1,0:T(1,128)} %get-tuple-element.63), calls=%async_computation.5 | async-start | bytes 65536 | tf_op jit(solution)/shard_map/all_to_all | solution.py:530
  181.0 8.0 %collective-permute-start.8 = (f32[1,8,168]{2,1,0:T(8,128)S(1)}, f32[1,8,168]{2,1,0:T(8,128)S(1)}, u32[]{:S(2)}, u32[]{:S(2)}) collective-permute-start(f32[1,8,168]{2,1,0:T(8,128)S(1)} %get-tuple-element.69), channel_id=1, source_target_pairs={{0,64},{64,128},{128,192},{192,256},{256,320},{320,384},{384,448},... | collective-permute-start | bytes 16136 | tf_op jit(solution)/shard_map/ppermute | solution.py:501
  189.1 3.3 %collective-permute-start.9 = (f32[7,1,168]{2,1,0:T(1,128)S(1)}, f32[7,1,168]{2,1,0:T(1,128)S(1)}, u32[]{:S(2)}, u32[]{:S(2)}) collective-permute-start(f32[7,1,168]{2,1,0:T(1,128)S(1)} %get-tuple-element.71), channel_id=1, source_target_pairs={{0,1},{1,2},{2,3},{3,4},{4,5},{5,6},{6,7},{7,8},{8,9},{9,10},{10,1... | collective-permute-start | bytes 14120 | tf_op jit(solution)/shard_map/ppermute | solution.py:501
  (16 other events, 108.4 us)

commit v4 on v3

--- a/solution.py
+++ b/solution.py
@@ -134,6 +134,8 @@
     plate = inner.reshape(64, 1)
     first = np.array([1.0] * 7 + [0.0])
     last = 1.0 - first
+    face = np.zeros((8, 1))
+    face[1:7, 0] = weights[1:7] * np.sum(stiffness[7, 1:7])
     k_parts = {}
     m_parts = {}
     for name, left, right in (("11", first, first), ("12", first, last), ("22", last, last)):
@@ -147,7 +149,7 @@
         qq=f32(qq), qqt=f32(qq.T), zf=f32(zf), zft=f32(zf.T), lam_ab=f32(lam_ab.reshape(160, 1)), lam_c=f32(lam_c),
         rep10=f32(np.tile(np.eye(ez), (1, 10))), rep8=f32(np.tile(np.eye(ez), (1, 8))),
         g8=f32(g8), g8t=f32(g8.T), zk=f32(zk), kk=f32(kk), ww=f32(ww), wz=f32(np.repeat(weights, ez)[None]),
-        inner=f32(plate),
+        inner=f32(plate), face=f32(face),
         zct=f32(np.tile(zc, (1, wide))), eye=f32(np.eye(LANES)),
         zl=f32(np.tile(zc.T, (wide, 1))),
         k_parts=k_parts, m_parts=m_parts,
@@ -245,19 +247,20 @@
         out_ref[peer, :, width:] = scr[...]
 
 
-def split_group(xl_ref, width):
-    rows = xl_ref.shape[0] * xl_ref.shape[1]
-    small = xl_ref[:, :, width : width + LANES].reshape(rows, LANES)
-    rc = jnp.sum(xl_ref[:, 0:1, width + LANES : width + 2 * LANES], axis=0)
-    return xl_ref[:, :, :width].reshape(rows, width), small, rc
+def split_group(group_ref, width):
+    rows = group_ref.shape[0] * group_ref.shape[1]
+    return group_ref[:, :, :width].reshape(rows, width), group_ref[:, :, width : width + LANES].reshape(rows, LANES)
 
 
 def spread(out_ref, row):
     out_ref[...] = jnp.broadcast_to(row[None], out_ref.shape)
 
 
-def coarse_in_kernel(width, idx_ref, xl_ref, eye_ref, out_ref, bx_ref, hi_ref, lo_ref, k_ref, m_ref):
-    factor, _, rc = split_group(xl_ref, width)
+def coarse_in_kernel(width, idx_ref, xl_ref, eye_ref, out_ref, bx_ref, hi_ref, lo_ref, k_ref, m_ref, group_ref, rc_ref):
+    factor, _ = split_group(xl_ref, width)
+    rc = jnp.sum(xl_ref[:, 0:1, width + LANES : width + 2 * LANES], axis=0)
+    rc_ref[...] = rc
+    group_ref[...] = xl_ref[:, :, : width + LANES]
     rows = factor.shape[0]
     rc_col = as_col(rc, eye_ref[:rows])
     part = jnp.sum(rc_col * factor, axis=0, keepdims=True)
@@ -281,7 +284,7 @@
 
 
 def coarse_out_kernel(width, sums_ref, xl_ref, eye_ref, h_ref, out_ref):
-    factor, _, _ = split_group(xl_ref, width)
+    factor, _ = split_group(xl_ref, width)
     rows = factor.shape[0]
     sums = jnp.sum(sums_ref[...], axis=0)
     part = jnp.sum(factor * sums[:, :width], axis=1, keepdims=True)
@@ -291,8 +294,9 @@
     out_ref[...] = jnp.broadcast_to(tile[None], out_ref.shape)
 
 
-def coarse_mid_kernel(width, got_ref, xl_ref, eye_ref, out_ref, x_ref):
-    factor, small, rc = split_group(xl_ref, width)
+def coarse_mid_kernel(width, got_ref, xl_ref, rc_ref, eye_ref, out_ref, x_ref):
+    factor, small = split_group(xl_ref, width)
+    rc = rc_ref[...]
     rows = factor.shape[0]
     eye = eye_ref[:rows]
     got = jnp.sum(got_ref[...], axis=0)
@@ -308,7 +312,7 @@
 
 def pair_kernel(width, idx_ref, sums_ref, xl_ref, eye_ref, b_ref, q_ref, u_ref, au_ref, s_ref, as_ref, inner_ref, zct_ref,
                 out_ref, scal_ref, r_ref):
-    factor, _, _ = split_group(xl_ref, width)
+    factor, _ = split_group(xl_ref, width)
     rows = factor.shape[0]
     sums = jnp.sum(sums_ref[...], axis=0)
     part = jnp.sum(factor * sums[:, :width], axis=1, keepdims=True)
@@ -334,7 +338,7 @@
 
 
 def last_in_kernel(width, got_ref, xl_ref, x0_ref, scal_ref, eye_ref, out_ref, x_ref):
-    _, small, _ = split_group(xl_ref, width)
+    _, small = split_group(xl_ref, width)
     eye = eye_ref[: small.shape[0]]
     got = jnp.sum(got_ref[...], axis=0)
     x1, wr, wt, scal = got[0:1], got[1:2], got[2:3], got[3:4]
@@ -420,12 +424,6 @@
     lo_ref[...] = out_ref[:, 0:2]
 
 
-def fold_v_kernel(v_ref, xl_ref, out_ref, hi_ref):
-    out_ref[...] = v_ref[0:7]
-    out_ref[0] = out_ref[0] + xl_ref[0]
-    hi_ref[...] = out_ref[:, 7:8]
-
-
 def gather_s(u_ref, y_ref, yl_ref, yh_ref):
     u_ref[...] = y_ref[:, 1:9]
     u_ref[:, 0:2] = u_ref[:, 0:2] + yl_ref[...]
@@ -448,11 +446,12 @@
 
 
 def apply_s_kernel(y_ref, yl_ref, yh_ref, k_ref, m_ref, *refs):
-    consts, (s_ref, as_ref) = refs[:-2], refs[-2:]
+    consts, (s_ref, as_ref, hi_ref) = refs[:-3], refs[-3:]
     nz = s_ref.shape[2]
     gather_s(s_ref, y_ref, yl_ref, yh_ref)
     out = apply(s_ref[...].reshape(64, nz), k_ref[...], m_ref[...], *(ref[...] for ref in consts))
     as_ref[...] = out.reshape(8, 8, nz)
+    hi_ref[...] = as_ref[7:8]
 
 
 def apply_p_kernel(idx_ref, u_ref, x_ref, k_ref, m_ref, inner_ref, zl_ref, *refs):
@@ -485,15 +484,21 @@
     lo_ref[...] = q_ref[:, 0:2]
 
 
-def apply_w_kernel(idx_ref, s_ref, x_ref, k_ref, m_ref, inner_ref, zl_ref, *refs):
+def apply_w_kernel(idx_ref, s_ref, x_ref, side_ref, k_ref, m_ref, ks_ref, inner_ref, zl_ref, face_ref, *refs):
     consts, (w_ref, v_ref, hi_ref) = refs[:-3], refs[-3:]
+    rep8, wz, g8, g8t = consts[:4]
     nz = s_ref.shape[2]
-    line = dot(x_ref[...] * lane_sel(idx_ref[0]), zl_ref[...])
-    w = s_ref[...].reshape(64, nz) + inner_ref[...] * line
+    x1 = x_ref[...]
+    left = lax.rem(idx_ref[0] + idx_ref[1] - 1, idx_ref[1])
+    lines = dot(rows_tile([x1 * lane_sel(idx_ref[0]), x1 * lane_sel(left)]), zl_ref[...])
+    w = s_ref[...].reshape(64, nz) + inner_ref[...] * lines[0:1]
     w_ref[...] = w.reshape(8, 8, nz)
     out = apply(w, k_ref[...], m_ref[...], *(ref[...] for ref in consts)).reshape(8, 8, nz)
     v_ref[...] = out
-    hi_ref[...] = out[7:8]
+    scale = dot(ks_ref[2:3], rep8[...]) * wz[...]
+    share = dot(scale * dot(lines, g8[...]), g8t[...])[1:2]
+    v_ref[0] = v_ref[0] + side_ref[0] + face_ref[...] * share
+    hi_ref[...] = v_ref[0:7, 7:8]
 
 
 def shift(value, axis, step):
@@ -535,8 +540,9 @@
                  idx, b, k, m, coarse_factor, scratch=[(8, aux)], limit=56)
     xl = swap_gx(pay)
 
-    outs = [(n_gy, 1, width), (52, 8, nz), (52, 1, nz), (52, 2, nz), (8, ez), (8, ez)]
-    pay, bx, hi, lo, ks, ms = run(kernel(coarse_in_kernel, width), outs, idx, xl, eye, free=(0,))
+    outs = [(n_gy, 1, width), (52, 8, nz), (52, 1, nz), (52, 2, nz), (8, ez), (8, ez),
+            (n_gx, c_dev, width + LANES), (1, LANES)]
+    pay, bx, hi, lo, ks, ms, members, rc = run(kernel(coarse_in_kernel, width), outs, idx, xl, eye, free=(0,))
     y_low, y_high = shift(hi, "gy", 1), shift(lo, "gy", -1)
     sums = swap_gy(pay)
 
@@ -548,9 +554,9 @@
     wide_u, u, au, h = run(apply_u_kernel, [(36, 8, nz), cube, cube, (8, LANES)], idx, b, y, y_low, y_high, k, m, inner, zct, *apply_tab,
                           free=(1, 2))
 
-    (pay,) = run(kernel(coarse_out_kernel, width), [group], sums, xl, eye, h)
+    (pay,) = run(kernel(coarse_out_kernel, width), [group], sums, members, eye, h)
     got = swap_gx(pay)
-    pay, x0 = run(kernel(coarse_mid_kernel, width), [(n_gy, 1, width + LANES), (1, LANES)], got, xl, eye, free=(0,))
+    pay, x0 = run(kernel(coarse_mid_kernel, width), [(n_gy, 1, width + LANES), (1, LANES)], got, members, rc, eye, free=(0,))
     sums = swap_gy(pay)
 
     p, qx, hi, lo = run(apply_p_kernel, [cube, (24, 8, nz), (24, 2, nz), (24, 2, nz)], idx, wide_u, x0, ks, ms, inner, zl, *apply_tab,
@@ -559,16 +565,15 @@
     q, y, hi, lo = run(schwarz_q_kernel, [cube, (8, 16, nz)] + sides, qx, y_low, y_high, ks, ms, *solve_tab,
                        scratch=[(24, 16, nz), (384, 10 * ez), (128, 10 * ez)])
     y_low, y_high = shift(hi, "gy", 1), shift(lo, "gy", -1)
-    s, a_s = run(apply_s_kernel, [cube, cube], y, y_low, y_high, k, m, *apply_tab)
-
-    pay, scal, resid = run(kernel(pair_kernel, width), [group, (1, LANES), cube], idx, sums, xl, eye, b, q, u, au, s, a_s, inner, zct)
+    s, a_s, hi = run(apply_s_kernel, [cube, cube, (1, 8, nz)], y, y_low, y_high, k, m, *apply_tab)
+    side = shift(hi, "gx", 1)
+
+    pay, scal, resid = run(kernel(pair_kernel, width), [group, (1, LANES), cube], idx, sums, members, eye, b, q, u, au, s, a_s, inner, zct)
     got = swap_gx(pay)
-    pay, x1 = run(kernel(last_in_kernel, width), [(n_gy, 1, LANES), (1, LANES)], got, xl, x0, scal, eye, free=(0,))
+    pay, x1 = run(kernel(last_in_kernel, width), [(n_gy, 1, LANES), (1, LANES)], got, members, x0, scal, eye, free=(0,))
     sums = swap_gy(pay)
 
-    w, v, hi = run(apply_w_kernel, [cube, cube, (1, 8, nz)], idx, s, x1, k, m, inner, zl, *apply_tab)
-    x_low = shift(hi, "gx", 1)
-    v, hi = run(fold_v_kernel, [(7, 8, nz), (7, 1, nz)], v, x_low)
+    w, v, hi = run(apply_w_kernel, [cube, cube, (7, 1, nz)], idx, s, x1, side, k, m, ks, inner, zl, tab["face"], *apply_tab)
     y_low = shift(hi, "gy", 1)
     sol, res = run(final_kernel, [(7, 7, nz), (7, 7, nz)], sums, scal, p, w, resid, q, v, y_low, free=(0, 1))
     return sol, res

time: 203 us -> 202 us (level)
    pallas_call x14 -> x13, Pallas kernels: 20.7 us -> 21.6 us  [run(): pl.pallas_call(kernel, out_shape=[(jax.ShapeDtypeStruct if i in free else...]
where the time goes in v4:
time: 202 us
  starting transfers between devices  79.6 us (39%)
  waiting for transfers between devices  59.8 us (30%)
  blocking collectives  38.6 us (19%)
  Pallas kernels  21.6 us (11%)
    all_to_all x3, starting transfers between devices, swap_gy(): return lax.all_to_all(value, 'gy', 0, 0)  69.1 us
    all_to_all x3, blocking collectives, swap_gx(): return lax.all_to_all(value, 'gx', 0, 0)  38.6 us
    all_to_all x3, waiting for transfers between devices, swap_gy(): return lax.all_to_all(value, 'gy', 0, 0)  30.1 us
    ppermute x10, waiting for transfers between devices, shift(): lax.ppermute(value, axis, [(i, (i + step) % count) for i in range(count)])  29.7 us
    pallas_call x13, Pallas kernels, run(): pl.pallas_call(kernel, out_shape=[(jax.ShapeDtypeStruct if i in free else...  21.6 us
    ppermute x10, starting transfers between devices, shift(): lax.ppermute(value, axis, [(i, (i + step) % count) for i in range(count)])  10.5 us
  transfers between devices with their start and end apart: 13, of which 13 were waited for; matrix products, arithmetic and copies ran while one was open for 0% of the time, Pallas kernels for 7%

profile of v4, /device:TPU:1, one launch (start us, length us, event | category | flops | bytes accessed | tf_op | source)
XLA Modules:
  0.0 201.8 jit_solution(12621814018119254193)
XLA Ops:
  2.5 19.3 %all_to_all.30.refs_1_ = f32[16,8,2048]{2,1,0:T(8,128)S(1)} all-to-all(f32[16,8,2048]{2,1,0:T(8,128)S(1)} %shard_map.230), channel_id=1, replica_groups=mesh['gx'=16,'gy'=64] {'gx'}, dimensions={0} | all-to-all | bytes 2097152 | tf_op jit(solution)/shard_map/all_to_all | solution.py:532
  23.3 35.1 %all-to-all-start.1 = ((f32[64,1,512]{2,1,0:T(1,128)}), f32[64,1,512]{2,1,0:T(1,128)S(1)}, u32[]{:S(2)}, u32[]{:S(2)}) async-start(f32[64,1,512]{2,1,0:T(1,128)} %get-tuple-element.38), calls=%async_computation.1 | async-start | bytes 262144 | tf_op jit(solution)/shard_map/all_to_all | solution.py:535
  60.1 2.3 %collective-permute-done.yl_ref = f32[52,1,168]{2,1,0:T(1,128)S(1)} collective-permute-done((f32[52,1,168]{2,1,0:T(1,128)S(1)}, f32[52,1,168]{2,1,0:T(1,128)S(1)}, u32[]{:S(2)}, u32[]{:S(2)}) %collective-permute-start) | collective-permute-done | bytes 34976 | tf_op jit(solution)/shard_map/ppermute | solution.py:506
  62.4 7.3 %collective-permute-done.1.yh_ref = f32[52,2,168]{2,1,0:T(2,128)S(1)} collective-permute-done((f32[52,2,168]{2,1,0:T(2,128)S(1)}, f32[52,2,168]{2,1,0:T(2,128)S(1)}, u32[]{:S(2)}, u32[]{:S(2)}) %collective-permute-start.1) | collective-permute-done | bytes 69920 | tf_op jit(solution)/shard_map/ppermute | solution.py:506
  70.4 5.4 %shard_map.232 = (f32[36,16,168]{2,1,0:T(8,128)S(1)}, f32[36,2,168]{2,1,0:T(2,128)S(1)}, f32[36,2,168]{2,1,0:T(2,128)S(1)}) custom-call(f32[52,8,168]{2,1,0:T(8,128)S(1)} %get-tuple-element.40.bx_ref, f32[52,1,168]{2,1,0:T(1,128)S(1)} %collective-permute-done.yl_ref, f32[52,2,168]{2,1,0:T(2,128)S(1)} %collective-permute-done.1.yh_ref, ...), custom_call_target="tpu_custom_call" | custom-call | flops 77414400 | bytes 1421760 | tf_op jit(solution)/shard_map/pallas_call | solution.py:162
  77.3 2.7 %collective-permute-done.3.yh_ref = f32[36,2,168]{2,1,0:T(2,128)S(1)} collective-permute-done((f32[36,2,168]{2,1,0:T(2,128)S(1)}, f32[36,2,168]{2,1,0:T(2,128)S(1)}, u32[]{:S(2)}, u32[]{:S(2)}) %collective-permute-start.3) | collective-permute-done | bytes 48416 | tf_op jit(solution)/shard_map/ppermute | solution.py:506
  80.1 1.8 shard_map.233
  81.9 7.1 %all-to-all-done.1.refs_0_ = f32[64,1,512]{2,1,0:T(1,128)S(1)} async-done(((f32[64,1,512]{2,1,0:T(1,128)}), f32[64,1,512]{2,1,0:T(1,128)S(1)}, u32[]{:S(2)}, u32[]{:S(2)}) %all-to-all-start.1) | async-done | bytes 131104 | tf_op jit(solution)/shard_map/all_to_all | solution.py:535
  89.2 9.9 %all_to_all.31.refs_0_ = f32[16,8,128]{2,1,0:T(8,128)S(1)} all-to-all(f32[16,8,128]{2,1,0:T(8,128)S(1)} %shard_map.234), channel_id=1, replica_groups=mesh['gx'=16,'gy'=64] {'gx'}, dimensions={0} | all-to-all | bytes 131072 | tf_op jit(solution)/shard_map/all_to_all | solution.py:532
  100.1 19.4 %all-to-all-start.3 = ((f32[64,1,640]{2,1,0:T(1,128)}), f32[64,1,640]{2,1,0:T(1,128)S(1)}, u32[]{:S(2)}, u32[]{:S(2)}) async-start(f32[64,1,640]{2,1,0:T(1,128)} %get-tuple-element.50), calls=%async_computation.3 | async-start | bytes 327680 | tf_op jit(solution)/shard_map/all_to_all | solution.py:535
  119.5 2.5 %shard_map.236 = (f32[8,8,168]{2,1,0:T(8,128)S(1)}, f32[24,8,168]{2,1,0:T(8,128)S(1)}, f32[24,2,168]{2,1,0:T(2,128)S(1)}, f32[24,2,168]{2,1,0:T(2,128)S(1)}) custom-call(s32[2]{0:T(128)S(1)} %copy-done.17, f32[36,8,168]{2,1,0:T(8,128)S(1)} %get-tuple-element.51.u_ref, f32[1,128]{1,0:T(1,128)S(1)} %get-tuple-element.52.x_ref.refs_2_, ...), custom_call_target="tpu_custom_call" | custom-call | flops 77414400 | bytes 941320 | tf_op jit(solution)/shard_map/pallas_call | solution.py:162
  122.0 1.6 collective-permute-start.4
  123.7 4.7 %collective-permute-done.4.yl_ref = f32[24,2,168]{2,1,0:T(2,128)S(1)} collective-permute-done((f32[24,2,168]{2,1,0:T(2,128)S(1)}, f32[24,2,168]{2,1,0:T(2,128)S(1)}, u32[]{:S(2)}, u32[]{:S(2)}) %collective-permute-start.4) | collective-permute-done | bytes 32288 | tf_op jit(solution)/shard_map/ppermute | solution.py:506
  128.4 3.6 %collective-permute-done.5.yh_ref = f32[24,2,168]{2,1,0:T(2,128)S(1)} collective-permute-done((f32[24,2,168]{2,1,0:T(2,128)S(1)}, f32[24,2,168]{2,1,0:T(2,128)S(1)}, u32[]{:S(2)}, u32[]{:S(2)}) %collective-permute-start.5) | collective-permute-done | bytes 32288 | tf_op jit(solution)/shard_map/ppermute | solution.py:506
  132.0 2.6 %shard_map.237 = (f32[8,8,168]{2,1,0:T(8,128)S(1)}, f32[8,16,168]{2,1,0:T(8,128)S(1)}, f32[8,2,168]{2,1,0:T(2,128)S(1)}, f32[8,2,168]{2,1,0:T(2,128)S(1)}) custom-call(f32[24,8,168]{2,1,0:T(8,128)S(1)} %get-tuple-element.53.qx_ref, f32[24,2,168]{2,1,0:T(2,128)S(1)} %collective-permute-done.4.yl_ref, f32[24,2,168]{2,1,0:T(2,128)S(1)} %collective-permute-done.5.yh_ref, ...), custom_call_target="tpu_custom_call" | custom-call | flops 77414400 | bytes 897600 | tf_op jit(solution)/shard_map/pallas_call | solution.py:162
  134.6 1.9 collective-permute-start.7
  139.1 13.6 %all-to-all-done.3.refs_1_ = f32[64,1,640]{2,1,0:T(1,128)S(1)} async-done(((f32[64,1,640]{2,1,0:T(1,128)}), f32[64,1,640]{2,1,0:T(1,128)S(1)}, u32[]{:S(2)}, u32[]{:S(2)}) %all-to-all-start.3) | async-done | bytes 163872 | tf_op jit(solution)/shard_map/all_to_all | solution.py:535
  153.7 9.5 %all_to_all.32.refs_0_ = f32[16,8,128]{2,1,0:T(8,128)S(1)} all-to-all(f32[16,8,128]{2,1,0:T(8,128)S(1)} %get-tuple-element.64), channel_id=1, replica_groups=mesh['gx'=16,'gy'=64] {'gx'}, dimensions={0} | all-to-all | bytes 131072 | tf_op jit(solution)/shard_map/all_to_all | solution.py:532
  164.1 14.6 %all-to-all-start.5 = ((f32[64,1,128]{2,1,0:T(1,128)}), f32[64,1,128]{2,1,0:T(1,128)S(1)}, u32[]{:S(2)}, u32[]{:S(2)}) async-start(f32[64,1,128]{2,1,0:T(1,128)} %get-tuple-element.66), calls=%async_computation.5 | async-start | bytes 65536 | tf_op jit(solution)/shard_map/all_to_all | solution.py:535
  178.7 2.2 %collective-permute-start.8 = (f32[1,8,168]{2,1,0:T(8,128)S(1)}, f32[1,8,168]{2,1,0:T(8,128)S(1)}, u32[]{:S(2)}, u32[]{:S(2)}) collective-permute-start(f32[1,8,168]{2,1,0:T(8,128)S(1)} %get-tuple-element.69), channel_id=1, source_target_pairs={{0,64},{64,128},{128,192},{192,256},{256,320},{320,384},{384,448},... | collective-permute-start | bytes 16136 | tf_op jit(solution)/shard_map/ppermute | solution.py:506
  180.9 5.8 %collective-permute-done.8.side_ref = f32[1,8,168]{2,1,0:T(8,128)S(1)} collective-permute-done((f32[1,8,168]{2,1,0:T(8,128)S(1)}, f32[1,8,168]{2,1,0:T(8,128)S(1)}, u32[]{:S(2)}, u32[]{:S(2)}) %collective-permute-start.8) | collective-permute-done | bytes 5408 | tf_op jit(solution)/shard_map/ppermute | solution.py:506
  186.7 1.6 shard_map.241
  188.3 2.5 %collective-permute-start.9 = (f32[7,1,168]{2,1,0:T(1,128)S(1)}, f32[7,1,168]{2,1,0:T(1,128)S(1)}, u32[]{:S(2)}, u32[]{:S(2)}) collective-permute-start(f32[7,1,168]{2,1,0:T(1,128)S(1)} %get-tuple-element.73), channel_id=1, source_target_pairs={{0,1},{1,2},{2,3},{3,4},{4,5},{5,6},{6,7},{7,8},{8,9},{9,10},{10,1... | collective-permute-start | bytes 14120 | tf_op jit(solution)/shard_map/ppermute | solution.py:506
  191.6 9.4 %all-to-all-done.5.sums_ref = f32[64,1,128]{2,1,0:T(1,128)S(1)} async-done(((f32[64,1,128]{2,1,0:T(1,128)}), f32[64,1,128]{2,1,0:T(1,128)S(1)}, u32[]{:S(2)}, u32[]{:S(2)}) %all-to-all-start.5) | async-done | bytes 32800 | tf_op jit(solution)/shard_map/all_to_all | solution.py:535
  (65 shorter events, 14.5 us)
Async XLA Ops:
  2.5 19.3 %copy-start.3 = (f32[128,128]{1,0:T(8,128)S(1)}, f32[128,128]{1,0:T(8,128)}, u32[]{:S(2)}) copy-start(f32[128,128]{1,0:T(8,128)} %constant.63.clone.refs_2_.refs_3_.refs_4_) | copy-start | bytes 196612
  2.5 19.3 %copy-start.17 = (s32[2]{0:T(128)S(1)}, s32[2]{0:T(128)}, u32[]{:S(2)}) copy-start(s32[2]{0:T(128)} %pad_add_fusion.refs_0_.idx_ref) | copy-start | bytes 28
  21.8 47.9 %copy-start.5 = (f32[168,240]{1,0:T(8,128)S(1)}, f32[168,240]{1,0:T(8,128)}, u32[]{:S(2)}) copy-start(f32[168,240]{1,0:T(8,128)} %constant.48.clone.refs_5_) | copy-start | bytes 483844
  21.8 47.9 %copy-start.6 = (f32[160,160]{1,0:T(8,128)S(1)}, f32[160,160]{1,0:T(8,128)}, u32[]{:S(2)}) copy-start(f32[160,160]{1,0:T(8,128)} %constant.47.clone.refs_4_) | copy-start | bytes 307204
  21.8 47.9 %copy-start.7 = (f32[160,160]{1,0:T(8,128)S(1)}, f32[160,160]{1,0:T(8,128)}, u32[]{:S(2)}) copy-start(f32[160,160]{1,0:T(8,128)} %constant.46.clone.refs_3_) | copy-start | bytes 307204
  21.8 47.9 %copy-start.15 = (f32[160,1]{1,0:T(8,128)S(1)}, f32[160,1]{1,0:T(8,128)}, u32[]{:S(2)}) copy-start(f32[160,1]{1,0:T(8,128)} %constant.50.clone.refs_1_) | copy-start | bytes 1924
  23.3 46.4 %copy-start.4 = (f32[240,168]{1,0:T(8,128)S(1)}, f32[240,168]{1,0:T(8,128)}, u32[]{:S(2)}) copy-start(f32[240,168]{1,0:T(8,128)} %constant.49.clone.refs_6_) | copy-start | bytes 483844
  23.3 46.4 %copy-start.16 = (f32[24,240]{1,0:T(8,128)S(1)}, f32[24,240]{1,0:T(8,128)}, u32[]{:S(2)}) copy-start(f32[24,240]{1,0:T(8,128)} %constant.52.clone.refs_0_) | copy-start | bytes 69124
  23.3 65.7 %all-to-all-start.1 = ((f32[64,1,512]{2,1,0:T(1,128)}), f32[64,1,512]{2,1,0:T(1,128)S(1)}, u32[]{:S(2)}, u32[]{:S(2)}) async-start(f32[64,1,512]{2,1,0:T(1,128)} %get-tuple-element.38), calls=%async_computation.1 | async-start | bytes 262144 | tf_op jit(solution)/shard_map/all_to_all | solution.py:535
  58.3 11.3 %collective-permute-start.1 = (f32[52,2,168]{2,1,0:T(2,128)S(1)}, f32[52,2,168]{2,1,0:T(2,128)S(1)}, u32[]{:S(2)}, u32[]{:S(2)}) collective-permute-start(f32[52,2,168]{2,1,0:T(2,128)S(1)} %get-tuple-element.42), channel_id=1, source_target_pairs={{0,63},{1,0},{2,1},{3,2},{4,3},{5,4},{6,5},{7,6},{8,7},{9,8},{10,9... | collective-permute-start | bytes 209672 | tf_op jit(solution)/shard_map/ppermute | solution.py:506
  58.8 3.5 %collective-permute-start = (f32[52,1,168]{2,1,0:T(1,128)S(1)}, f32[52,1,168]{2,1,0:T(1,128)S(1)}, u32[]{:S(2)}, u32[]{:S(2)}) collective-permute-start(f32[52,1,168]{2,1,0:T(1,128)S(1)} %get-tuple-element.41), channel_id=1, source_target_pairs={{0,1},{1,2},{2,3},{3,4},{4,5},{5,6},{6,7},{7,8},{8,9},{9,10},{10,1... | collective-permute-start | bytes 104840 | tf_op jit(solution)/shard_map/ppermute | solution.py:506
  70.4 9.7 %copy-start.10 = (f32[64,64]{1,0:T(8,128)S(1)}, f32[64,64]{1,0:T(8,128)}, u32[]{:S(2)}) copy-start(f32[64,64]{1,0:T(8,128)} %constant.57.clone.refs_5_) | copy-start | bytes 49156
  75.9 1.4 collective-permute-start.2
  75.9 4.1 %collective-permute-start.3 = (f32[36,2,168]{2,1,0:T(2,128)S(1)}, f32[36,2,168]{2,1,0:T(2,128)S(1)}, u32[]{:S(2)}, u32[]{:S(2)}) collective-permute-start(f32[36,2,168]{2,1,0:T(2,128)S(1)} %get-tuple-element.47), channel_id=1, source_target_pairs={{0,63},{1,0},{2,1},{3,2},{4,3},{5,4},{6,5},{7,6},{8,7},{9,8},{10,9... | collective-permute-start | bytes 145160 | tf_op jit(solution)/shard_map/ppermute | solution.py:506
  100.1 19.4 %copy-start.8 = (f32[128,168]{1,0:T(8,128)S(1)}, f32[128,168]{1,0:T(8,128)}, u32[]{:S(2)}) copy-start(f32[128,168]{1,0:T(8,128)} %constant.64.clone.zl_ref) | copy-start | bytes 258052
  100.1 52.6 %all-to-all-start.3 = ((f32[64,1,640]{2,1,0:T(1,128)}), f32[64,1,640]{2,1,0:T(1,128)S(1)}, u32[]{:S(2)}, u32[]{:S(2)}) async-start(f32[64,1,640]{2,1,0:T(1,128)} %get-tuple-element.50), calls=%async_computation.3 | async-start | bytes 327680 | tf_op jit(solution)/shard_map/all_to_all | solution.py:535
  122.0 6.3 %collective-permute-start.4 = (f32[24,2,168]{2,1,0:T(2,128)S(1)}, f32[24,2,168]{2,1,0:T(2,128)S(1)}, u32[]{:S(2)}, u32[]{:S(2)}) collective-permute-start(f32[24,2,168]{2,1,0:T(2,128)S(1)} %get-tuple-element.54), channel_id=1, source_target_pairs={{0,1},{1,2},{2,3},{3,4},{4,5},{5,6},{6,7},{7,8},{8,9},{9,10},{10,1... | collective-permute-start | bytes 96776 | tf_op jit(solution)/shard_map/ppermute | solution.py:506
  123.7 8.3 %collective-permute-start.5 = (f32[24,2,168]{2,1,0:T(2,128)S(1)}, f32[24,2,168]{2,1,0:T(2,128)S(1)}, u32[]{:S(2)}, u32[]{:S(2)}) collective-permute-start(f32[24,2,168]{2,1,0:T(2,128)S(1)} %get-tuple-element.55), channel_id=1, source_target_pairs={{0,63},{1,0},{2,1},{3,2},{4,3},{5,4},{6,5},{7,6},{8,7},{9,8},{10,9... | collective-permute-start | bytes 96776 | tf_op jit(solution)/shard_map/ppermute | solution.py:506
  134.6 2.6 %collective-permute-start.6 = (f32[8,2,168]{2,1,0:T(2,128)S(1)}, f32[8,2,168]{2,1,0:T(2,128)S(1)}, u32[]{:S(2)}, u32[]{:S(2)}) collective-permute-start(f32[8,2,168]{2,1,0:T(2,128)S(1)} %get-tuple-element.60), channel_id=1, source_target_pairs={{0,1},{1,2},{2,3},{3,4},{4,5},{5,6},{6,7},{7,8},{8,9},{9,10},{10,1... | collective-permute-start | bytes 32264 | tf_op jit(solution)/shard_map/ppermute | solution.py:506
  134.6 3.5 %collective-permute-start.7 = (f32[8,2,168]{2,1,0:T(2,128)S(1)}, f32[8,2,168]{2,1,0:T(2,128)S(1)}, u32[]{:S(2)}, u32[]{:S(2)}) collective-permute-start(f32[8,2,168]{2,1,0:T(2,128)S(1)} %get-tuple-element.61), channel_id=1, source_target_pairs={{0,63},{1,0},{2,1},{3,2},{4,3},{5,4},{6,5},{7,6},{8,7},{9,8},{10,9... | collective-permute-start | bytes 32264 | tf_op jit(solution)/shard_map/ppermute | solution.py:506
  164.1 22.6 %copy-start.21 = (f32[8,1]{1,0:T(8,128)S(1)}, f32[8,1]{1,0:T(8,128)}, u32[]{:S(2)}) copy-start(f32[8,1]{1,0:T(8,128)} %constant.61.clone.face_ref) | copy-start | bytes 100
  164.1 36.9 %all-to-all-start.5 = ((f32[64,1,128]{2,1,0:T(1,128)}), f32[64,1,128]{2,1,0:T(1,128)S(1)}, u32[]{:S(2)}, u32[]{:S(2)}) async-start(f32[64,1,128]{2,1,0:T(1,128)} %get-tuple-element.66), calls=%async_computation.5 | async-start | bytes 65536 | tf_op jit(solution)/shard_map/all_to_all | solution.py:535
  178.7 8.0 %collective-permute-start.8 = (f32[1,8,168]{2,1,0:T(8,128)S(1)}, f32[1,8,168]{2,1,0:T(8,128)S(1)}, u32[]{:S(2)}, u32[]{:S(2)}) collective-permute-start(f32[1,8,168]{2,1,0:T(8,128)S(1)} %get-tuple-element.69), channel_id=1, source_target_pairs={{0,64},{64,128},{128,192},{192,256},{256,320},{320,384},{384,448},... | collective-permute-start | bytes 16136 | tf_op jit(solution)/shard_map/ppermute | solution.py:506
  188.3 3.3 %collective-permute-start.9 = (f32[7,1,168]{2,1,0:T(1,128)S(1)}, f32[7,1,168]{2,1,0:T(1,128)S(1)}, u32[]{:S(2)}, u32[]{:S(2)}) collective-permute-start(f32[7,1,168]{2,1,0:T(1,128)S(1)} %get-tuple-element.73), channel_id=1, source_target_pairs={{0,1},{1,2},{2,3},{3,4},{4,5},{5,6},{6,7},{7,8},{8,9},{9,10},{10,1... | collective-permute-start | bytes 14120 | tf_op jit(solution)/shard_map/ppermute | solution.py:506
  (12 other events, 90.7 us)

commit v5 on v4

--- a/solution.py
+++ b/solution.py
@@ -264,7 +264,9 @@
     rows = factor.shape[0]
     rc_col = as_col(rc, eye_ref[:rows])
     part = jnp.sum(rc_col * factor, axis=0, keepdims=True)
-    spread(out_ref, part)
+    half = width // 2
+    core = lax.broadcasted_iota(jnp.int32, out_ref.shape, 0) & 1
+    out_ref[...] = jnp.where(core == 0, part[:, :half][None], part[:, half:][None])
     count = xl_ref.shape[0]
     nz, ez = bx_ref.shape[2], k_ref.shape[1]
     base = width + 2 * LANES
@@ -283,11 +285,17 @@
     lo_ref[...] = bx_ref[:, 0:2]
 
 
-def coarse_out_kernel(width, sums_ref, xl_ref, eye_ref, h_ref, out_ref):
+def join_halves(width, idx_ref, mine_ref, other_ref):
+    half = width // 2
+    mine, other = mine_ref[:, :half], other_ref[:, :half]
+    even = idx_ref[2] == 0
+    return jnp.concatenate([jnp.where(even, mine, other), jnp.where(even, other, mine)], axis=1)
+
+
+def coarse_out_kernel(width, idx_ref, mine_ref, other_ref, xl_ref, eye_ref, h_ref, out_ref):
     factor, _ = split_group(xl_ref, width)
     rows = factor.shape[0]
-    sums = jnp.sum(sums_ref[...], axis=0)
-    part = jnp.sum(factor * sums[:, :width], axis=1, keepdims=True)
+    part = jnp.sum(factor * join_halves(width, idx_ref, mine_ref, other_ref), axis=1, keepdims=True)
     x_part = as_row(part, eye_ref[:rows])
     spot = lax.broadcasted_iota(jnp.int32, (8, LANES), 0)
     tile = jnp.where(spot == 0, x_part, h_ref[...])
@@ -306,18 +314,26 @@
     part = jnp.sum(rc1_col * factor, axis=0, keepdims=True)
     rho = lane_get(scal, 0) + total_row(rc * x0)
     den = lane_get(scal, 1) + total_row(x0 * (h + rc1))
-    spread(out_ref, jnp.concatenate([part, lane_put([rho, den])], axis=1))
+    scal = lane_put([rho, den])
+    half = width // 2
+    core = lax.broadcasted_iota(jnp.int32, out_ref.shape, 0) & 1
+    first = jnp.concatenate([part[:, :half], scal], axis=1)
+    second = jnp.concatenate([part[:, half:], scal], axis=1)
+    out_ref[...] = jnp.where(core == 0, first[None], second[None])
     x_ref[...] = x0
 
 
-def pair_kernel(width, idx_ref, sums_ref, xl_ref, eye_ref, b_ref, q_ref, u_ref, au_ref, s_ref, as_ref, inner_ref, zct_ref,
+def sum_kernel(sums_ref, out_ref):
+    out_ref[...] = jnp.sum(sums_ref[...], axis=0)
+
+
+def pair_kernel(width, idx_ref, mine_ref, other_ref, xl_ref, eye_ref, b_ref, q_ref, u_ref, au_ref, s_ref, as_ref, inner_ref, zct_ref,
                 out_ref, scal_ref, r_ref):
     factor, _ = split_group(xl_ref, width)
     rows = factor.shape[0]
-    sums = jnp.sum(sums_ref[...], axis=0)
-    part = jnp.sum(factor * sums[:, :width], axis=1, keepdims=True)
+    part = jnp.sum(factor * join_halves(width, idx_ref, mine_ref, other_ref), axis=1, keepdims=True)
     x_part = as_row(part, eye_ref[:rows])
-    scal = sums[:, width:]
+    scal = mine_ref[:, width // 2 :]
     rho, den = lane_get(scal, 0), lane_get(scal, 1)
     step = rho / den
     sel = lane_sel(idx_ref[0])
@@ -516,7 +532,7 @@
     k = stiff_coef.reshape(1, ez)
     m = mass_coef.reshape(1, ez)
     b = right_side
-    idx = jnp.stack([lax.axis_index("gx"), jnp.int32(n_gx)])
+    idx = jnp.stack([lax.axis_index("gx"), jnp.int32(n_gx), lax.axis_index("gy") & 1])
     solve_tab = [tab[name] for name in SOLVE]
     apply_tab = [tab[name] for name in APPLY]
     inner, zct, zl, eye = (tab[name] for name in ("inner", "zct", "zl", "eye"))
@@ -533,6 +549,10 @@
 
     def swap_gy(value):
         return lax.all_to_all(value, "gy", 0, 0)
+
+    def halves(sums):
+        (mine,) = run(sum_kernel, [sums.shape[1:]], sums)
+        return mine, lax.ppermute(mine, "gy", [(i, i ^ 1) for i in range(n_gy)])
 
     group = (n_gx, c_dev, LANES)
     aux = -(-(2 * LANES + 7 * nz) // LANES) * LANES
@@ -540,7 +560,7 @@
                  idx, b, k, m, coarse_factor, scratch=[(8, aux)], limit=56)
     xl = swap_gx(pay)
 
-    outs = [(n_gy, 1, width), (52, 8, nz), (52, 1, nz), (52, 2, nz), (8, ez), (8, ez),
+    outs = [(n_gy, 1, width // 2), (52, 8, nz), (52, 1, nz), (52, 2, nz), (8, ez), (8, ez),
             (n_gx, c_dev, width + LANES), (1, LANES)]
     pay, bx, hi, lo, ks, ms, members, rc = run(kernel(coarse_in_kernel, width), outs, idx, xl, eye, free=(0,))
     y_low, y_high = shift(hi, "gy", 1), shift(lo, "gy", -1)
@@ -554,9 +574,10 @@
     wide_u, u, au, h = run(apply_u_kernel, [(36, 8, nz), cube, cube, (8, LANES)], idx, b, y, y_low, y_high, k, m, inner, zct, *apply_tab,
                           free=(1, 2))
 
-    (pay,) = run(kernel(coarse_out_kernel, width), [group], sums, members, eye, h)
+    mine, other = halves(sums)
+    (pay,) = run(kernel(coarse_out_kernel, width), [group], idx, mine, other, members, eye, h)
     got = swap_gx(pay)
-    pay, x0 = run(kernel(coarse_mid_kernel, width), [(n_gy, 1, width + LANES), (1, LANES)], got, members, rc, eye, free=(0,))
+    pay, x0 = run(kernel(coarse_mid_kernel, width), [(n_gy, 1, width // 2 + LANES), (1, LANES)], got, members, rc, eye, free=(0,))
     sums = swap_gy(pay)
 
     p, qx, hi, lo = run(apply_p_kernel, [cube, (24, 8, nz), (24, 2, nz), (24, 2, nz)], idx, wide_u, x0, ks, ms, inner, zl, *apply_tab,
@@ -568,7 +589,8 @@
     s, a_s, hi = run(apply_s_kernel, [cube, cube, (1, 8, nz)], y, y_low, y_high, k, m, *apply_tab)
     side = shift(hi, "gx", 1)
 
-    pay, scal, resid = run(kernel(pair_kernel, width), [group, (1, LANES), cube], idx, sums, members, eye, b, q, u, au, s, a_s, inner, zct)
+    mine, other = halves(sums)
+    pay, scal, resid = run(kernel(pair_kernel, width), [group, (1, LANES), cube], idx, mine, other, members, eye, b, q, u, au, s, a_s, inner, zct)
     got = swap_gx(pay)
     pay, x1 = run(kernel(last_in_kernel, width), [(n_gy, 1, LANES), (1, LANES)], got, members, x0, scal, eye, free=(0,))
     sums = swap_gy(pay)

time: 202 us -> 192 us (0.950)
  waiting for transfers between devices: 59.8 us -> 51.1 us
    ppermute x10, waiting for transfers between devices: 29.7 us -> 16.2 us  [shift(): lax.ppermute(value, axis, [(i, (i + step) % count) for i in range(count)])]
    all_to_all x3, starting transfers between devices: 69.1 us -> 59.1 us  [swap_gy(): return lax.all_to_all(value, 'gy', 0, 0)]
    ppermute x0 -> x2, starting transfers between devices: none -> 7.37 us  [halves(): return (mine, lax.ppermute(mine, 'gy', [(i, i ^ 1) for i in range(n_gy)]))]
    all_to_all x3, waiting for transfers between devices: 30.1 us -> 34.8 us  [swap_gy(): return lax.all_to_all(value, 'gy', 0, 0)]
    pallas_call x13 -> x15, Pallas kernels: 21.6 us -> 22.1 us  [run(): pl.pallas_call(kernel, out_shape=[(jax.ShapeDtypeStruct if i in free else...]
  transfers between devices with their start and end apart: 13 -> 15, of which waited for: 13 -> 9; matrix products, arithmetic and copies ran while one was open for 0% -> 0% of each run, Pallas kernels for 7% -> 8%
where the time goes in v5:
time: 192 us
  starting transfers between devices  77.7 us (40%)
  waiting for transfers between devices  51.1 us (27%)
  blocking collectives  38.6 us (20%)
  Pallas kernels  22.1 us (12%)
    all_to_all x3, starting transfers between devices, swap_gy(): return lax.all_to_all(value, 'gy', 0, 0)  59.1 us
    all_to_all x3, blocking collectives, swap_gx(): return lax.all_to_all(value, 'gx', 0, 0)  38.6 us
    all_to_all x3, waiting for transfers between devices, swap_gy(): return lax.all_to_all(value, 'gy', 0, 0)  34.8 us
    pallas_call x15, Pallas kernels, run(): pl.pallas_call(kernel, out_shape=[(jax.ShapeDtypeStruct if i in free else...  22.1 us
    ppermute x10, waiting for transfers between devices, shift(): lax.ppermute(value, axis, [(i, (i + step) % count) for i in range(count)])  16.2 us
    ppermute x10, starting transfers between devices, shift(): lax.ppermute(value, axis, [(i, (i + step) % count) for i in range(count)])  11.2 us
    ppermute x2, starting transfers between devices, halves(): return (mine, lax.ppermute(mine, 'gy', [(i, i ^ 1) for i in range(n_gy)]))  7.37 us
  transfers between devices with their start and end apart: 15, of which 9 were waited for; matrix products, arithmetic and copies ran while one was open for 0% of the time, Pallas kernels for 8%

profile of v5, /device:TPU:1, one launch (start us, length us, event | category | flops | bytes accessed | tf_op | source)
XLA Modules:
  0.0 191.9 jit_solution(11988954317688630028)
XLA Ops:
  2.6 19.3 %all_to_all.30.refs_1_ = f32[16,8,2048]{2,1,0:T(8,128)S(1)} all-to-all(f32[16,8,2048]{2,1,0:T(8,128)S(1)} %shard_map.230), channel_id=1, replica_groups=mesh['gx'=16,'gy'=64] {'gx'}, dimensions={0} | all-to-all | bytes 2097152 | tf_op jit(solution)/shard_map/all_to_all | solution.py:548
  23.3 35.1 %all-to-all-start.1 = ((f32[64,1,256]{2,1,0:T(1,128)}), f32[64,1,256]{2,1,0:T(1,128)S(1)}, u32[]{:S(2)}, u32[]{:S(2)}) async-start(f32[64,1,256]{2,1,0:T(1,128)} %get-tuple-element.38), calls=%async_computation.1 | async-start | bytes 131072 | tf_op jit(solution)/shard_map/all_to_all | solution.py:551
  60.1 2.3 %collective-permute-done.1.yl_ref = f32[52,1,168]{2,1,0:T(1,128)S(1)} collective-permute-done((f32[52,1,168]{2,1,0:T(1,128)S(1)}, f32[52,1,168]{2,1,0:T(1,128)S(1)}, u32[]{:S(2)}, u32[]{:S(2)}) %collective-permute-start.1) | collective-permute-done | bytes 34976 | tf_op jit(solution)/shard_map/ppermute | solution.py:522
  62.4 1.7 collective-permute-done.2.yh_ref
  64.8 5.5 %shard_map.233 = (f32[36,16,168]{2,1,0:T(8,128)S(1)}, f32[36,2,168]{2,1,0:T(2,128)S(1)}, f32[36,2,168]{2,1,0:T(2,128)S(1)}) custom-call(f32[52,8,168]{2,1,0:T(8,128)S(1)} %get-tuple-element.40.bx_ref, f32[52,1,168]{2,1,0:T(1,128)S(1)} %collective-permute-done.1.yl_ref, f32[52,2,168]{2,1,0:T(2,128)S(1)} %collective-permute-done.2.yh_ref, ...), custom_call_target="tpu_custom_call" | custom-call | flops 77414400 | bytes 1421760 | tf_op jit(solution)/shard_map/pallas_call | solution.py:162
  70.4 2.6 %collective-permute-start.4 = (f32[36,2,168]{2,1,0:T(2,128)S(1)}, f32[36,2,168]{2,1,0:T(2,128)S(1)}, u32[]{:S(2)}, u32[]{:S(2)}) collective-permute-start(f32[36,2,168]{2,1,0:T(2,128)S(1)} %get-tuple-element.47), channel_id=1, source_target_pairs={{0,63},{1,0},{2,1},{3,2},{4,3},{5,4},{6,5},{7,6},{8,7},{9,8},{10,9... | collective-permute-start | bytes 145160 | tf_op jit(solution)/shard_map/ppermute | solution.py:522
  73.0 10.5 %all-to-all-done.1.sums_ref = f32[64,1,256]{2,1,0:T(1,128)S(1)} async-done(((f32[64,1,256]{2,1,0:T(1,128)}), f32[64,1,256]{2,1,0:T(1,128)S(1)}, u32[]{:S(2)}, u32[]{:S(2)}) %all-to-all-start.1) | async-done | bytes 65568 | tf_op jit(solution)/shard_map/all_to_all | solution.py:551
  83.5 3.8 %collective-permute-start = (f32[1,256]{1,0:T(1,128)S(1)}, f32[1,256]{1,0:T(1,128)S(1)}, u32[]{:S(2)}, u32[]{:S(2)}) collective-permute-start(f32[1,256]{1,0:T(1,128)S(1)} %shard_map.232.refs_1_), channel_id=1, source_target_pairs={{0,1},{1,0},{2,3},{3,2},{4,5},{5,4},{6,7},{7,6},{8,9},{9,8},{10,11... | collective-permute-start | bytes 3080 | tf_op jit(solution)/shard_map/ppermute | solution.py:555
  87.5 1.8 shard_map.234
  90.0 9.9 %all_to_all.31.refs_0_ = f32[16,8,128]{2,1,0:T(8,128)S(1)} all-to-all(f32[16,8,128]{2,1,0:T(8,128)S(1)} %shard_map.235), channel_id=1, replica_groups=mesh['gx'=16,'gy'=64] {'gx'}, dimensions={0} | all-to-all | bytes 131072 | tf_op jit(solution)/shard_map/all_to_all | solution.py:548
  100.8 13.7 %all-to-all-start.3 = ((f32[64,1,384]{2,1,0:T(1,128)}), f32[64,1,384]{2,1,0:T(1,128)S(1)}, u32[]{:S(2)}, u32[]{:S(2)}) async-start(f32[64,1,384]{2,1,0:T(1,128)} %get-tuple-element.50), calls=%async_computation.3 | async-start | bytes 196608 | tf_op jit(solution)/shard_map/all_to_all | solution.py:551
  114.5 2.5 %shard_map.238 = (f32[8,8,168]{2,1,0:T(8,128)S(1)}, f32[24,8,168]{2,1,0:T(8,128)S(1)}, f32[24,2,168]{2,1,0:T(2,128)S(1)}, f32[24,2,168]{2,1,0:T(2,128)S(1)}) custom-call(s32[3]{0:T(128)S(1)} %copy-done.17, f32[36,8,168]{2,1,0:T(8,128)S(1)} %get-tuple-element.51.u_ref, f32[1,128]{1,0:T(1,128)S(1)} %get-tuple-element.52.x_ref.refs_2_, ...), custom_call_target="tpu_custom_call" | custom-call | flops 77414400 | bytes 941324 | tf_op jit(solution)/shard_map/pallas_call | solution.py:162
  118.7 2.9 %collective-permute-done.6.yl_ref = f32[24,2,168]{2,1,0:T(2,128)S(1)} collective-permute-done((f32[24,2,168]{2,1,0:T(2,128)S(1)}, f32[24,2,168]{2,1,0:T(2,128)S(1)}, u32[]{:S(2)}, u32[]{:S(2)}) %collective-permute-start.6) | collective-permute-done | bytes 32288 | tf_op jit(solution)/shard_map/ppermute | solution.py:522
  121.5 2.8 %collective-permute-done.7.yh_ref = f32[24,2,168]{2,1,0:T(2,128)S(1)} collective-permute-done((f32[24,2,168]{2,1,0:T(2,128)S(1)}, f32[24,2,168]{2,1,0:T(2,128)S(1)}, u32[]{:S(2)}, u32[]{:S(2)}) %collective-permute-start.7) | collective-permute-done | bytes 32288 | tf_op jit(solution)/shard_map/ppermute | solution.py:522
  124.3 2.6 %shard_map.239 = (f32[8,8,168]{2,1,0:T(8,128)S(1)}, f32[8,16,168]{2,1,0:T(8,128)S(1)}, f32[8,2,168]{2,1,0:T(2,128)S(1)}, f32[8,2,168]{2,1,0:T(2,128)S(1)}) custom-call(f32[24,8,168]{2,1,0:T(8,128)S(1)} %get-tuple-element.53.qx_ref, f32[24,2,168]{2,1,0:T(2,128)S(1)} %collective-permute-done.6.yl_ref, f32[24,2,168]{2,1,0:T(2,128)S(1)} %collective-permute-done.7.yh_ref, ...), custom_call_target="tpu_custom_call" | custom-call | flops 77414400 | bytes 897600 | tf_op jit(solution)/shard_map/pallas_call | solution.py:162
  127.5 14.9 %all-to-all-done.3.sums_ref = f32[64,1,384]{2,1,0:T(1,128)S(1)} async-done(((f32[64,1,384]{2,1,0:T(1,128)}), f32[64,1,384]{2,1,0:T(1,128)S(1)}, u32[]{:S(2)}, u32[]{:S(2)}) %all-to-all-start.3) | async-done | bytes 98336 | tf_op jit(solution)/shard_map/all_to_all | solution.py:551
  142.5 3.5 %collective-permute-start.5 = (f32[1,384]{1,0:T(1,128)S(1)}, f32[1,384]{1,0:T(1,128)S(1)}, u32[]{:S(2)}, u32[]{:S(2)}) collective-permute-start(f32[1,384]{1,0:T(1,128)S(1)} %shard_map.237.refs_1_), channel_id=1, source_target_pairs={{0,1},{1,0},{2,3},{3,2},{4,5},{5,4},{6,7},{7,6},{8,9},{9,8},{10,11... | collective-permute-start | bytes 4616 | tf_op jit(solution)/shard_map/ppermute | solution.py:555
  147.9 9.5 %all_to_all.32.refs_0_ = f32[16,8,128]{2,1,0:T(8,128)S(1)} all-to-all(f32[16,8,128]{2,1,0:T(8,128)S(1)} %get-tuple-element.64), channel_id=1, replica_groups=mesh['gx'=16,'gy'=64] {'gx'}, dimensions={0} | all-to-all | bytes 131072 | tf_op jit(solution)/shard_map/all_to_all | solution.py:548
  158.3 10.3 %all-to-all-start.5 = ((f32[64,1,128]{2,1,0:T(1,128)}), f32[64,1,128]{2,1,0:T(1,128)S(1)}, u32[]{:S(2)}, u32[]{:S(2)}) async-start(f32[64,1,128]{2,1,0:T(1,128)} %get-tuple-element.66), calls=%async_computation.5 | async-start | bytes 65536 | tf_op jit(solution)/shard_map/all_to_all | solution.py:551
  168.7 2.2 %collective-permute-start.10 = (f32[1,8,168]{2,1,0:T(8,128)S(1)}, f32[1,8,168]{2,1,0:T(8,128)S(1)}, u32[]{:S(2)}, u32[]{:S(2)}) collective-permute-start(f32[1,8,168]{2,1,0:T(8,128)S(1)} %get-tuple-element.69), channel_id=1, source_target_pairs={{0,64},{64,128},{128,192},{192,256},{256,320},{320,384},{384,448},... | collective-permute-start | bytes 16136 | tf_op jit(solution)/shard_map/ppermute | solution.py:522
  170.9 5.8 %collective-permute-done.10.side_ref = f32[1,8,168]{2,1,0:T(8,128)S(1)} collective-permute-done((f32[1,8,168]{2,1,0:T(8,128)S(1)}, f32[1,8,168]{2,1,0:T(8,128)S(1)}, u32[]{:S(2)}, u32[]{:S(2)}) %collective-permute-start.10) | collective-permute-done | bytes 5408 | tf_op jit(solution)/shard_map/ppermute | solution.py:522
  176.7 1.6 shard_map.243
  178.3 2.5 %collective-permute-start.11 = (f32[7,1,168]{2,1,0:T(1,128)S(1)}, f32[7,1,168]{2,1,0:T(1,128)S(1)}, u32[]{:S(2)}, u32[]{:S(2)}) collective-permute-start(f32[7,1,168]{2,1,0:T(1,128)S(1)} %get-tuple-element.73), channel_id=1, source_target_pairs={{0,1},{1,2},{2,3},{3,4},{4,5},{5,6},{6,7},{7,8},{8,9},{9,10},{10,1... | collective-permute-start | bytes 14120 | tf_op jit(solution)/shard_map/ppermute | solution.py:522
  181.6 9.4 %all-to-all-done.5.sums_ref = f32[64,1,128]{2,1,0:T(1,128)S(1)} async-done(((f32[64,1,128]{2,1,0:T(1,128)}), f32[64,1,128]{2,1,0:T(1,128)S(1)}, u32[]{:S(2)}, u32[]{:S(2)}) %all-to-all-start.5) | async-done | bytes 32800 | tf_op jit(solution)/shard_map/all_to_all | solution.py:551
  (71 shorter events, 14.3 us)
Async XLA Ops:
  21.9 42.3 %copy-start.4 = (f32[240,168]{1,0:T(8,128)S(1)}, f32[240,168]{1,0:T(8,128)}, u32[]{:S(2)}) copy-start(f32[240,168]{1,0:T(8,128)} %constant.54.clone.refs_6_) | copy-start | bytes 483844
  21.9 42.3 %copy-start.5 = (f32[168,240]{1,0:T(8,128)S(1)}, f32[168,240]{1,0:T(8,128)}, u32[]{:S(2)}) copy-start(f32[168,240]{1,0:T(8,128)} %constant.53.clone.refs_5_) | copy-start | bytes 483844
  21.9 42.3 %copy-start.6 = (f32[160,160]{1,0:T(8,128)S(1)}, f32[160,160]{1,0:T(8,128)}, u32[]{:S(2)}) copy-start(f32[160,160]{1,0:T(8,128)} %constant.52.clone.refs_4_) | copy-start | bytes 307204
  21.9 42.2 %copy-start.7 = (f32[160,160]{1,0:T(8,128)S(1)}, f32[160,160]{1,0:T(8,128)}, u32[]{:S(2)}) copy-start(f32[160,160]{1,0:T(8,128)} %constant.51.clone.refs_3_) | copy-start | bytes 307204
  23.3 40.8 %copy-start.15 = (f32[160,1]{1,0:T(8,128)S(1)}, f32[160,1]{1,0:T(8,128)}, u32[]{:S(2)}) copy-start(f32[160,1]{1,0:T(8,128)} %constant.55.clone.refs_1_) | copy-start | bytes 1924
  23.3 40.9 %copy-start.16 = (f32[24,240]{1,0:T(8,128)S(1)}, f32[24,240]{1,0:T(8,128)}, u32[]{:S(2)}) copy-start(f32[24,240]{1,0:T(8,128)} %constant.57.clone.refs_0_) | copy-start | bytes 69124
  23.3 60.1 %all-to-all-start.1 = ((f32[64,1,256]{2,1,0:T(1,128)}), f32[64,1,256]{2,1,0:T(1,128)S(1)}, u32[]{:S(2)}, u32[]{:S(2)}) async-start(f32[64,1,256]{2,1,0:T(1,128)} %get-tuple-element.38), calls=%async_computation.1 | async-start | bytes 131072 | tf_op jit(solution)/shard_map/all_to_all | solution.py:551
  58.4 5.7 %collective-permute-start.2 = (f32[52,2,168]{2,1,0:T(2,128)S(1)}, f32[52,2,168]{2,1,0:T(2,128)S(1)}, u32[]{:S(2)}, u32[]{:S(2)}) collective-permute-start(f32[52,2,168]{2,1,0:T(2,128)S(1)} %get-tuple-element.42), channel_id=1, source_target_pairs={{0,63},{1,0},{2,1},{3,2},{4,3},{5,4},{6,5},{7,6},{8,7},{9,8},{10,9... | collective-permute-start | bytes 209672 | tf_op jit(solution)/shard_map/ppermute | solution.py:522
  58.8 3.5 %collective-permute-start.1 = (f32[52,1,168]{2,1,0:T(1,128)S(1)}, f32[52,1,168]{2,1,0:T(1,128)S(1)}, u32[]{:S(2)}, u32[]{:S(2)}) collective-permute-start(f32[52,1,168]{2,1,0:T(1,128)S(1)} %get-tuple-element.41), channel_id=1, source_target_pairs={{0,1},{1,2},{2,3},{3,4},{4,5},{5,6},{6,7},{7,8},{8,9},{9,10},{10,1... | collective-permute-start | bytes 104840 | tf_op jit(solution)/shard_map/ppermute | solution.py:522
  64.8 22.6 %copy-start.11 = (f32[64,1]{1,0:T(8,128)S(1)}, f32[64,1]{1,0:T(8,128)}, u32[]{:S(2)}) copy-start(f32[64,1]{1,0:T(8,128)} %constant.65.clone.inner_ref.refs_11_) | copy-start | bytes 772
  64.8 22.6 %copy-start.12 = (f32[7,7,168]{2,1,0:T(8,128)S(1)}, f32[7,7,168]{2,1,0:T(8,128)}, u32[]{:S(2)}) copy-start(f32[7,7,168]{2,1,0:T(8,128)} %refs_5_.7) | copy-start | bytes 98788
  64.8 22.6 %copy-start.14 = (f32[168,128]{1,0:T(8,128)S(1)}, f32[168,128]{1,0:T(8,128)}, u32[]{:S(2)}) copy-start(f32[168,128]{1,0:T(8,128)} %constant.67.clone.zct_ref.refs_12_) | copy-start | bytes 258052
  70.3 17.1 %collective-permute-start.3 = (f32[36,2,168]{2,1,0:T(2,128)S(1)}, f32[36,2,168]{2,1,0:T(2,128)S(1)}, u32[]{:S(2)}, u32[]{:S(2)}) collective-permute-start(f32[36,2,168]{2,1,0:T(2,128)S(1)} %get-tuple-element.46), channel_id=1, source_target_pairs={{0,1},{1,2},{2,3},{3,4},{4,5},{5,6},{6,7},{7,8},{8,9},{9,10},{10,1... | collective-permute-start | bytes 145160 | tf_op jit(solution)/shard_map/ppermute | solution.py:522
  70.4 17.0 %collective-permute-start.4 = (f32[36,2,168]{2,1,0:T(2,128)S(1)}, f32[36,2,168]{2,1,0:T(2,128)S(1)}, u32[]{:S(2)}, u32[]{:S(2)}) collective-permute-start(f32[36,2,168]{2,1,0:T(2,128)S(1)} %get-tuple-element.47), channel_id=1, source_target_pairs={{0,63},{1,0},{2,1},{3,2},{4,3},{5,4},{6,5},{7,6},{8,7},{9,8},{10,9... | collective-permute-start | bytes 145160 | tf_op jit(solution)/shard_map/ppermute | solution.py:522
  83.5 5.7 %collective-permute-start = (f32[1,256]{1,0:T(1,128)S(1)}, f32[1,256]{1,0:T(1,128)S(1)}, u32[]{:S(2)}, u32[]{:S(2)}) collective-permute-start(f32[1,256]{1,0:T(1,128)S(1)} %shard_map.232.refs_1_), channel_id=1, source_target_pairs={{0,1},{1,0},{2,3},{3,2},{4,5},{5,4},{6,7},{7,6},{8,9},{9,8},{10,11... | collective-permute-start | bytes 3080 | tf_op jit(solution)/shard_map/ppermute | solution.py:555
  100.8 41.6 %all-to-all-start.3 = ((f32[64,1,384]{2,1,0:T(1,128)}), f32[64,1,384]{2,1,0:T(1,128)S(1)}, u32[]{:S(2)}, u32[]{:S(2)}) async-start(f32[64,1,384]{2,1,0:T(1,128)} %get-tuple-element.50), calls=%async_computation.3 | async-start | bytes 196608 | tf_op jit(solution)/shard_map/all_to_all | solution.py:551
  117.0 4.5 %collective-permute-start.6 = (f32[24,2,168]{2,1,0:T(2,128)S(1)}, f32[24,2,168]{2,1,0:T(2,128)S(1)}, u32[]{:S(2)}, u32[]{:S(2)}) collective-permute-start(f32[24,2,168]{2,1,0:T(2,128)S(1)} %get-tuple-element.54), channel_id=1, source_target_pairs={{0,1},{1,2},{2,3},{3,4},{4,5},{5,6},{6,7},{7,8},{8,9},{9,10},{10,1... | collective-permute-start | bytes 96776 | tf_op jit(solution)/shard_map/ppermute | solution.py:522
  118.6 5.7 %collective-permute-start.7 = (f32[24,2,168]{2,1,0:T(2,128)S(1)}, f32[24,2,168]{2,1,0:T(2,128)S(1)}, u32[]{:S(2)}, u32[]{:S(2)}) collective-permute-start(f32[24,2,168]{2,1,0:T(2,128)S(1)} %get-tuple-element.55), channel_id=1, source_target_pairs={{0,63},{1,0},{2,1},{3,2},{4,3},{5,4},{6,5},{7,6},{8,7},{9,8},{10,9... | collective-permute-start | bytes 96776 | tf_op jit(solution)/shard_map/ppermute | solution.py:522
  126.9 19.1 %collective-permute-start.8 = (f32[8,2,168]{2,1,0:T(2,128)S(1)}, f32[8,2,168]{2,1,0:T(2,128)S(1)}, u32[]{:S(2)}, u32[]{:S(2)}) collective-permute-start(f32[8,2,168]{2,1,0:T(2,128)S(1)} %get-tuple-element.60), channel_id=1, source_target_pairs={{0,1},{1,2},{2,3},{3,4},{4,5},{5,6},{6,7},{7,8},{8,9},{9,10},{10,1... | collective-permute-start | bytes 32264 | tf_op jit(solution)/shard_map/ppermute | solution.py:522
  127.0 19.1 %collective-permute-start.9 = (f32[8,2,168]{2,1,0:T(2,128)S(1)}, f32[8,2,168]{2,1,0:T(2,128)S(1)}, u32[]{:S(2)}, u32[]{:S(2)}) collective-permute-start(f32[8,2,168]{2,1,0:T(2,128)S(1)} %get-tuple-element.61), channel_id=1, source_target_pairs={{0,63},{1,0},{2,1},{3,2},{4,3},{5,4},{6,5},{7,6},{8,7},{9,8},{10,9... | collective-permute-start | bytes 32264 | tf_op jit(solution)/shard_map/ppermute | solution.py:522
  142.5 4.5 %collective-permute-start.5 = (f32[1,384]{1,0:T(1,128)S(1)}, f32[1,384]{1,0:T(1,128)S(1)}, u32[]{:S(2)}, u32[]{:S(2)}) collective-permute-start(f32[1,384]{1,0:T(1,128)S(1)} %shard_map.237.refs_1_), channel_id=1, source_target_pairs={{0,1},{1,0},{2,3},{3,2},{4,5},{5,4},{6,7},{7,6},{8,9},{9,8},{10,11... | collective-permute-start | bytes 4616 | tf_op jit(solution)/shard_map/ppermute | solution.py:555
  158.3 32.7 %all-to-all-start.5 = ((f32[64,1,128]{2,1,0:T(1,128)}), f32[64,1,128]{2,1,0:T(1,128)S(1)}, u32[]{:S(2)}, u32[]{:S(2)}) async-start(f32[64,1,128]{2,1,0:T(1,128)} %get-tuple-element.66), calls=%async_computation.5 | async-start | bytes 65536 | tf_op jit(solution)/shard_map/all_to_all | solution.py:551
  168.7 8.0 %collective-permute-start.10 = (f32[1,8,168]{2,1,0:T(8,128)S(1)}, f32[1,8,168]{2,1,0:T(8,128)S(1)}, u32[]{:S(2)}, u32[]{:S(2)}) collective-permute-start(f32[1,8,168]{2,1,0:T(8,128)S(1)} %get-tuple-element.69), channel_id=1, source_target_pairs={{0,64},{64,128},{128,192},{192,256},{256,320},{320,384},{384,448},... | collective-permute-start | bytes 16136 | tf_op jit(solution)/shard_map/ppermute | solution.py:522
  178.3 3.3 %collective-permute-start.11 = (f32[7,1,168]{2,1,0:T(1,128)S(1)}, f32[7,1,168]{2,1,0:T(1,128)S(1)}, u32[]{:S(2)}, u32[]{:S(2)}) collective-permute-start(f32[7,1,168]{2,1,0:T(1,128)S(1)} %get-tuple-element.73), channel_id=1, source_target_pairs={{0,1},{1,2},{2,3},{3,4},{4,5},{5,6},{6,7},{7,8},{8,9},{9,10},{10,1... | collective-permute-start | bytes 14120 | tf_op jit(solution)/shard_map/ppermute | solution.py:522
  (14 other events, 197.2 us)

commit v6 on v5

--- a/solution.py
+++ b/solution.py
@@ -237,11 +237,11 @@
     rc = dot(line, span_mask((nz, LANES), 1, span, 0)) * sel
     scr[...] = jnp.zeros_like(scr)
     scr[:, :LANES] = small
-    scr[0:1, LANES : 2 * LANES] = rc
-    scr[1:2, LANES : LANES + ez] = k
-    scr[2:3, LANES : LANES + ez] = m
+    scr[7:8, LANES : 2 * LANES] = rc
+    scr[7:8, 2 * LANES : 2 * LANES + ez] = k
+    scr[7:8, 3 * LANES : 3 * LANES + ez] = m
     for x in range(7):
-        scr[:7, 2 * LANES + nz * x : 2 * LANES + nz * (x + 1)] = b_ref[x]
+        scr[:7, LANES + nz * x : LANES + nz * (x + 1)] = b_ref[x]
     for peer in range(out_ref.shape[0]):
         out_ref[peer, :, :width] = x_ref[:, peer * width : (peer + 1) * width]
         out_ref[peer, :, width:] = scr[...]
@@ -258,7 +258,8 @@
 
 def coarse_in_kernel(width, idx_ref, xl_ref, eye_ref, out_ref, bx_ref, hi_ref, lo_ref, k_ref, m_ref, group_ref, rc_ref):
     factor, _ = split_group(xl_ref, width)
-    rc = jnp.sum(xl_ref[:, 0:1, width + LANES : width + 2 * LANES], axis=0)
+    base = width + LANES
+    rc = jnp.sum(xl_ref[:, 7:8, base : base + LANES], axis=0)
     rc_ref[...] = rc
     group_ref[...] = xl_ref[:, :, : width + LANES]
     rows = factor.shape[0]
@@ -269,7 +270,6 @@
     out_ref[...] = jnp.where(core == 0, part[:, :half][None], part[:, half:][None])
     count = xl_ref.shape[0]
     nz, ez = bx_ref.shape[2], k_ref.shape[1]
-    base = width + 2 * LANES
     place = 0
     for apart in range(-4, 5):
         slot = lax.rem(idx_ref[0] + (apart + 2 * count), count)
@@ -277,8 +277,8 @@
             bx_ref[place] = xl_ref[slot, :, base + nz * x : base + nz * (x + 1)]
             place += 1
         if -4 < apart < 4:
-            k_ref[apart + 3 : apart + 4] = xl_ref[slot, 1:2, width + LANES : width + LANES + ez]
-            m_ref[apart + 3 : apart + 4] = xl_ref[slot, 2:3, width + LANES : width + LANES + ez]
+            k_ref[apart + 3 : apart + 4] = xl_ref[slot, 7:8, base + LANES : base + LANES + ez]
+            m_ref[apart + 3 : apart + 4] = xl_ref[slot, 7:8, base + 2 * LANES : base + 2 * LANES + ez]
     k_ref[7:8] = k_ref[6:7]
     m_ref[7:8] = m_ref[6:7]
     hi_ref[...] = bx_ref[:, 6:7]
@@ -297,9 +297,7 @@
     rows = factor.shape[0]
     part = jnp.sum(factor * join_halves(width, idx_ref, mine_ref, other_ref), axis=1, keepdims=True)
     x_part = as_row(part, eye_ref[:rows])
-    spot = lax.broadcasted_iota(jnp.int32, (8, LANES), 0)
-    tile = jnp.where(spot == 0, x_part, h_ref[...])
-    out_ref[...] = jnp.broadcast_to(tile[None], out_ref.shape)
+    spread(out_ref, jnp.concatenate([x_part, h_ref[1:2], h_ref[2:3]], axis=1))
 
 
 def coarse_mid_kernel(width, got_ref, xl_ref, rc_ref, eye_ref, out_ref, x_ref):
@@ -308,7 +306,7 @@
     rows = factor.shape[0]
     eye = eye_ref[:rows]
     got = jnp.sum(got_ref[...], axis=0)
-    x0, h, scal = got[0:1], got[1:2], got[2:3]
+    x0, h, scal = got[:, :LANES], got[:, LANES : 2 * LANES], got[:, 2 * LANES :]
     rc1_col = jnp.sum(small * x0 + eye * h, axis=1, keepdims=True)
     rc1 = as_row(rc1_col, eye)
     part = jnp.sum(rc1_col * factor, axis=0, keepdims=True)
@@ -348,8 +346,7 @@
     inner = inner_ref[...]
     wr = dot(jnp.sum(inner * resid, axis=0, keepdims=True), zct_ref[...]) * sel
     wt = dot(jnp.sum(inner * at, axis=0, keepdims=True), zct_ref[...]) * sel
-    tile = rows_tile([x_part, wr, wt, lane_put([total(resid * t), total(t * at)])])
-    out_ref[...] = jnp.broadcast_to(tile[None], out_ref.shape)
+    spread(out_ref, jnp.concatenate([x_part, wr, wt, lane_put([total(resid * t), total(t * at)])], axis=1))
     scal_ref[...] = lane_put([rho, den])
 
 
@@ -357,7 +354,7 @@
     _, small = split_group(xl_ref, width)
     eye = eye_ref[: small.shape[0]]
     got = jnp.sum(got_ref[...], axis=0)
-    x1, wr, wt, scal = got[0:1], got[1:2], got[2:3], got[3:4]
+    x1, wr, wt, scal = (got[:, LANES * row : LANES * (row + 1)] for row in range(4))
     step = lane_get(scal_ref[...], 0) / lane_get(scal_ref[...], 1)
     c = x0_ref[...] - step * x1
     tc = as_row(jnp.sum(small * c, axis=1, keepdims=True), eye)
@@ -554,8 +551,7 @@
         (mine,) = run(sum_kernel, [sums.shape[1:]], sums)
         return mine, lax.ppermute(mine, "gy", [(i, i ^ 1) for i in range(n_gy)])
 
-    group = (n_gx, c_dev, LANES)
-    aux = -(-(2 * LANES + 7 * nz) // LANES) * LANES
+    aux = -(-(LANES + 7 * nz) // LANES) * LANES
     (pay,) = run(kernel(first_kernel, tab["k_parts"], tab["m_parts"], width), [(n_gx, c_dev, width + aux)],
                  idx, b, k, m, coarse_factor, scratch=[(8, aux)], limit=56)
     xl = swap_gx(pay)
@@ -575,7 +571,7 @@
                           free=(1, 2))
 
     mine, other = halves(sums)
-    (pay,) = run(kernel(coarse_out_kernel, width), [group], idx, mine, other, members, eye, h)
+    (pay,) = run(kernel(coarse_out_kernel, width), [(n_gx, 1, 3 * LANES)], idx, mine, other, members, eye, h)
     got = swap_gx(pay)
     pay, x0 = run(kernel(coarse_mid_kernel, width), [(n_gy, 1, width // 2 + LANES), (1, LANES)], got, members, rc, eye, free=(0,))
     sums = swap_gy(pay)
@@ -590,7 +586,7 @@
     side = shift(hi, "gx", 1)
 
     mine, other = halves(sums)
-    pay, scal, resid = run(kernel(pair_kernel, width), [group, (1, LANES), cube], idx, mine, other, members, eye, b, q, u, au, s, a_s, inner, zct)
+    pay, scal, resid = run(kernel(pair_kernel, width), [(n_gx, 1, 4 * LANES), (1, LANES), cube], idx, mine, other, members, eye, b, q, u, au, s, a_s, inner, zct)
     got = swap_gx(pay)
     pay, x1 = run(kernel(last_in_kernel, width), [(n_gy, 1, LANES), (1, LANES)], got, members, x0, scal, eye, free=(0,))
     sums = swap_gy(pay)

time: 192 us -> 191 us (level)
  no operation moved by 1% of the time
where the time goes in v6:
time: 191 us
  starting transfers between devices  77.3 us (40%)
  waiting for transfers between devices  51.1 us (27%)
  blocking collectives  37.9 us (20%)
  Pallas kernels  21.9 us (11%)
    all_to_all x3, starting transfers between devices, swap_gy(): return lax.all_to_all(value, 'gy', 0, 0)  58.7 us
    all_to_all x3, blocking collectives, swap_gx(): return lax.all_to_all(value, 'gx', 0, 0)  37.9 us
    all_to_all x3, waiting for transfers between devices, swap_gy(): return lax.all_to_all(value, 'gy', 0, 0)  34.8 us
    pallas_call x15, Pallas kernels, run(): pl.pallas_call(kernel, out_shape=[(jax.ShapeDtypeStruct if i in free else...  21.9 us
    ppermute x10, waiting for transfers between devices, shift(): lax.ppermute(value, axis, [(i, (i + step) % count) for i in range(count)])  16.2 us
    ppermute x10, starting transfers between devices, shift(): lax.ppermute(value, axis, [(i, (i + step) % count) for i in range(count)])  11.2 us
    ppermute x2, starting transfers between devices, halves(): return (mine, lax.ppermute(mine, 'gy', [(i, i ^ 1) for i in range(n_gy)]))  7.37 us
  transfers between devices with their start and end apart: 15, of which 9 were waited for; matrix products, arithmetic and copies ran while one was open for 0% of the time, Pallas kernels for 8%

profile of v6, /device:TPU:1, one launch (start us, length us, event | category | flops | bytes accessed | tf_op | source)
XLA Modules:
  0.0 190.7 jit_solution(3313936074401321135)
XLA Ops:
  2.6 18.9 %all_to_all.30.refs_1_ = f32[16,8,1920]{2,1,0:T(8,128)S(1)} all-to-all(f32[16,8,1920]{2,1,0:T(8,128)S(1)} %shard_map.230), channel_id=1, replica_groups=mesh['gx'=16,'gy'=64] {'gx'}, dimensions={0} | all-to-all | bytes 1966080 | tf_op jit(solution)/shard_map/all_to_all | solution.py:545
  22.9 34.7 %all-to-all-start.1 = ((f32[64,1,256]{2,1,0:T(1,128)}), f32[64,1,256]{2,1,0:T(1,128)S(1)}, u32[]{:S(2)}, u32[]{:S(2)}) async-start(f32[64,1,256]{2,1,0:T(1,128)} %get-tuple-element.38), calls=%async_computation.1 | async-start | bytes 131072 | tf_op jit(solution)/shard_map/all_to_all | solution.py:548
  59.4 2.3 %collective-permute-done.1.yl_ref = f32[52,1,168]{2,1,0:T(1,128)S(1)} collective-permute-done((f32[52,1,168]{2,1,0:T(1,128)S(1)}, f32[52,1,168]{2,1,0:T(1,128)S(1)}, u32[]{:S(2)}, u32[]{:S(2)}) %collective-permute-start.1) | collective-permute-done | bytes 34976 | tf_op jit(solution)/shard_map/ppermute | solution.py:519
  61.7 1.7 collective-permute-done.2.yh_ref
  64.1 5.5 %shard_map.233 = (f32[36,16,168]{2,1,0:T(8,128)S(1)}, f32[36,2,168]{2,1,0:T(2,128)S(1)}, f32[36,2,168]{2,1,0:T(2,128)S(1)}) custom-call(f32[52,8,168]{2,1,0:T(8,128)S(1)} %get-tuple-element.40.bx_ref, f32[52,1,168]{2,1,0:T(1,128)S(1)} %collective-permute-done.1.yl_ref, f32[52,2,168]{2,1,0:T(2,128)S(1)} %collective-permute-done.2.yh_ref, ...), custom_call_target="tpu_custom_call" | custom-call | flops 77414400 | bytes 1421760 | tf_op jit(solution)/shard_map/pallas_call | solution.py:162
  69.7 2.6 %collective-permute-start.4 = (f32[36,2,168]{2,1,0:T(2,128)S(1)}, f32[36,2,168]{2,1,0:T(2,128)S(1)}, u32[]{:S(2)}, u32[]{:S(2)}) collective-permute-start(f32[36,2,168]{2,1,0:T(2,128)S(1)} %get-tuple-element.47), channel_id=1, source_target_pairs={{0,63},{1,0},{2,1},{3,2},{4,3},{5,4},{6,5},{7,6},{8,7},{9,8},{10,9... | collective-permute-start | bytes 145160 | tf_op jit(solution)/shard_map/ppermute | solution.py:519
  72.3 10.5 %all-to-all-done.1.sums_ref = f32[64,1,256]{2,1,0:T(1,128)S(1)} async-done(((f32[64,1,256]{2,1,0:T(1,128)}), f32[64,1,256]{2,1,0:T(1,128)S(1)}, u32[]{:S(2)}, u32[]{:S(2)}) %all-to-all-start.1) | async-done | bytes 65568 | tf_op jit(solution)/shard_map/all_to_all | solution.py:548
  82.8 3.8 %collective-permute-start = (f32[1,256]{1,0:T(1,128)S(1)}, f32[1,256]{1,0:T(1,128)S(1)}, u32[]{:S(2)}, u32[]{:S(2)}) collective-permute-start(f32[1,256]{1,0:T(1,128)S(1)} %shard_map.232.refs_1_), channel_id=1, source_target_pairs={{0,1},{1,0},{2,3},{3,2},{4,5},{5,4},{6,7},{7,6},{8,9},{9,8},{10,11... | collective-permute-start | bytes 3080 | tf_op jit(solution)/shard_map/ppermute | solution.py:552
  86.8 1.8 shard_map.234
  89.3 9.8 %all_to_all.31.refs_0_ = f32[16,1,384]{2,1,0:T(1,128)S(1)} all-to-all(f32[16,1,384]{2,1,0:T(1,128)S(1)} %shard_map.235), channel_id=1, replica_groups=mesh['gx'=16,'gy'=64] {'gx'}, dimensions={0} | all-to-all | bytes 49152 | tf_op jit(solution)/shard_map/all_to_all | solution.py:545
  99.9 13.7 %all-to-all-start.3 = ((f32[64,1,384]{2,1,0:T(1,128)}), f32[64,1,384]{2,1,0:T(1,128)S(1)}, u32[]{:S(2)}, u32[]{:S(2)}) async-start(f32[64,1,384]{2,1,0:T(1,128)} %get-tuple-element.50), calls=%async_computation.3 | async-start | bytes 196608 | tf_op jit(solution)/shard_map/all_to_all | solution.py:548
  113.6 2.5 %shard_map.238 = (f32[8,8,168]{2,1,0:T(8,128)S(1)}, f32[24,8,168]{2,1,0:T(8,128)S(1)}, f32[24,2,168]{2,1,0:T(2,128)S(1)}, f32[24,2,168]{2,1,0:T(2,128)S(1)}) custom-call(s32[3]{0:T(128)S(1)} %copy-done.17, f32[36,8,168]{2,1,0:T(8,128)S(1)} %get-tuple-element.51.u_ref, f32[1,128]{1,0:T(1,128)S(1)} %get-tuple-element.52.x_ref.refs_2_, ...), custom_call_target="tpu_custom_call" | custom-call | flops 77414400 | bytes 941324 | tf_op jit(solution)/shard_map/pallas_call | solution.py:162
  117.8 2.9 %collective-permute-done.6.yl_ref = f32[24,2,168]{2,1,0:T(2,128)S(1)} collective-permute-done((f32[24,2,168]{2,1,0:T(2,128)S(1)}, f32[24,2,168]{2,1,0:T(2,128)S(1)}, u32[]{:S(2)}, u32[]{:S(2)}) %collective-permute-start.6) | collective-permute-done | bytes 32288 | tf_op jit(solution)/shard_map/ppermute | solution.py:519
  120.7 2.8 %collective-permute-done.7.yh_ref = f32[24,2,168]{2,1,0:T(2,128)S(1)} collective-permute-done((f32[24,2,168]{2,1,0:T(2,128)S(1)}, f32[24,2,168]{2,1,0:T(2,128)S(1)}, u32[]{:S(2)}, u32[]{:S(2)}) %collective-permute-start.7) | collective-permute-done | bytes 32288 | tf_op jit(solution)/shard_map/ppermute | solution.py:519
  123.4 2.6 %shard_map.239 = (f32[8,8,168]{2,1,0:T(8,128)S(1)}, f32[8,16,168]{2,1,0:T(8,128)S(1)}, f32[8,2,168]{2,1,0:T(2,128)S(1)}, f32[8,2,168]{2,1,0:T(2,128)S(1)}) custom-call(f32[24,8,168]{2,1,0:T(8,128)S(1)} %get-tuple-element.53.qx_ref, f32[24,2,168]{2,1,0:T(2,128)S(1)} %collective-permute-done.6.yl_ref, f32[24,2,168]{2,1,0:T(2,128)S(1)} %collective-permute-done.7.yh_ref, ...), custom_call_target="tpu_custom_call" | custom-call | flops 77414400 | bytes 897600 | tf_op jit(solution)/shard_map/pallas_call | solution.py:162
  126.6 14.9 %all-to-all-done.3.sums_ref = f32[64,1,384]{2,1,0:T(1,128)S(1)} async-done(((f32[64,1,384]{2,1,0:T(1,128)}), f32[64,1,384]{2,1,0:T(1,128)S(1)}, u32[]{:S(2)}, u32[]{:S(2)}) %all-to-all-start.3) | async-done | bytes 98336 | tf_op jit(solution)/shard_map/all_to_all | solution.py:548
  141.6 3.5 %collective-permute-start.5 = (f32[1,384]{1,0:T(1,128)S(1)}, f32[1,384]{1,0:T(1,128)S(1)}, u32[]{:S(2)}, u32[]{:S(2)}) collective-permute-start(f32[1,384]{1,0:T(1,128)S(1)} %shard_map.237.refs_1_), channel_id=1, source_target_pairs={{0,1},{1,0},{2,3},{3,2},{4,5},{5,4},{6,7},{7,6},{8,9},{9,8},{10,11... | collective-permute-start | bytes 4616 | tf_op jit(solution)/shard_map/ppermute | solution.py:552
  147.0 9.3 %all_to_all.32.refs_0_ = f32[16,1,512]{2,1,0:T(1,128)S(1)} all-to-all(f32[16,1,512]{2,1,0:T(1,128)S(1)} %get-tuple-element.64), channel_id=1, replica_groups=mesh['gx'=16,'gy'=64] {'gx'}, dimensions={0} | all-to-all | bytes 65536 | tf_op jit(solution)/shard_map/all_to_all | solution.py:545
  157.2 10.3 %all-to-all-start.5 = ((f32[64,1,128]{2,1,0:T(1,128)}), f32[64,1,128]{2,1,0:T(1,128)S(1)}, u32[]{:S(2)}, u32[]{:S(2)}) async-start(f32[64,1,128]{2,1,0:T(1,128)} %get-tuple-element.66), calls=%async_computation.5 | async-start | bytes 65536 | tf_op jit(solution)/shard_map/all_to_all | solution.py:548
  167.5 2.2 %collective-permute-start.10 = (f32[1,8,168]{2,1,0:T(8,128)S(1)}, f32[1,8,168]{2,1,0:T(8,128)S(1)}, u32[]{:S(2)}, u32[]{:S(2)}) collective-permute-start(f32[1,8,168]{2,1,0:T(8,128)S(1)} %get-tuple-element.69), channel_id=1, source_target_pairs={{0,64},{64,128},{128,192},{192,256},{256,320},{320,384},{384,448},... | collective-permute-start | bytes 16136 | tf_op jit(solution)/shard_map/ppermute | solution.py:519
  169.7 5.8 %collective-permute-done.10.side_ref = f32[1,8,168]{2,1,0:T(8,128)S(1)} collective-permute-done((f32[1,8,168]{2,1,0:T(8,128)S(1)}, f32[1,8,168]{2,1,0:T(8,128)S(1)}, u32[]{:S(2)}, u32[]{:S(2)}) %collective-permute-start.10) | collective-permute-done | bytes 5408 | tf_op jit(solution)/shard_map/ppermute | solution.py:519
  175.5 1.6 shard_map.243
  177.2 2.5 %collective-permute-start.11 = (f32[7,1,168]{2,1,0:T(1,128)S(1)}, f32[7,1,168]{2,1,0:T(1,128)S(1)}, u32[]{:S(2)}, u32[]{:S(2)}) collective-permute-start(f32[7,1,168]{2,1,0:T(1,128)S(1)} %get-tuple-element.73), channel_id=1, source_target_pairs={{0,1},{1,2},{2,3},{3,4},{4,5},{5,6},{6,7},{7,8},{8,9},{9,10},{10,1... | collective-permute-start | bytes 14120 | tf_op jit(solution)/shard_map/ppermute | solution.py:519
  180.5 9.4 %all-to-all-done.5.sums_ref = f32[64,1,128]{2,1,0:T(1,128)S(1)} async-done(((f32[64,1,128]{2,1,0:T(1,128)}), f32[64,1,128]{2,1,0:T(1,128)S(1)}, u32[]{:S(2)}, u32[]{:S(2)}) %all-to-all-start.5) | async-done | bytes 32800 | tf_op jit(solution)/shard_map/all_to_all | solution.py:548
  (71 shorter events, 14.1 us)
Async XLA Ops:
  21.5 41.9 %copy-start.4 = (f32[240,168]{1,0:T(8,128)S(1)}, f32[240,168]{1,0:T(8,128)}, u32[]{:S(2)}) copy-start(f32[240,168]{1,0:T(8,128)} %constant.54.clone.refs_6_) | copy-start | bytes 483844
  21.5 41.9 %copy-start.5 = (f32[168,240]{1,0:T(8,128)S(1)}, f32[168,240]{1,0:T(8,128)}, u32[]{:S(2)}) copy-start(f32[168,240]{1,0:T(8,128)} %constant.53.clone.refs_5_) | copy-start | bytes 483844
  21.5 41.9 %copy-start.6 = (f32[160,160]{1,0:T(8,128)S(1)}, f32[160,160]{1,0:T(8,128)}, u32[]{:S(2)}) copy-start(f32[160,160]{1,0:T(8,128)} %constant.52.clone.refs_4_) | copy-start | bytes 307204
  21.5 41.9 %copy-start.7 = (f32[160,160]{1,0:T(8,128)S(1)}, f32[160,160]{1,0:T(8,128)}, u32[]{:S(2)}) copy-start(f32[160,160]{1,0:T(8,128)} %constant.51.clone.refs_3_) | copy-start | bytes 307204
  22.9 40.5 %copy-start.15 = (f32[160,1]{1,0:T(8,128)S(1)}, f32[160,1]{1,0:T(8,128)}, u32[]{:S(2)}) copy-start(f32[160,1]{1,0:T(8,128)} %constant.55.clone.refs_1_) | copy-start | bytes 1924
  22.9 40.5 %copy-start.16 = (f32[24,240]{1,0:T(8,128)S(1)}, f32[24,240]{1,0:T(8,128)}, u32[]{:S(2)}) copy-start(f32[24,240]{1,0:T(8,128)} %constant.57.clone.refs_0_) | copy-start | bytes 69124
  22.9 59.8 %all-to-all-start.1 = ((f32[64,1,256]{2,1,0:T(1,128)}), f32[64,1,256]{2,1,0:T(1,128)S(1)}, u32[]{:S(2)}, u32[]{:S(2)}) async-start(f32[64,1,256]{2,1,0:T(1,128)} %get-tuple-element.38), calls=%async_computation.1 | async-start | bytes 131072 | tf_op jit(solution)/shard_map/all_to_all | solution.py:548
  57.7 5.7 %collective-permute-start.2 = (f32[52,2,168]{2,1,0:T(2,128)S(1)}, f32[52,2,168]{2,1,0:T(2,128)S(1)}, u32[]{:S(2)}, u32[]{:S(2)}) collective-permute-start(f32[52,2,168]{2,1,0:T(2,128)S(1)} %get-tuple-element.42), channel_id=1, source_target_pairs={{0,63},{1,0},{2,1},{3,2},{4,3},{5,4},{6,5},{7,6},{8,7},{9,8},{10,9... | collective-permute-start | bytes 209672 | tf_op jit(solution)/shard_map/ppermute | solution.py:519
  58.1 3.5 %collective-permute-start.1 = (f32[52,1,168]{2,1,0:T(1,128)S(1)}, f32[52,1,168]{2,1,0:T(1,128)S(1)}, u32[]{:S(2)}, u32[]{:S(2)}) collective-permute-start(f32[52,1,168]{2,1,0:T(1,128)S(1)} %get-tuple-element.41), channel_id=1, source_target_pairs={{0,1},{1,2},{2,3},{3,4},{4,5},{5,6},{6,7},{7,8},{8,9},{9,10},{10,1... | collective-permute-start | bytes 104840 | tf_op jit(solution)/shard_map/ppermute | solution.py:519
  64.1 22.6 %copy-start.11 = (f32[64,1]{1,0:T(8,128)S(1)}, f32[64,1]{1,0:T(8,128)}, u32[]{:S(2)}) copy-start(f32[64,1]{1,0:T(8,128)} %constant.65.clone.inner_ref.refs_11_) | copy-start | bytes 772
  64.1 22.6 %copy-start.12 = (f32[7,7,168]{2,1,0:T(8,128)S(1)}, f32[7,7,168]{2,1,0:T(8,128)}, u32[]{:S(2)}) copy-start(f32[7,7,168]{2,1,0:T(8,128)} %refs_5_.7) | copy-start | bytes 98788
  64.1 22.6 %copy-start.14 = (f32[168,128]{1,0:T(8,128)S(1)}, f32[168,128]{1,0:T(8,128)}, u32[]{:S(2)}) copy-start(f32[168,128]{1,0:T(8,128)} %constant.67.clone.zct_ref.refs_12_) | copy-start | bytes 258052
  69.6 17.1 %collective-permute-start.3 = (f32[36,2,168]{2,1,0:T(2,128)S(1)}, f32[36,2,168]{2,1,0:T(2,128)S(1)}, u32[]{:S(2)}, u32[]{:S(2)}) collective-permute-start(f32[36,2,168]{2,1,0:T(2,128)S(1)} %get-tuple-element.46), channel_id=1, source_target_pairs={{0,1},{1,2},{2,3},{3,4},{4,5},{5,6},{6,7},{7,8},{8,9},{9,10},{10,1... | collective-permute-start | bytes 145160 | tf_op jit(solution)/shard_map/ppermute | solution.py:519
  69.7 17.0 %collective-permute-start.4 = (f32[36,2,168]{2,1,0:T(2,128)S(1)}, f32[36,2,168]{2,1,0:T(2,128)S(1)}, u32[]{:S(2)}, u32[]{:S(2)}) collective-permute-start(f32[36,2,168]{2,1,0:T(2,128)S(1)} %get-tuple-element.47), channel_id=1, source_target_pairs={{0,63},{1,0},{2,1},{3,2},{4,3},{5,4},{6,5},{7,6},{8,7},{9,8},{10,9... | collective-permute-start | bytes 145160 | tf_op jit(solution)/shard_map/ppermute | solution.py:519
  82.8 5.7 %collective-permute-start = (f32[1,256]{1,0:T(1,128)S(1)}, f32[1,256]{1,0:T(1,128)S(1)}, u32[]{:S(2)}, u32[]{:S(2)}) collective-permute-start(f32[1,256]{1,0:T(1,128)S(1)} %shard_map.232.refs_1_), channel_id=1, source_target_pairs={{0,1},{1,0},{2,3},{3,2},{4,5},{5,4},{6,7},{7,6},{8,9},{9,8},{10,11... | collective-permute-start | bytes 3080 | tf_op jit(solution)/shard_map/ppermute | solution.py:552
  99.9 41.6 %all-to-all-start.3 = ((f32[64,1,384]{2,1,0:T(1,128)}), f32[64,1,384]{2,1,0:T(1,128)S(1)}, u32[]{:S(2)}, u32[]{:S(2)}) async-start(f32[64,1,384]{2,1,0:T(1,128)} %get-tuple-element.50), calls=%async_computation.3 | async-start | bytes 196608 | tf_op jit(solution)/shard_map/all_to_all | solution.py:548
  116.1 4.5 %collective-permute-start.6 = (f32[24,2,168]{2,1,0:T(2,128)S(1)}, f32[24,2,168]{2,1,0:T(2,128)S(1)}, u32[]{:S(2)}, u32[]{:S(2)}) collective-permute-start(f32[24,2,168]{2,1,0:T(2,128)S(1)} %get-tuple-element.54), channel_id=1, source_target_pairs={{0,1},{1,2},{2,3},{3,4},{4,5},{5,6},{6,7},{7,8},{8,9},{9,10},{10,1... | collective-permute-start | bytes 96776 | tf_op jit(solution)/shard_map/ppermute | solution.py:519
  117.8 5.7 %collective-permute-start.7 = (f32[24,2,168]{2,1,0:T(2,128)S(1)}, f32[24,2,168]{2,1,0:T(2,128)S(1)}, u32[]{:S(2)}, u32[]{:S(2)}) collective-permute-start(f32[24,2,168]{2,1,0:T(2,128)S(1)} %get-tuple-element.55), channel_id=1, source_target_pairs={{0,63},{1,0},{2,1},{3,2},{4,3},{5,4},{6,5},{7,6},{8,7},{9,8},{10,9... | collective-permute-start | bytes 96776 | tf_op jit(solution)/shard_map/ppermute | solution.py:519
  126.0 19.1 %collective-permute-start.8 = (f32[8,2,168]{2,1,0:T(2,128)S(1)}, f32[8,2,168]{2,1,0:T(2,128)S(1)}, u32[]{:S(2)}, u32[]{:S(2)}) collective-permute-start(f32[8,2,168]{2,1,0:T(2,128)S(1)} %get-tuple-element.60), channel_id=1, source_target_pairs={{0,1},{1,2},{2,3},{3,4},{4,5},{5,6},{6,7},{7,8},{8,9},{9,10},{10,1... | collective-permute-start | bytes 32264 | tf_op jit(solution)/shard_map/ppermute | solution.py:519
  126.1 19.1 %collective-permute-start.9 = (f32[8,2,168]{2,1,0:T(2,128)S(1)}, f32[8,2,168]{2,1,0:T(2,128)S(1)}, u32[]{:S(2)}, u32[]{:S(2)}) collective-permute-start(f32[8,2,168]{2,1,0:T(2,128)S(1)} %get-tuple-element.61), channel_id=1, source_target_pairs={{0,63},{1,0},{2,1},{3,2},{4,3},{5,4},{6,5},{7,6},{8,7},{9,8},{10,9... | collective-permute-start | bytes 32264 | tf_op jit(solution)/shard_map/ppermute | solution.py:519
  141.6 4.5 %collective-permute-start.5 = (f32[1,384]{1,0:T(1,128)S(1)}, f32[1,384]{1,0:T(1,128)S(1)}, u32[]{:S(2)}, u32[]{:S(2)}) collective-permute-start(f32[1,384]{1,0:T(1,128)S(1)} %shard_map.237.refs_1_), channel_id=1, source_target_pairs={{0,1},{1,0},{2,3},{3,2},{4,5},{5,4},{6,7},{7,6},{8,9},{9,8},{10,11... | collective-permute-start | bytes 4616 | tf_op jit(solution)/shard_map/ppermute | solution.py:552
  157.2 32.7 %all-to-all-start.5 = ((f32[64,1,128]{2,1,0:T(1,128)}), f32[64,1,128]{2,1,0:T(1,128)S(1)}, u32[]{:S(2)}, u32[]{:S(2)}) async-start(f32[64,1,128]{2,1,0:T(1,128)} %get-tuple-element.66), calls=%async_computation.5 | async-start | bytes 65536 | tf_op jit(solution)/shard_map/all_to_all | solution.py:548
  167.5 8.0 %collective-permute-start.10 = (f32[1,8,168]{2,1,0:T(8,128)S(1)}, f32[1,8,168]{2,1,0:T(8,128)S(1)}, u32[]{:S(2)}, u32[]{:S(2)}) collective-permute-start(f32[1,8,168]{2,1,0:T(8,128)S(1)} %get-tuple-element.69), channel_id=1, source_target_pairs={{0,64},{64,128},{128,192},{192,256},{256,320},{320,384},{384,448},... | collective-permute-start | bytes 16136 | tf_op jit(solution)/shard_map/ppermute | solution.py:519
  177.2 3.3 %collective-permute-start.11 = (f32[7,1,168]{2,1,0:T(1,128)S(1)}, f32[7,1,168]{2,1,0:T(1,128)S(1)}, u32[]{:S(2)}, u32[]{:S(2)}) collective-permute-start(f32[7,1,168]{2,1,0:T(1,128)S(1)} %get-tuple-element.73), channel_id=1, source_target_pairs={{0,1},{1,2},{2,3},{3,4},{4,5},{5,6},{6,7},{7,8},{8,9},{9,10},{10,1... | collective-permute-start | bytes 14120 | tf_op jit(solution)/shard_map/ppermute | solution.py:519
  (14 other events, 196.5 us)

commit v7 on v6

--- a/solution.py
+++ b/solution.py
@@ -397,9 +397,10 @@
     lines[...] = dot(block, zf[...])
     acc[...] = jnp.zeros_like(acc)
     lam = lam_ab[...] + lam_c[...]
+    k_lines, m_lines = dot(k_ref[...], rep10[...]), dot(m_ref[...], rep10[...])
     for c in range(count):
-        k, m = k_ref[first + c : first + c + 1], m_ref[first + c : first + c + 1]
-        den = dot(k, rep10[...]) * lam + dot(m, rep10[...])
+        spot = slice(first + c, first + c + 1)
+        den = k_lines[spot] * lam + m_lines[spot]
         spectral = dot(qqt[...], lines[112 * c : 112 * c + 160]) / den
         low = max(128 - 112 * c, 0)
         high = min(112 * (count - 1) + 32 - 112 * c, 160)
@@ -485,9 +486,9 @@
     su[...] = dot(whole, g8[...])
     sk[...] = dot(whole, zk[...])
     acc[...] = jnp.zeros_like(acc)
+    k_lines, m_lines = dot(k_ref[...], rep8[...]), dot(m_ref[...], rep8[...]) * wz[...]
     for c in range(5):
-        k_line = dot(k_ref[c + 1 : c + 2], rep8[...])
-        m_line = dot(m_ref[c + 1 : c + 2], rep8[...]) * wz[...]
+        k_line, m_line = k_lines[c + 1 : c + 2], m_lines[c + 1 : c + 2]
         part = slice(56 * c, 56 * c + 64)
         u = su[part]
         out = (k_line * wz[...]) * dot(kk[...], u) + ww[...] * (k_line * sk[part] + m_line * u)

time: 191 us -> 191 us (level)
  transfers between devices with their start and end apart: 15 -> 15, of which waited for: 9 -> 9; matrix products, arithmetic and copies ran while one was open for 0% -> 0% of each run, Pallas kernels for 8% -> 7%
where the time goes in v7:
time: 191 us; the launch traced here: 190 us
  starting transfers between devices  76.6 us (40%)
  waiting for transfers between devices  52 us (27%)
  blocking collectives  37.9 us (20%)
  Pallas kernels  21.1 us (11%)
    all_to_all x3, starting transfers between devices, swap_gy(): return lax.all_to_all(value, 'gy', 0, 0)  58 us
    all_to_all x3, blocking collectives, swap_gx(): return lax.all_to_all(value, 'gx', 0, 0)  37.9 us
    all_to_all x3, waiting for transfers between devices, swap_gy(): return lax.all_to_all(value, 'gy', 0, 0)  35.7 us
    pallas_call x15, Pallas kernels, run(): pl.pallas_call(kernel, out_shape=[(jax.ShapeDtypeStruct if i in free else...  21.1 us
    ppermute x10, waiting for transfers between devices, shift(): lax.ppermute(value, axis, [(i, (i + step) % count) for i in range(count)])  16.3 us
    ppermute x10, starting transfers between devices, shift(): lax.ppermute(value, axis, [(i, (i + step) % count) for i in range(count)])  11.2 us
    ppermute x2, starting transfers between devices, halves(): return (mine, lax.ppermute(mine, 'gy', [(i, i ^ 1) for i in range(n_gy)]))  7.36 us
  transfers between devices with their start and end apart: 15, of which 9 were waited for; matrix products, arithmetic and copies ran while one was open for 0% of the time, Pallas kernels for 7%

profile of v7, /device:TPU:1, one launch (start us, length us, event | category | flops | bytes accessed | tf_op | source)
XLA Modules:
  0.0 190.0 jit_solution(7407306981829631740)
XLA Ops:
  2.6 18.9 %all_to_all.30.refs_1_ = f32[16,8,1920]{2,1,0:T(8,128)S(1)} all-to-all(f32[16,8,1920]{2,1,0:T(8,128)S(1)} %shard_map.230), channel_id=1, replica_groups=mesh['gx'=16,'gy'=64] {'gx'}, dimensions={0} | all-to-all | bytes 1966080 | tf_op jit(solution)/shard_map/all_to_all | solution.py:546
  22.9 34.7 %all-to-all-start.1 = ((f32[64,1,256]{2,1,0:T(1,128)}), f32[64,1,256]{2,1,0:T(1,128)S(1)}, u32[]{:S(2)}, u32[]{:S(2)}) async-start(f32[64,1,256]{2,1,0:T(1,128)} %get-tuple-element.38), calls=%async_computation.1 | async-start | bytes 131072 | tf_op jit(solution)/shard_map/all_to_all | solution.py:549
  59.4 2.3 %collective-permute-done.1.yl_ref = f32[52,1,168]{2,1,0:T(1,128)S(1)} collective-permute-done((f32[52,1,168]{2,1,0:T(1,128)S(1)}, f32[52,1,168]{2,1,0:T(1,128)S(1)}, u32[]{:S(2)}, u32[]{:S(2)}) %collective-permute-start.1) | collective-permute-done | bytes 34976 | tf_op jit(solution)/shard_map/ppermute | solution.py:520
  61.7 1.7 collective-permute-done.2.yh_ref
  64.1 4.9 %shard_map.233 = (f32[36,16,168]{2,1,0:T(8,128)S(1)}, f32[36,2,168]{2,1,0:T(2,128)S(1)}, f32[36,2,168]{2,1,0:T(2,128)S(1)}) custom-call(f32[52,8,168]{2,1,0:T(8,128)S(1)} %get-tuple-element.40.bx_ref, f32[52,1,168]{2,1,0:T(1,128)S(1)} %collective-permute-done.1.yl_ref, f32[52,2,168]{2,1,0:T(2,128)S(1)} %collective-permute-done.2.yh_ref, ...), custom_call_target="tpu_custom_call" | custom-call | flops 77414400 | bytes 1421760 | tf_op jit(solution)/shard_map/pallas_call | solution.py:162
  69.1 2.6 %collective-permute-start.4 = (f32[36,2,168]{2,1,0:T(2,128)S(1)}, f32[36,2,168]{2,1,0:T(2,128)S(1)}, u32[]{:S(2)}, u32[]{:S(2)}) collective-permute-start(f32[36,2,168]{2,1,0:T(2,128)S(1)} %get-tuple-element.47), channel_id=1, source_target_pairs={{0,63},{1,0},{2,1},{3,2},{4,3},{5,4},{6,5},{7,6},{8,7},{9,8},{10,9... | collective-permute-start | bytes 145160 | tf_op jit(solution)/shard_map/ppermute | solution.py:520
  71.7 11.0 %all-to-all-done.1.sums_ref = f32[64,1,256]{2,1,0:T(1,128)S(1)} async-done(((f32[64,1,256]{2,1,0:T(1,128)}), f32[64,1,256]{2,1,0:T(1,128)S(1)}, u32[]{:S(2)}, u32[]{:S(2)}) %all-to-all-start.1) | async-done | bytes 65568 | tf_op jit(solution)/shard_map/all_to_all | solution.py:549
  82.8 3.8 %collective-permute-start = (f32[1,256]{1,0:T(1,128)S(1)}, f32[1,256]{1,0:T(1,128)S(1)}, u32[]{:S(2)}, u32[]{:S(2)}) collective-permute-start(f32[1,256]{1,0:T(1,128)S(1)} %shard_map.232.refs_1_), channel_id=1, source_target_pairs={{0,1},{1,0},{2,3},{3,2},{4,5},{5,4},{6,7},{7,6},{8,9},{9,8},{10,11... | collective-permute-start | bytes 3080 | tf_op jit(solution)/shard_map/ppermute | solution.py:553
  86.8 1.8 shard_map.234
  89.3 9.8 %all_to_all.31.refs_0_ = f32[16,1,384]{2,1,0:T(1,128)S(1)} all-to-all(f32[16,1,384]{2,1,0:T(1,128)S(1)} %shard_map.235), channel_id=1, replica_groups=mesh['gx'=16,'gy'=64] {'gx'}, dimensions={0} | all-to-all | bytes 49152 | tf_op jit(solution)/shard_map/all_to_all | solution.py:546
  99.9 13.1 %all-to-all-start.3 = ((f32[64,1,384]{2,1,0:T(1,128)}), f32[64,1,384]{2,1,0:T(1,128)S(1)}, u32[]{:S(2)}, u32[]{:S(2)}) async-start(f32[64,1,384]{2,1,0:T(1,128)} %get-tuple-element.50), calls=%async_computation.3 | async-start | bytes 196608 | tf_op jit(solution)/shard_map/all_to_all | solution.py:549
  113.1 2.3 %shard_map.238 = (f32[8,8,168]{2,1,0:T(8,128)S(1)}, f32[24,8,168]{2,1,0:T(8,128)S(1)}, f32[24,2,168]{2,1,0:T(2,128)S(1)}, f32[24,2,168]{2,1,0:T(2,128)S(1)}) custom-call(s32[3]{0:T(128)S(1)} %copy-done.17, f32[36,8,168]{2,1,0:T(8,128)S(1)} %get-tuple-element.51.u_ref, f32[1,128]{1,0:T(1,128)S(1)} %get-tuple-element.52.x_ref.refs_2_, ...), custom_call_target="tpu_custom_call" | custom-call | flops 77414400 | bytes 941324 | tf_op jit(solution)/shard_map/pallas_call | solution.py:162
  117.1 3.1 %collective-permute-done.6.yl_ref = f32[24,2,168]{2,1,0:T(2,128)S(1)} collective-permute-done((f32[24,2,168]{2,1,0:T(2,128)S(1)}, f32[24,2,168]{2,1,0:T(2,128)S(1)}, u32[]{:S(2)}, u32[]{:S(2)}) %collective-permute-start.6) | collective-permute-done | bytes 32288 | tf_op jit(solution)/shard_map/ppermute | solution.py:520
  120.1 2.6 %collective-permute-done.7.yh_ref = f32[24,2,168]{2,1,0:T(2,128)S(1)} collective-permute-done((f32[24,2,168]{2,1,0:T(2,128)S(1)}, f32[24,2,168]{2,1,0:T(2,128)S(1)}, u32[]{:S(2)}, u32[]{:S(2)}) %collective-permute-start.7) | collective-permute-done | bytes 32288 | tf_op jit(solution)/shard_map/ppermute | solution.py:520
  122.8 2.4 %shard_map.239 = (f32[8,8,168]{2,1,0:T(8,128)S(1)}, f32[8,16,168]{2,1,0:T(8,128)S(1)}, f32[8,2,168]{2,1,0:T(2,128)S(1)}, f32[8,2,168]{2,1,0:T(2,128)S(1)}) custom-call(f32[24,8,168]{2,1,0:T(8,128)S(1)} %get-tuple-element.53.qx_ref, f32[24,2,168]{2,1,0:T(2,128)S(1)} %collective-permute-done.6.yl_ref, f32[24,2,168]{2,1,0:T(2,128)S(1)} %collective-permute-done.7.yh_ref, ...), custom_call_target="tpu_custom_call" | custom-call | flops 77414400 | bytes 897600 | tf_op jit(solution)/shard_map/pallas_call | solution.py:162
  125.7 15.3 %all-to-all-done.3.sums_ref = f32[64,1,384]{2,1,0:T(1,128)S(1)} async-done(((f32[64,1,384]{2,1,0:T(1,128)}), f32[64,1,384]{2,1,0:T(1,128)S(1)}, u32[]{:S(2)}, u32[]{:S(2)}) %all-to-all-start.3) | async-done | bytes 98336 | tf_op jit(solution)/shard_map/all_to_all | solution.py:549
  141.1 3.5 %collective-permute-start.5 = (f32[1,384]{1,0:T(1,128)S(1)}, f32[1,384]{1,0:T(1,128)S(1)}, u32[]{:S(2)}, u32[]{:S(2)}) collective-permute-start(f32[1,384]{1,0:T(1,128)S(1)} %shard_map.237.refs_1_), channel_id=1, source_target_pairs={{0,1},{1,0},{2,3},{3,2},{4,5},{5,4},{6,7},{7,6},{8,9},{9,8},{10,11... | collective-permute-start | bytes 4616 | tf_op jit(solution)/shard_map/ppermute | solution.py:553
  146.5 9.2 %all_to_all.32.refs_0_ = f32[16,1,512]{2,1,0:T(1,128)S(1)} all-to-all(f32[16,1,512]{2,1,0:T(1,128)S(1)} %get-tuple-element.64), channel_id=1, replica_groups=mesh['gx'=16,'gy'=64] {'gx'}, dimensions={0} | all-to-all | bytes 65536 | tf_op jit(solution)/shard_map/all_to_all | solution.py:546
  156.6 10.2 %all-to-all-start.5 = ((f32[64,1,128]{2,1,0:T(1,128)}), f32[64,1,128]{2,1,0:T(1,128)S(1)}, u32[]{:S(2)}, u32[]{:S(2)}) async-start(f32[64,1,128]{2,1,0:T(1,128)} %get-tuple-element.66), calls=%async_computation.5 | async-start | bytes 65536 | tf_op jit(solution)/shard_map/all_to_all | solution.py:549
  166.8 2.2 %collective-permute-start.10 = (f32[1,8,168]{2,1,0:T(8,128)S(1)}, f32[1,8,168]{2,1,0:T(8,128)S(1)}, u32[]{:S(2)}, u32[]{:S(2)}) collective-permute-start(f32[1,8,168]{2,1,0:T(8,128)S(1)} %get-tuple-element.69), channel_id=1, source_target_pairs={{0,64},{64,128},{128,192},{192,256},{256,320},{320,384},{384,448},... | collective-permute-start | bytes 16136 | tf_op jit(solution)/shard_map/ppermute | solution.py:520
  169.0 5.8 %collective-permute-done.10.side_ref = f32[1,8,168]{2,1,0:T(8,128)S(1)} collective-permute-done((f32[1,8,168]{2,1,0:T(8,128)S(1)}, f32[1,8,168]{2,1,0:T(8,128)S(1)}, u32[]{:S(2)}, u32[]{:S(2)}) %collective-permute-start.10) | collective-permute-done | bytes 5408 | tf_op jit(solution)/shard_map/ppermute | solution.py:520
  174.8 1.6 shard_map.243
  176.5 2.5 %collective-permute-start.11 = (f32[7,1,168]{2,1,0:T(1,128)S(1)}, f32[7,1,168]{2,1,0:T(1,128)S(1)}, u32[]{:S(2)}, u32[]{:S(2)}) collective-permute-start(f32[7,1,168]{2,1,0:T(1,128)S(1)} %get-tuple-element.73), channel_id=1, source_target_pairs={{0,1},{1,2},{2,3},{3,4},{4,5},{5,6},{6,7},{7,8},{8,9},{9,10},{10,1... | collective-permute-start | bytes 14120 | tf_op jit(solution)/shard_map/ppermute | solution.py:520
  179.8 9.4 %all-to-all-done.5.sums_ref = f32[64,1,128]{2,1,0:T(1,128)S(1)} async-done(((f32[64,1,128]{2,1,0:T(1,128)}), f32[64,1,128]{2,1,0:T(1,128)S(1)}, u32[]{:S(2)}, u32[]{:S(2)}) %all-to-all-start.5) | async-done | bytes 32800 | tf_op jit(solution)/shard_map/all_to_all | solution.py:549
  (71 shorter events, 14.1 us)
Async XLA Ops:
  21.5 41.9 %copy-start.4 = (f32[240,168]{1,0:T(8,128)S(1)}, f32[240,168]{1,0:T(8,128)}, u32[]{:S(2)}) copy-start(f32[240,168]{1,0:T(8,128)} %constant.54.clone.refs_6_) | copy-start | bytes 483844
  21.5 41.9 %copy-start.5 = (f32[168,240]{1,0:T(8,128)S(1)}, f32[168,240]{1,0:T(8,128)}, u32[]{:S(2)}) copy-start(f32[168,240]{1,0:T(8,128)} %constant.53.clone.refs_5_) | copy-start | bytes 483844
  21.5 41.9 %copy-start.6 = (f32[160,160]{1,0:T(8,128)S(1)}, f32[160,160]{1,0:T(8,128)}, u32[]{:S(2)}) copy-start(f32[160,160]{1,0:T(8,128)} %constant.52.clone.refs_4_) | copy-start | bytes 307204
  21.5 41.9 %copy-start.7 = (f32[160,160]{1,0:T(8,128)S(1)}, f32[160,160]{1,0:T(8,128)}, u32[]{:S(2)}) copy-start(f32[160,160]{1,0:T(8,128)} %constant.51.clone.refs_3_) | copy-start | bytes 307204
  22.9 40.5 %copy-start.15 = (f32[160,1]{1,0:T(8,128)S(1)}, f32[160,1]{1,0:T(8,128)}, u32[]{:S(2)}) copy-start(f32[160,1]{1,0:T(8,128)} %constant.55.clone.refs_1_) | copy-start | bytes 1924
  22.9 40.5 %copy-start.16 = (f32[24,240]{1,0:T(8,128)S(1)}, f32[24,240]{1,0:T(8,128)}, u32[]{:S(2)}) copy-start(f32[24,240]{1,0:T(8,128)} %constant.57.clone.refs_0_) | copy-start | bytes 69124
  22.9 59.8 %all-to-all-start.1 = ((f32[64,1,256]{2,1,0:T(1,128)}), f32[64,1,256]{2,1,0:T(1,128)S(1)}, u32[]{:S(2)}, u32[]{:S(2)}) async-start(f32[64,1,256]{2,1,0:T(1,128)} %get-tuple-element.38), calls=%async_computation.1 | async-start | bytes 131072 | tf_op jit(solution)/shard_map/all_to_all | solution.py:549
  57.7 5.7 %collective-permute-start.2 = (f32[52,2,168]{2,1,0:T(2,128)S(1)}, f32[52,2,168]{2,1,0:T(2,128)S(1)}, u32[]{:S(2)}, u32[]{:S(2)}) collective-permute-start(f32[52,2,168]{2,1,0:T(2,128)S(1)} %get-tuple-element.42), channel_id=1, source_target_pairs={{0,63},{1,0},{2,1},{3,2},{4,3},{5,4},{6,5},{7,6},{8,7},{9,8},{10,9... | collective-permute-start | bytes 209672 | tf_op jit(solution)/shard_map/ppermute | solution.py:520
  58.1 3.5 %collective-permute-start.1 = (f32[52,1,168]{2,1,0:T(1,128)S(1)}, f32[52,1,168]{2,1,0:T(1,128)S(1)}, u32[]{:S(2)}, u32[]{:S(2)}) collective-permute-start(f32[52,1,168]{2,1,0:T(1,128)S(1)} %get-tuple-element.41), channel_id=1, source_target_pairs={{0,1},{1,2},{2,3},{3,4},{4,5},{5,6},{6,7},{7,8},{8,9},{9,10},{10,1... | collective-permute-start | bytes 104840 | tf_op jit(solution)/shard_map/ppermute | solution.py:520
  64.1 22.6 %copy-start.11 = (f32[64,1]{1,0:T(8,128)S(1)}, f32[64,1]{1,0:T(8,128)}, u32[]{:S(2)}) copy-start(f32[64,1]{1,0:T(8,128)} %constant.65.clone.inner_ref.refs_11_) | copy-start | bytes 772
  64.1 22.6 %copy-start.12 = (f32[7,7,168]{2,1,0:T(8,128)S(1)}, f32[7,7,168]{2,1,0:T(8,128)}, u32[]{:S(2)}) copy-start(f32[7,7,168]{2,1,0:T(8,128)} %refs_5_.7) | copy-start | bytes 98788
  64.1 22.6 %copy-start.14 = (f32[168,128]{1,0:T(8,128)S(1)}, f32[168,128]{1,0:T(8,128)}, u32[]{:S(2)}) copy-start(f32[168,128]{1,0:T(8,128)} %constant.67.clone.zct_ref.refs_12_) | copy-start | bytes 258052
  69.0 17.6 %collective-permute-start.3 = (f32[36,2,168]{2,1,0:T(2,128)S(1)}, f32[36,2,168]{2,1,0:T(2,128)S(1)}, u32[]{:S(2)}, u32[]{:S(2)}) collective-permute-start(f32[36,2,168]{2,1,0:T(2,128)S(1)} %get-tuple-element.46), channel_id=1, source_target_pairs={{0,1},{1,2},{2,3},{3,4},{4,5},{5,6},{6,7},{7,8},{8,9},{9,10},{10,1... | collective-permute-start | bytes 145160 | tf_op jit(solution)/shard_map/ppermute | solution.py:520
  69.1 17.6 %collective-permute-start.4 = (f32[36,2,168]{2,1,0:T(2,128)S(1)}, f32[36,2,168]{2,1,0:T(2,128)S(1)}, u32[]{:S(2)}, u32[]{:S(2)}) collective-permute-start(f32[36,2,168]{2,1,0:T(2,128)S(1)} %get-tuple-element.47), channel_id=1, source_target_pairs={{0,63},{1,0},{2,1},{3,2},{4,3},{5,4},{6,5},{7,6},{8,7},{9,8},{10,9... | collective-permute-start | bytes 145160 | tf_op jit(solution)/shard_map/ppermute | solution.py:520
  82.8 5.7 %collective-permute-start = (f32[1,256]{1,0:T(1,128)S(1)}, f32[1,256]{1,0:T(1,128)S(1)}, u32[]{:S(2)}, u32[]{:S(2)}) collective-permute-start(f32[1,256]{1,0:T(1,128)S(1)} %shard_map.232.refs_1_), channel_id=1, source_target_pairs={{0,1},{1,0},{2,3},{3,2},{4,5},{5,4},{6,7},{7,6},{8,9},{9,8},{10,11... | collective-permute-start | bytes 3080 | tf_op jit(solution)/shard_map/ppermute | solution.py:553
  99.9 41.1 %all-to-all-start.3 = ((f32[64,1,384]{2,1,0:T(1,128)}), f32[64,1,384]{2,1,0:T(1,128)S(1)}, u32[]{:S(2)}, u32[]{:S(2)}) async-start(f32[64,1,384]{2,1,0:T(1,128)} %get-tuple-element.50), calls=%async_computation.3 | async-start | bytes 196608 | tf_op jit(solution)/shard_map/all_to_all | solution.py:549
  115.4 4.7 %collective-permute-start.6 = (f32[24,2,168]{2,1,0:T(2,128)S(1)}, f32[24,2,168]{2,1,0:T(2,128)S(1)}, u32[]{:S(2)}, u32[]{:S(2)}) collective-permute-start(f32[24,2,168]{2,1,0:T(2,128)S(1)} %get-tuple-element.54), channel_id=1, source_target_pairs={{0,1},{1,2},{2,3},{3,4},{4,5},{5,6},{6,7},{7,8},{8,9},{9,10},{10,1... | collective-permute-start | bytes 96776 | tf_op jit(solution)/shard_map/ppermute | solution.py:520
  117.1 5.7 %collective-permute-start.7 = (f32[24,2,168]{2,1,0:T(2,128)S(1)}, f32[24,2,168]{2,1,0:T(2,128)S(1)}, u32[]{:S(2)}, u32[]{:S(2)}) collective-permute-start(f32[24,2,168]{2,1,0:T(2,128)S(1)} %get-tuple-element.55), channel_id=1, source_target_pairs={{0,63},{1,0},{2,1},{3,2},{4,3},{5,4},{6,5},{7,6},{8,7},{9,8},{10,9... | collective-permute-start | bytes 96776 | tf_op jit(solution)/shard_map/ppermute | solution.py:520
  125.2 19.4 %collective-permute-start.8 = (f32[8,2,168]{2,1,0:T(2,128)S(1)}, f32[8,2,168]{2,1,0:T(2,128)S(1)}, u32[]{:S(2)}, u32[]{:S(2)}) collective-permute-start(f32[8,2,168]{2,1,0:T(2,128)S(1)} %get-tuple-element.60), channel_id=1, source_target_pairs={{0,1},{1,2},{2,3},{3,4},{4,5},{5,6},{6,7},{7,8},{8,9},{9,10},{10,1... | collective-permute-start | bytes 32264 | tf_op jit(solution)/shard_map/ppermute | solution.py:520
  125.2 19.4 %collective-permute-start.9 = (f32[8,2,168]{2,1,0:T(2,128)S(1)}, f32[8,2,168]{2,1,0:T(2,128)S(1)}, u32[]{:S(2)}, u32[]{:S(2)}) collective-permute-start(f32[8,2,168]{2,1,0:T(2,128)S(1)} %get-tuple-element.61), channel_id=1, source_target_pairs={{0,63},{1,0},{2,1},{3,2},{4,3},{5,4},{6,5},{7,6},{8,7},{9,8},{10,9... | collective-permute-start | bytes 32264 | tf_op jit(solution)/shard_map/ppermute | solution.py:520
  141.1 4.5 %collective-permute-start.5 = (f32[1,384]{1,0:T(1,128)S(1)}, f32[1,384]{1,0:T(1,128)S(1)}, u32[]{:S(2)}, u32[]{:S(2)}) collective-permute-start(f32[1,384]{1,0:T(1,128)S(1)} %shard_map.237.refs_1_), channel_id=1, source_target_pairs={{0,1},{1,0},{2,3},{3,2},{4,5},{5,4},{6,7},{7,6},{8,9},{9,8},{10,11... | collective-permute-start | bytes 4616 | tf_op jit(solution)/shard_map/ppermute | solution.py:553
  156.6 32.5 %all-to-all-start.5 = ((f32[64,1,128]{2,1,0:T(1,128)}), f32[64,1,128]{2,1,0:T(1,128)S(1)}, u32[]{:S(2)}, u32[]{:S(2)}) async-start(f32[64,1,128]{2,1,0:T(1,128)} %get-tuple-element.66), calls=%async_computation.5 | async-start | bytes 65536 | tf_op jit(solution)/shard_map/all_to_all | solution.py:549
  166.8 8.0 %collective-permute-start.10 = (f32[1,8,168]{2,1,0:T(8,128)S(1)}, f32[1,8,168]{2,1,0:T(8,128)S(1)}, u32[]{:S(2)}, u32[]{:S(2)}) collective-permute-start(f32[1,8,168]{2,1,0:T(8,128)S(1)} %get-tuple-element.69), channel_id=1, source_target_pairs={{0,64},{64,128},{128,192},{192,256},{256,320},{320,384},{384,448},... | collective-permute-start | bytes 16136 | tf_op jit(solution)/shard_map/ppermute | solution.py:520
  176.5 3.3 %collective-permute-start.11 = (f32[7,1,168]{2,1,0:T(1,128)S(1)}, f32[7,1,168]{2,1,0:T(1,128)S(1)}, u32[]{:S(2)}, u32[]{:S(2)}) collective-permute-start(f32[7,1,168]{2,1,0:T(1,128)S(1)} %get-tuple-element.73), channel_id=1, source_target_pairs={{0,1},{1,2},{2,3},{3,4},{4,5},{5,6},{6,7},{7,8},{8,9},{9,10},{10,1... | collective-permute-start | bytes 14120 | tf_op jit(solution)/shard_map/ppermute | solution.py:520
  (14 other events, 197.9 us)
